TPU v7x, 512 devices: a whole 4x4x16 slice. The times are simulated.
512 devices in a mesh: req: 64 (over y, z), head: 8 (over x, core).
Axes of the slice: x: 4, y: 4, z: 16, core: 2. Of those that a mesh axis runs over, the one named last changes fastest.
Arguments:
- tokens: bfloat16 [256, 2048], P('req'), may hold values from -1.1953125 to 1.1953125
- lengths: int32 [256], replicated, may hold values from 1 to 1021, as said below
- kv_cache: bfloat16 [1, 2, 65536, 8, 128], P(None, None, 'req', 'head'), may hold values from -24 to 24
- w_qkv: bfloat16 [1, 2048, 8, 512], P(None, 'req', 'head'), may hold values from -0.125 to 0.125
- w_headgate: bfloat16 [1, 2048, 16], P(None, None, 'head'), may hold values from -0.125 to 0.125
- w_out: bfloat16 [1, 2048, 2048], P(None, 'head', 'req'), may hold values from -0.5 to 0.5
- in_gain: float32 [1, 2048], replicated, may hold values from 0.5 to 1.5
- q_gain: float32 [1, 128], replicated, may hold values from 0.1 to 1.9
- k_gain: float32 [1, 128], replicated, may hold values from 0.1 to 1.9
- post_gain: float32 [1, 2048], replicated, may hold values from 0.5 to 1.5
- w_gate: bfloat16 [1, 2048, 6144], P(None, 'head', 'req'), may hold values from -0.125 to 0.125
- w_up: bfloat16 [1, 2048, 6144], P(None, 'head', 'req'), may hold values from -0.125 to 0.125
- w_down: bfloat16 [1, 6144, 2048], P(None, 'req', 'head'), may hold values from -0.078125 to 0.078125
- final_gain: float32 [2048], replicated, may hold values from 0.5 to 1.5
- w_vocab: bfloat16 [2048, 131072], P(None, ('req', 'head')), may hold values from -0.125 to 0.125
Outputs:
- logits: bfloat16 [256, 131072], P(None, ('req', 'head'))
Inputs may be any that keep to these rules, and one draw needn't show every extreme that they name: On every index of req the lengths of its 4 requests sum to at most 1024. On 8 indices, drawn anew, they sum to exactly 1024 and one request there is longer than 512; on one of these the other requests hold one token each. On every other index each length is at most 128 and one is exactly 128.
All inputs are finite; a program needn't handle non-finite values.
Results may differ from a plain program's by a relative error of at most 0.015.
Values may be sent and summed in bfloat16 or wider, within the bound.
No kernel may reach another device: no remote copies, remote signals or barrier semaphores. Data moves between devices by JAX's collectives and lax.ppermute only.
A program may use at most 64 MiB of HBM per device.

v0:
```python
import jax
import jax.numpy as jnp
from jax import lax
from jax.sharding import PartitionSpec as P

BLOCK = 256


EPSILON = 1e-06
ROPE_THETA = 1000000.0


def rms_scale(values, gain):
    mean_square = jnp.mean(values * values, axis=-1, keepdims=True)
    return values * lax.rsqrt(mean_square + EPSILON) * gain


def rotate(values, position):
    half_dim = values.shape[-1] // 2
    frequency = ROPE_THETA ** (-2.0 * jnp.arange(half_dim, dtype=jnp.float32) / values.shape[-1])
    angles = position.astype(jnp.float32)[:, None] * frequency[None, :]
    target_shape = (angles.shape[0],) + (1,) * (values.ndim - 2) + (half_dim,)
    cosine = jnp.cos(angles).reshape(target_shape)
    sine_part = jnp.sin(angles).reshape(target_shape)
    first_half = values[..., :half_dim]
    second = values[..., half_dim:]
    return jnp.concatenate(
        [first_half * cosine - second * sine_part, second * cosine + first_half * sine_part],
        axis=-1,
    )


def block_count(used_slots):
    return (used_slots + BLOCK - 1) // BLOCK


def slot_sums(queries, key_rows, value_rows, starts, limits, first_slot, blocks_needed):
    score_scale = queries.shape[-1] ** (-0.5)

    def block_step(block_index, carry):
        summed, denominator = carry
        first_row = block_index * BLOCK
        key_block = lax.dynamic_slice_in_dim(key_rows, first_row, BLOCK, 0)
        value_block = lax.dynamic_slice_in_dim(value_rows, first_row, BLOCK, 0)
        scores = (
            jnp.einsum("rgqd,sgd->rgqs", queries, key_block, preferred_element_type=jnp.float32)
            * score_scale
        )
        slot_index = first_slot + first_row + jnp.arange(BLOCK, dtype=jnp.int32)
        inside = (slot_index[None, :] >= starts[:, None]) & (slot_index[None, :] < limits[:, None])
        weights = jnp.where(inside[:, None, None, :], jnp.exp(scores), 0.0)
        rounded = weights.astype(jnp.bfloat16)
        summed = summed + jnp.einsum(
            "rgqs,sgd->rgqd", rounded, value_block, preferred_element_type=jnp.float32
        )
        return (summed, denominator + jnp.sum(weights, axis=-1))

    initial = (jnp.zeros(queries.shape, jnp.float32), jnp.zeros(queries.shape[:-1], jnp.float32))
    return lax.fori_loop(0, blocks_needed, block_step, initial)


def bounds_of(lengths, device_index, row_count):
    own_lengths = lax.dynamic_slice_in_dim(lengths, device_index * row_count, row_count)
    starts = jnp.cumsum(own_lengths) - own_lengths
    limits = starts + own_lengths
    return (starts, limits)


def attend(queries, new_key, new_value, cache_layer, lengths, row_count):
    req_index = lax.axis_index("req")
    starts, limits = bounds_of(lengths, req_index, row_count)
    used_slots = limits[-1]
    summed, denominator = slot_sums(
        queries, cache_layer[0], cache_layer[1], starts, limits, 0, block_count(used_slots)
    )
    score_scale = queries.shape[-1] ** (-0.5)
    own_score = (
        jnp.einsum("rgqd,rgd->rgq", queries, new_key, preferred_element_type=jnp.float32)
        * score_scale
    )
    own_weight = jnp.exp(own_score)
    denominator = denominator + own_weight
    summed = summed + jnp.einsum(
        "rgq,rgd->rgqd",
        own_weight.astype(jnp.bfloat16),
        new_value,
        preferred_element_type=jnp.float32,
    )
    return summed / denominator[..., None]


def local(
    tokens,
    lengths,
    kv_cache,
    w_qkv,
    w_headgate,
    w_out,
    in_gain,
    q_gain,
    k_gain,
    post_gain,
    w_gate,
    w_up,
    w_down,
    final_gain,
    w_vocab,
):
    row_count = tokens.shape[0]
    model_width = tokens.shape[1]
    local_kv = w_qkv.shape[2]
    column_count = w_qkv.shape[3]
    group_size = w_headgate.shape[2] // local_kv
    head_dim = q_gain.shape[1]
    req_index = lax.axis_index("req")
    positions = lax.dynamic_slice_in_dim(lengths, req_index * row_count, row_count)
    slice_width = model_width // lax.axis_size("head")
    slice_start = lax.axis_index("head") * slice_width
    stream = tokens
    normed = rms_scale(stream.astype(jnp.float32), in_gain[0]).astype(jnp.bfloat16)
    weight_block = w_qkv[0].reshape(w_qkv.shape[1], local_kv * column_count)
    exchanged = lax.all_to_all(normed, "req", split_axis=1, concat_axis=0, tiled=True)
    qkv = lax.psum_scatter(
        jnp.dot(exchanged, weight_block, preferred_element_type=jnp.float32),
        "req",
        scatter_dimension=0,
        tiled=True,
    )
    qkv = qkv.reshape(row_count, local_kv, column_count)
    queries = qkv[:, :, : group_size * head_dim].reshape(row_count, local_kv, group_size, head_dim)
    new_key = qkv[:, :, group_size * head_dim : (group_size + 1) * head_dim]
    new_value = qkv[:, :, (group_size + 1) * head_dim :].astype(jnp.bfloat16)
    queries = rotate(rms_scale(queries, q_gain[0]), positions).astype(jnp.bfloat16)
    new_key = rotate(rms_scale(new_key, k_gain[0]), positions).astype(jnp.bfloat16)
    head_gate = jax.nn.sigmoid(jnp.dot(normed, w_headgate[0], preferred_element_type=jnp.float32))
    head_gate = head_gate.reshape(row_count, local_kv, group_size)
    cache_layer = kv_cache[0]
    attended = attend(queries, new_key, new_value, cache_layer, lengths, row_count)
    mixed_heads = (
        (attended * head_gate[..., None])
        .astype(jnp.bfloat16)
        .reshape(row_count, local_kv * group_size * head_dim)
    )
    out_block = w_out[0]
    partial_out = jnp.dot(
        lax.all_gather(mixed_heads, "req", axis=0, tiled=True),
        out_block,
        preferred_element_type=jnp.float32,
    )
    summed_out = lax.psum(partial_out, "head")
    projected = lax.all_to_all(summed_out, "req", split_axis=0, concat_axis=1, tiled=True)
    stream = (stream.astype(jnp.float32) + projected).astype(jnp.bfloat16)
    normed_two = rms_scale(stream.astype(jnp.float32), post_gain[0]).astype(jnp.bfloat16)
    own_slice = lax.dynamic_slice_in_dim(normed_two, slice_start, slice_width, 1)
    gate_block = w_gate[0]
    up_block = w_up[0]
    portion = lax.all_gather(own_slice, "req", axis=0, tiled=True)
    gate_rows = jnp.dot(portion, gate_block, preferred_element_type=jnp.float32)
    up_rows = jnp.dot(portion, up_block, preferred_element_type=jnp.float32)
    partial_mlp = jnp.concatenate([gate_rows, up_rows], axis=1)
    both_parts = lax.psum(partial_mlp, "head")
    hidden_width = gate_block.shape[1]
    hidden = (jax.nn.silu(both_parts[:, :hidden_width]) * both_parts[:, hidden_width:]).astype(
        jnp.bfloat16
    )
    down_block = w_down[0]
    down_part = lax.psum_scatter(
        jnp.dot(hidden, down_block, preferred_element_type=jnp.float32),
        "req",
        scatter_dimension=0,
        tiled=True,
    )
    stream_slice = lax.dynamic_slice_in_dim(stream, slice_start, slice_width, 1)
    new_slice = (stream_slice.astype(jnp.float32) + down_part).astype(jnp.bfloat16)
    stream = lax.all_gather(new_slice, "head", axis=1, tiled=True)
    final_norm = rms_scale(stream.astype(jnp.float32), final_gain).astype(jnp.bfloat16)
    scored = jnp.dot(
        lax.all_gather(final_norm, "req", axis=0, tiled=True),
        w_vocab,
        preferred_element_type=jnp.float32,
    )
    return scored.astype(jnp.bfloat16)


def solution(mesh):
    in_specs = (
        P("req", None),
        P(),
        P(None, None, "req", "head", None),
        P(None, "req", "head", None),
        P(None, None, "head"),
        P(None, "head", "req"),
        P(),
        P(),
        P(),
        P(),
        P(None, "head", "req"),
        P(None, "head", "req"),
        P(None, "req", "head"),
        P(),
        P(None, ("req", "head")),
    )
    out_specs = P(None, ("req", "head"))
    return jax.shard_map(local, mesh=mesh, in_specs=in_specs, out_specs=out_specs, check_vma=False)
```

profile of v0, /device:TPU:1, one launch (start us, length us, event | category | flops | bytes accessed | tf_op | source)
XLA Modules:
  0.0 1030.9 jit_solution(7837290134652525117)
XLA Ops:
  6.5 0.9 fusion.28
  7.5 0.8 fusion.30
  9.1 19.4 %all-to-all-start = ((bf16[4,64,32]{2,0,1:T(4,128)(2,1)}), bf16[4,64,32]{2,0,1:T(4,128)(2,1)S(1)}, u32[]{:S(2)}, u32[]{:S(2)}) async-start(bf16[4,64,32]{2,0,1:T(4,128)(2,1)} %copy.22), calls=%async_computation | async-start | bytes 131072 | tf_op jit(solution)/shard_map/all_to_all | solution.py:122
  29.6 12.4 %all-to-all-done = bf16[4,64,32]{2,0,1:T(4,128)(2,1)S(1)} async-done(((bf16[4,64,32]{2,0,1:T(4,128)(2,1)}), bf16[4,64,32]{2,0,1:T(4,128)(2,1)S(1)}, u32[]{:S(2)}, u32[]{:S(2)}) %all-to-all-start) | async-done | bytes 16416 | tf_op jit(solution)/shard_map/all_to_all | solution.py:122
  42.0 1.0 fusion.32
  44.4 1.3 dynamic-slice
  46.6 244.2 %all-reduce.8.cloned.1.call-done = f32[256,512]{1,0:T(8,128)} async-done(((f32[256,512]{1,0:T(8,128)}), f32[256,512]{1,0:T(8,128)}) %all-reduce.8.cloned.1.call-update) | async-done | bytes 524304
  290.8 0.7 dynamic-slice_bitcast_fusion
  294.6 1.0 while.12
  295.6 71.2 %all-gather = bf16[64,4,256]{2,1,0:T(4,128)(2,1)S(1)} all-gather(bf16[1,4,256]{2,1,0:T(4,128)(2,1)S(1)} %fusion.52), channel_id=1, replica_groups=mesh['req'=64,'head'=8] {'req'}, dimensions={0}, use_global_device_ids=true | all-gather | bytes 133120 | tf_op jit(solution)/shard_map/all_gather | solution.py:146
  367.7 57.8 %psum.14 = f32[64,4,32]{2,1,0:T(4,128)S(1)} all-reduce(f32[64,4,32]{2,1,0:T(4,128)S(1)} %bitcast.140), channel_id=1, replica_groups=mesh['req'=64,'head'=8] {'head'}, use_global_device_ids=true, to_apply=%region_8.9 | all-reduce | flops 8192 | bytes 65536 | tf_op jit(solution)/shard_map/psum | solution.py:150
  425.5 0.8 reshape.402
  426.2 10.3 %all-to-all-start.1 = ((f32[64,1,128]{2,1,0:T(1,128)}), f32[64,1,128]{2,1,0:T(1,128)S(1)}, u32[]{:S(2)}, u32[]{:S(2)}) async-start(f32[64,1,128]{2,1,0:T(1,128)} %reshape.402), calls=%async_computation.1 | async-start | bytes 65536 | tf_op jit(solution)/shard_map/all_to_all | solution.py:151
  436.6 0.8 dynamic-slice.4
  437.4 12.4 %all-to-all-done.1 = f32[64,1,128]{2,1,0:T(1,128)S(1)} async-done(((f32[64,1,128]{2,1,0:T(1,128)}), f32[64,1,128]{2,1,0:T(1,128)S(1)}, u32[]{:S(2)}, u32[]{:S(2)}) %all-to-all-start.1) | async-done | bytes 32800 | tf_op jit(solution)/shard_map/all_to_all | solution.py:151
  451.5 70.7 %all-gather.1 = bf16[64,4,256]{2,1,0:T(4,128)(2,1)S(1)} all-gather(bf16[1,4,256]{2,1,0:T(4,128)(2,1)S(1)} %fusion.51), channel_id=1, replica_groups=mesh['req'=64,'head'=8] {'req'}, dimensions={0}, use_global_device_ids=true | all-gather | bytes 133120 | tf_op jit(solution)/shard_map/all_gather | solution.py:157
  522.3 0.8 copy-done.5
  524.8 93.4 %all-reduce.6.cloned.1.call-done = f32[256,192]{0,1:T(8,128)} async-done(((f32[256,192]{0,1:T(8,128)}), f32[256,192]{0,1:T(8,128)}) %all-reduce.6.cloned.1.call-update) | async-done | bytes 196624 | tf_op jit(solution)/shard_map/psum | solution.py:161
  618.1 1.9 fusion.17
  620.1 254.2 %all-reduce.10.cloned.1.call-done = f32[256,256]{1,0:T(8,128)} async-done(((f32[256,256]{1,0:T(8,128)}), f32[256,256]{1,0:T(8,128)}) %all-reduce.10.cloned.1.call-update) | async-done | bytes 262160
  875.0 22.9 %all_gather.14 = bf16[4,2048]{1,0:T(4,128)(2,1)S(1)} all-gather(bf16[4,256]{1,0:T(4,128)(2,1)S(1)} %fusion.40), channel_id=1, replica_groups=mesh['req'=64,'head'=8] {'head'}, dimensions={1}, use_global_device_ids=true | all-gather | bytes 18432 | tf_op jit(solution)/shard_map/all_gather | solution.py:175
  899.3 122.6 %all-gather.5.cloned.1.call-done = bf16[64,4,2048]{2,1,0:T(4,128)(2,1)} async-done(((bf16[1,4,2048]{2,1,0:T(4,128)(2,1)}), bf16[64,4,2048]{2,1,0:T(4,128)(2,1)}) %all-gather.5.cloned.1.call-update) | async-done | bytes 1048592 | tf_op jit(solution)/shard_map/all_gather | solution.py:178
  1021.9 1.3 reshape.394
  1023.2 1.1 convolution_convert_fusion
  (100 shorter events, 13.3 us)
Async XLA Ops:
  6.5 1016.7 %copy-start = (bf16[2048,256]{1,0:T(8,128)(2,1)S(1)}, bf16[2048,256]{1,0:T(8,128)(2,1)}, u32[]{:S(2)}) copy-start(bf16[2048,256]{1,0:T(8,128)(2,1)} %param.31) | copy-start | bytes 3145732
  6.5 1.0 copy-start.2
  9.1 32.9 %copy-start.7 = (bf16[1,32,1,512]{3,1,2,0:T(8,128)(2,1)S(1)}, bf16[1,32,1,512]{3,1,2,0:T(8,128)(2,1)}, u32[]{:S(2)}) copy-start(bf16[1,32,1,512]{3,1,2,0:T(8,128)(2,1)} %param.20) | copy-start | bytes 98308
  9.1 32.9 %all-to-all-start = ((bf16[4,64,32]{2,0,1:T(4,128)(2,1)}), bf16[4,64,32]{2,0,1:T(4,128)(2,1)S(1)}, u32[]{:S(2)}, u32[]{:S(2)}) async-start(bf16[4,64,32]{2,0,1:T(4,128)(2,1)} %copy.22), calls=%async_computation | async-start | bytes 131072 | tf_op jit(solution)/shard_map/all_to_all | solution.py:122
  28.5 262.3 %all-reduce.8.cloned.1.call-start = ((), (), s32[]{:S(2)}) async-start(), calls=%async_computation.4 | async-start | bytes 1048576
  28.6 0.7 copy-start.12
  42.0 4.5 copy-start.1
  44.4 2.0 copy-start.14
  291.5 0.6 copy-start.3
  291.6 0.7 copy-start.10
  292.4 0.7 slice-start
  293.2 0.7 copy-start.4
  293.4 0.7 copy-start.11
  366.8 0.7 copy-start.8
  426.2 23.5 %all-to-all-start.1 = ((f32[64,1,128]{2,1,0:T(1,128)}), f32[64,1,128]{2,1,0:T(1,128)S(1)}, u32[]{:S(2)}, u32[]{:S(2)}) async-start(f32[64,1,128]{2,1,0:T(1,128)} %reshape.402), calls=%async_computation.1 | async-start | bytes 65536 | tf_op jit(solution)/shard_map/all_to_all | solution.py:151
  436.5 181.6 %all-reduce.6.cloned.1.call-start = ((), (), s32[]{:S(2)}) async-start(), calls=%async_computation.2 | async-start | bytes 393216 | tf_op jit(solution)/shard_map/psum | solution.py:161
  522.2 0.8 copy-start.5
  523.0 0.8 copy-start.6
  524.7 93.5 %copy-start.13 = (bf16[1,96,256]{2,1,0:T(8,128)(2,1)S(1)}, bf16[1,96,256]{2,1,0:T(8,128)(2,1)}, u32[]{:S(2)}) copy-start(bf16[1,96,256]{2,1,0:T(8,128)(2,1)} %param.29) | copy-start | bytes 147460
  524.7 349.6 %all-reduce.10.cloned.1.call-start = ((), (), s32[]{:S(2)}) async-start(), calls=%async_computation.5 | async-start | bytes 524288
  620.0 401.8 %all-gather.5.cloned.1.call-start = ((), (), s32[]{:S(2)}) async-start(), calls=%async_computation.3 | async-start | bytes 1064960 | tf_op jit(solution)/shard_map/all_gather | solution.py:178
  897.9 0.7 copy-start.9
Sparse Core Ops, SparseCore 0:
  43.2 247.5 all-reduce.7
  524.8 93.2 all-reduce.5
  621.6 252.6 all-reduce.9
  899.4 122.4 all-gather.4
where the time goes:
time: 1040 us; the launch traced here: 1030 us
  waiting for transfers between devices  739 us (71%)
  blocking collectives  223 us (21%)
  starting transfers between devices  29.9 us (3%)
  between operations  14.7 us (1%)
  local copies, waits for them, and re-layouts  12.6 us (1%)
    unnamed x6, waiting for transfers between devices  498 us
    all_gather x1, waiting for transfers between devices, local(): lax.all_gather(final_norm, 'req', axis=0, tiled=True)  123 us
    psum x1, waiting for transfers between devices, local(): both_parts = lax.psum(partial_mlp, 'head')  93.4 us
    all_gather x1, blocking collectives, local(): lax.all_gather(mixed_heads, 'req', axis=0, tiled=True)  71.2 us
    all_gather x1, blocking collectives, local(): portion = lax.all_gather(own_slice, 'req', axis=0, tiled=True)  70.7 us
    psum x1, blocking collectives, local(): summed_out = lax.psum(partial_out, 'head')  57.8 us
    all_gather x1, blocking collectives, local(): stream = lax.all_gather(new_slice, 'head', axis=1, tiled=True)  22.9 us
  transfers between devices with their start and end apart: 6, of which 6 were waited for; matrix products, arithmetic and copies ran while one was open for 0% of the time, Pallas kernels for 0%

commit v1 on v0

v1 whole, which is shorter than its diff:
```python
import jax
import jax.numpy as jnp
from jax import lax
from jax.sharding import Mesh
from jax.sharding import PartitionSpec as P

EPSILON = 1e-06
ROPE_THETA = 1000000.0
Y, Z, X, C = 4, 16, 4, 2
F32, BF16 = jnp.float32, jnp.bfloat16


def rms_scale(values, gain):
    mean_square = jnp.mean(values * values, axis=-1, keepdims=True)
    return values * lax.rsqrt(mean_square + EPSILON) * gain


def rotate(values, cosine, sine):
    half = values.shape[-1] // 2
    a, b = values[..., :half], values[..., half:]
    return jnp.concatenate([a * cosine - b * sine, b * cosine + a * sine], axis=-1)


def swap(values, axes):
    return lax.all_to_all(values, axes, split_axis=0, concat_axis=0, tiled=True)


def spread(values, axes, count):
    return swap(jnp.broadcast_to(values[None], (count,) + values.shape), axes)


def local(
    tokens,
    lengths,
    kv_cache,
    w_qkv,
    w_headgate,
    w_out,
    in_gain,
    q_gain,
    k_gain,
    post_gain,
    w_gate,
    w_up,
    w_down,
    final_gain,
    w_vocab,
):
    rows, width = tokens.shape
    head_dim = q_gain.shape[1]
    columns = w_qkv.shape[3]
    req = lax.axis_index(("y", "z"))
    ix, ic = lax.axis_index("x"), lax.axis_index("c")

    qkv_block = lax.all_gather(w_qkv[0, :, 0], "y", axis=0, tiled=True)
    out_part = lax.all_gather(w_out[0].T, "z", axis=0, tiled=True)
    out_block = lax.all_gather(out_part, "y", axis=0, tiled=True)
    gate_up = jnp.concatenate([w_gate[0].T, w_up[0].T], axis=0)
    gate_up = lax.all_gather(gate_up, "x", axis=0)
    down = lax.all_gather(w_down[0], "x", axis=0)

    positions = lax.dynamic_slice_in_dim(lengths, req * rows, rows)
    starts = jnp.cumsum(positions) - positions
    limits = starts + positions

    normed = rms_scale(tokens.astype(F32), in_gain[0]).astype(BF16)
    head_gate = jax.nn.sigmoid(jnp.dot(normed, w_headgate[0], preferred_element_type=F32))

    depth = width // (Y * Z)
    sent = normed.reshape(rows, Y, Z, depth).transpose(2, 0, 1, 3).reshape(Z, rows, Y * depth)
    arrived = swap(sent, "z").reshape(Z * rows, Y * depth)
    part = jnp.dot(arrived, qkv_block, preferred_element_type=F32).astype(BF16)
    qkv = jnp.sum(swap(part.reshape(Z, rows, columns), "z").astype(F32), axis=0)

    half = head_dim // 2
    frequency = ROPE_THETA ** (-2.0 * jnp.arange(half, dtype=F32) / head_dim)
    angles = positions.astype(F32)[:, None] * frequency[None, :]
    cosine, sine = jnp.cos(angles), jnp.sin(angles)
    query = qkv[:, : 2 * head_dim].reshape(rows, 2, head_dim)
    query = rotate(rms_scale(query, q_gain[0]), cosine[:, None], sine[:, None]).astype(BF16)
    key = qkv[:, 2 * head_dim : 3 * head_dim]
    key = rotate(rms_scale(key, k_gain[0]), cosine, sine).astype(BF16)
    value = qkv[:, 3 * head_dim :].astype(BF16)

    scale = head_dim ** (-0.5)
    keys, values = kv_cache[0, 0, :, 0], kv_cache[0, 1, :, 0]
    slots = keys.shape[0]
    score = jnp.einsum("rqd,sd->rqs", query, keys, preferred_element_type=F32) * scale
    slot = jnp.arange(slots, dtype=jnp.int32)
    inside = (slot[None, :] >= starts[:, None]) & (slot[None, :] < limits[:, None])
    weight = jnp.where(inside[:, None, :], jnp.exp(score), 0.0)
    own = jnp.exp(jnp.sum(query.astype(F32) * key.astype(F32)[:, None], axis=-1) * scale)
    total = jnp.sum(weight, axis=-1) + own
    summed = jnp.einsum("rqs,sd->rqd", weight.astype(BF16), values, preferred_element_type=F32)
    summed = summed + own.astype(BF16).astype(F32)[..., None] * value.astype(F32)[:, None]
    attended = summed / total[..., None]
    mixed = (attended * head_gate[..., None]).astype(BF16).reshape(rows, 2 * head_dim)

    part = lax.dot_general(mixed, out_block, (((1,), (1,)), ((), ())), preferred_element_type=F32)
    projected = jnp.sum(spread(part, ("x", "c"), X * C), axis=0)
    stream = (tokens.astype(F32) + projected).astype(BF16)
    normed_two = rms_scale(stream.astype(F32), post_gain[0]).astype(BF16)

    def mine(array):
        row = lax.dynamic_slice_in_dim(array, ix, 1, 0).reshape(X, C, width // (X * C))
        return lax.dynamic_slice_in_dim(row, ic, 1, 1).reshape(1, width // C)

    batch = spread(mine(normed_two), ("y", "z"), Y * Z).reshape(Y * Z, width // C)
    gate_up = gate_up.transpose(1, 0, 2).reshape(gate_up.shape[1], width // C)
    part = lax.dot_general(batch, gate_up, (((1,), (1,)), ((), ())), preferred_element_type=F32)
    both = jnp.sum(lax.all_gather(part, "c", axis=0), axis=0)
    units = w_gate.shape[2]
    hidden = (jax.nn.silu(both[:, :units]) * both[:, units:]).astype(BF16)
    down = down.transpose(1, 0, 2).reshape(units, width // C)
    part = jnp.dot(hidden, down, preferred_element_type=F32).astype(BF16)
    lowered = jnp.sum(swap(part.reshape(Y * Z, 1, width // C), ("y", "z")).astype(F32), axis=0)
    piece = (mine(stream).astype(F32) + lowered).astype(BF16)

    piece = spread(piece, ("y", "z"), Y * Z).reshape(Y * Z, width // C)
    piece = spread(piece, "x", X).reshape(X * Y * Z, width // C)
    whole = lax.all_gather(piece, "c", axis=0)
    mean_square = jnp.sum(jnp.square(whole.astype(F32)), axis=(0, 2)) / width
    gain = final_gain.reshape(X, C, width // (X * C)).transpose(1, 0, 2).reshape(C, 1, width // C)
    final = (whole.astype(F32) * lax.rsqrt(mean_square + EPSILON)[None, :, None] * gain).astype(BF16)
    vocab = w_vocab.reshape(X, C, width // (X * C), w_vocab.shape[1]).transpose(1, 0, 2, 3)
    vocab = vocab.reshape(C, width // C, w_vocab.shape[1])
    logits = jnp.dot(final[0], vocab[0], preferred_element_type=F32)
    logits = logits + jnp.dot(final[1], vocab[1], preferred_element_type=F32)
    logits = logits.astype(BF16).reshape(X, Y * Z, w_vocab.shape[1]).transpose(1, 0, 2)
    return logits.reshape(X * Y * Z, w_vocab.shape[1])


def solution(mesh):
    fine = Mesh(mesh.devices.reshape(Y, Z, X, C), ("y", "z", "x", "c"))
    req, head = ("y", "z"), ("x", "c")
    in_specs = (
        P(req, None),
        P(),
        P(None, None, req, head, None),
        P(None, req, head, None),
        P(None, None, head),
        P(None, head, req),
        P(),
        P(),
        P(),
        P(),
        P(None, head, req),
        P(None, head, req),
        P(None, req, head),
        P(),
        P(None, req + head),
    )
    out_specs = P(None, req + head)
    return jax.shard_map(local, mesh=fine, in_specs=in_specs, out_specs=out_specs, check_vma=False)
```

time: 1040 us -> 242 us (0.23)
  waiting for transfers between devices: 739 us -> 50.5 us
  blocking collectives: 223 us -> 96.2 us
  starting transfers between devices: 29.9 us -> 58.9 us
    unnamed x6 -> x2, waiting for transfers between devices: 498 us -> 0.03 us
    all_gather x1 -> x2, waiting for transfers between devices: 123 us -> 18.2 us  [the longest x1 15.4 us: local(): whole = lax.all_gather(piece, 'c', axis=0)]
    all_gather x3 -> x5, blocking collectives: 165 us -> 64.9 us  [the longest x1 27 us: local(): out_part = lax.all_gather(w_out[0].T, 'z', axis=0, tiled=True)]
    psum x1 -> x0, waiting for transfers between devices: 93.4 us -> none  [local(): both_parts = lax.psum(partial_mlp, 'head')]
    psum x1 -> x0, blocking collectives: 57.8 us -> none  [local(): summed_out = lax.psum(partial_out, 'head')]
    all_to_all x0 -> x2, blocking collectives: none -> 31.3 us  [swap(): return lax.all_to_all(values, axes, split_axis=0, concat_axis=0, tiled=True)]
    all_to_all x2 -> x5, starting transfers between devices: 29.7 us -> 58.8 us  [swap(): return lax.all_to_all(values, axes, split_axis=0, concat_axis=0, tiled=True)]
    all_to_all x2 -> x5, waiting for transfers between devices: 24.8 us -> 32.3 us  [swap(): return lax.all_to_all(values, axes, split_axis=0, concat_axis=0, tiled=True)]
  transfers between devices with their start and end apart: 6 -> 7, of which waited for: 6 -> 5; matrix products, arithmetic and copies ran while one was open for 0% -> 2% of each run, Pallas kernels for 0% -> 0%
where the time goes in v1:
time: 242 us; the launch traced here: 241 us
  blocking collectives  96.2 us (40%)
  starting transfers between devices  58.9 us (24%)
  waiting for transfers between devices  50.5 us (21%)
  between operations  13.8 us (6%)
  other arithmetic  10.3 us (4%)
  local copies, waits for them, and re-layouts  7.77 us (3%)
  matrix products  3.4 us (1%)
    all_to_all x5, starting transfers between devices, swap(): return lax.all_to_all(values, axes, split_axis=0, concat_axis=0, tiled=True)  58.8 us
    all_to_all x5, waiting for transfers between devices, swap(): return lax.all_to_all(values, axes, split_axis=0, concat_axis=0, tiled=True)  32.3 us
    all_to_all x2, blocking collectives, swap(): return lax.all_to_all(values, axes, split_axis=0, concat_axis=0, tiled=True)  31.3 us
    all_gather x1, blocking collectives, local(): out_part = lax.all_gather(w_out[0].T, 'z', axis=0, tiled=True)  27 us
    all_gather x1, waiting for transfers between devices, local(): whole = lax.all_gather(piece, 'c', axis=0)  15.4 us
    all_gather x1, blocking collectives, local(): qkv_block = lax.all_gather(w_qkv[0, :, 0], 'y', axis=0, tiled=True)  10.2 us
    all_gather x1, blocking collectives, local(): gate_up = lax.all_gather(gate_up, 'x', axis=0)  9.93 us
    all_gather x1, blocking collectives, local(): down = lax.all_gather(w_down[0], 'x', axis=0)  9.83 us
  transfers between devices with their start and end apart: 7, of which 5 were waited for; matrix products, arithmetic and copies ran while one was open for 2% of the time, Pallas kernels for 0%

profile of v1, /device:TPU:1, one launch (start us, length us, event | category | flops | bytes accessed | tf_op | source)
XLA Modules:
  0.0 240.8 jit_solution(1843471291022749129)
XLA Ops:
  6.5 0.9 fusion.26
  7.5 0.8 fusion.28
  9.1 15.7 %all-to-all-start = ((bf16[16,4,128]{2,1,0:T(4,128)(2,1)}), bf16[16,4,128]{2,1,0:T(4,128)(2,1)S(1)}, u32[]{:S(2)}, u32[]{:S(2)}) async-start(bf16[16,4,128]{2,1,0:T(4,128)(2,1)} %copy.39), calls=%async_computation | async-start | bytes 32768 | tf_op jit(solution)/shard_map/all_to_all | solution.py:25
  24.9 27.0 %all_gather.28 = bf16[512,256]{1,0:T(8,128)(2,1)} all-gather(bf16[32,256]{1,0:T(8,128)(2,1)} %bitcast.114), channel_id=1, replica_groups=mesh['y'=4,'z'=16,'x'=4,'c'=2] {'z'}, dimensions={0}, use_global_device_ids=true | all-gather | bytes 278528 | tf_op jit(solution)/shard_map/all_gather | solution.py:56
  52.0 0.8 dynamic-slice_bitcast_fusion
  53.8 10.2 %all-gather = bf16[1,128,1,512]{3,1,2,0:T(8,128)(2,1)S(1)} all-gather(bf16[1,32,1,512]{3,1,2,0:T(8,128)(2,1)} %param.18), channel_id=2, replica_groups=mesh['y'=4,'z'=16,'x'=4,'c'=2] {'y'}, dimensions={1}, use_global_device_ids=true | all-gather | bytes 163840 | tf_op jit(solution)/shard_map/all_gather | solution.py:55
  64.8 7.5 %all-to-all-start.1 = ((bf16[16,4,512]{2,1,0:T(4,128)(2,1)}), bf16[16,4,512]{2,1,0:T(4,128)(2,1)S(1)}, u32[]{:S(2)}, u32[]{:S(2)}) async-start(bf16[16,4,512]{2,1,0:T(4,128)(2,1)} %reshape.262), calls=%async_computation.1 | async-start | bytes 131072 | tf_op jit(solution)/shard_map/all_to_all | solution.py:25
  72.5 11.4 %all-to-all-done.1 = bf16[16,4,512]{2,1,0:T(4,128)(2,1)S(1)} async-done(((bf16[16,4,512]{2,1,0:T(4,128)(2,1)}), bf16[16,4,512]{2,1,0:T(4,128)(2,1)S(1)}, u32[]{:S(2)}, u32[]{:S(2)}) %all-to-all-start.1) | async-done | bytes 65568 | tf_op jit(solution)/shard_map/all_to_all | solution.py:25
  85.1 2.8 %all-gather.6.cloned.1.call-done = bf16[2048,256]{1,0:T(8,128)(2,1)} async-done(((bf16[512,256]{1,0:T(8,128)(2,1)}), bf16[2048,256]{1,0:T(8,128)(2,1)}) %all-gather.6.cloned.1.call-update) | async-done | bytes 1048592 | tf_op jit(solution)/shard_map/all_gather | solution.py:57
  87.9 1.7 fusion.14
  90.4 14.3 %all-to-all-start.2 = ((f32[8,4,2048]{2,1,0:T(4,128)}), f32[8,4,2048]{2,1,0:T(4,128)S(1)}, u32[]{:S(2)}, u32[]{:S(2)}) async-start(f32[8,4,2048]{2,1,0:T(4,128)} %broadcast_in_dim.26), calls=%async_computation.2 | async-start | bytes 524288 | tf_op jit(solution)/shard_map/all_to_all | solution.py:25
  104.6 6.5 %all-to-all-done.2 = f32[8,4,2048]{2,1,0:T(4,128)S(1)} async-done(((f32[8,4,2048]{2,1,0:T(4,128)}), f32[8,4,2048]{2,1,0:T(4,128)S(1)}, u32[]{:S(2)}, u32[]{:S(2)}) %all-to-all-start.2) | async-done | bytes 262176 | tf_op jit(solution)/shard_map/all_to_all | solution.py:25
  113.4 1.4 reduce.7
  115.6 6.1 %all-to-all-start.3 = ((bf16[64,2,512]{2,1,0:T(2,128)(2,1)}), bf16[64,2,512]{2,1,0:T(2,128)(2,1)S(1)}, u32[]{:S(2)}, u32[]{:S(2)}) async-start(bf16[64,2,512]{2,1,0:T(2,128)(2,1)} %reshape.284), calls=%async_computation.3 | async-start | bytes 262144 | tf_op jit(solution)/shard_map/all_to_all | solution.py:25
  121.7 9.8 %all_gather.34 = bf16[4,96,256]{2,1,0:T(8,128)(2,1)S(1)} all-gather(bf16[1,96,256]{2,1,0:T(8,128)(2,1)S(1)} %copy-done.6), channel_id=1, replica_groups=mesh['y'=4,'z'=16,'x'=4,'c'=2] {'x'}, dimensions={0}, use_global_device_ids=true | all-gather | bytes 245760 | tf_op jit(solution)/shard_map/all_gather | solution.py:60
  131.6 9.9 %all-gather.1 = bf16[768,256]{1,0:T(8,128)(2,1)S(1)} all-gather(bf16[192,256]{1,0:T(8,128)(2,1)S(1)} %pad_maximum_fusion), channel_id=3, replica_groups=mesh['y'=4,'z'=16,'x'=4,'c'=2] {'x'}, dimensions={0}, use_global_device_ids=true | all-gather | bytes 491520 | tf_op jit(solution)/shard_map/all_gather | solution.py:59
  142.3 7.9 %all-gather.2 = f32[128,192]{1,0:T(8,128)S(1)} all-gather(f32[64,192]{1,0:T(8,128)S(1)} %fusion.22), channel_id=4, replica_groups=mesh['y'=4,'z'=16,'x'=4,'c'=2] {'c'}, dimensions={0}, use_global_device_ids=true | all-gather | bytes 147456 | tf_op jit(solution)/shard_map/all_gather | solution.py:111
  151.9 15.1 %all-to-all-start.4 = ((bf16[64,2,512]{2,1,0:T(2,128)(2,1)}), bf16[64,2,512]{2,1,0:T(2,128)(2,1)S(1)}, u32[]{:S(2)}, u32[]{:S(2)}) async-start(bf16[64,2,512]{2,1,0:T(2,128)(2,1)} %reshape.286), calls=%async_computation.4 | async-start | bytes 262144 | tf_op jit(solution)/shard_map/all_to_all | solution.py:25
  167.1 14.4 %all-to-all-done.4 = bf16[64,2,512]{2,1,0:T(2,128)(2,1)S(1)} async-done(((bf16[64,2,512]{2,1,0:T(2,128)(2,1)}), bf16[64,2,512]{2,1,0:T(2,128)(2,1)S(1)}, u32[]{:S(2)}, u32[]{:S(2)}) %all-to-all-start.4) | async-done | bytes 131104 | tf_op jit(solution)/shard_map/all_to_all | solution.py:25
  182.0 1.4 reduce.9
  183.5 21.1 %all_to_all.35 = bf16[64,2,512]{2,1,0:T(2,128)(2,1)S(1)} all-to-all(bf16[64,2,512]{2,1,0:T(2,128)(2,1)S(1)} %reshape.288), channel_id=1, replica_groups=mesh['y'=4,'z'=16,'x'=4,'c'=2] {'y','z'}, dimensions={0} | all-to-all | bytes 262144 | tf_op jit(solution)/shard_map/all_to_all | solution.py:25
  204.9 10.1 %all_to_all.36 = bf16[4,64,1024]{2,1,0:T(8,128)(2,1)} all-to-all(bf16[4,64,1024]{2,1,0:T(8,128)(2,1)S(1)} %broadcast_in_dim.31), channel_id=1, replica_groups=mesh['y'=4,'z'=16,'x'=4,'c'=2] {'x'}, dimensions={0} | all-to-all | bytes 1048576 | tf_op jit(solution)/shard_map/all_to_all | solution.py:25
  215.2 15.4 %all-gather.8.cloned.1.call-done = bf16[2,256,1024]{2,1,0:T(8,128)(2,1)} async-done(((bf16[1,256,1024]{2,1,0:T(8,128)(2,1)}), bf16[2,256,1024]{2,1,0:T(8,128)(2,1)}) %all-gather.8.cloned.1.call-update) | async-done | bytes 1048592 | tf_op jit(solution)/shard_map/all_gather | solution.py:121
  230.6 1.6 fusion
  (97 shorter events, 12.9 us)
Async XLA Ops:
  6.5 65.8 %copy-start = (bf16[1,2048,2]{1,2,0:T(2,128)(2,1)S(1)}, bf16[1,2048,2]{1,2,0:T(2,128)(2,1)}, u32[]{:S(2)}) copy-start(bf16[1,2048,2]{1,2,0:T(2,128)(2,1)} %param.19) | copy-start | bytes 24580
  6.5 77.6 %copy-start.9 = (f32[1,128]{1,0:T(1,128)S(1)}, f32[1,128]{1,0:T(1,128)}, u32[]{:S(2)}) copy-start(f32[1,128]{1,0:T(1,128)} %param.23) | copy-start | bytes 1540
  6.5 77.9 %copy-start.10 = (f32[1,128]{1,0:T(1,128)S(1)}, f32[1,128]{1,0:T(1,128)}, u32[]{:S(2)}) copy-start(f32[1,128]{1,0:T(1,128)} %param.22) | copy-start | bytes 1540
  6.5 78.2 %copy-start.11 = (bf16[1,2,1024,1,128]{4,2,3,1,0:T(8,128)(2,1)S(1)}, bf16[1,2,1024,1,128]{4,2,3,1,0:T(8,128)(2,1)}, u32[]{:S(2)}) copy-start(bf16[1,2,1024,1,128]{4,2,3,1,0:T(8,128)(2,1)} %param.17) | copy-start | bytes 1572868
  9.1 54.8 %all-to-all-start = ((bf16[16,4,128]{2,1,0:T(4,128)(2,1)}), bf16[16,4,128]{2,1,0:T(4,128)(2,1)S(1)}, u32[]{:S(2)}, u32[]{:S(2)}) async-start(bf16[16,4,128]{2,1,0:T(4,128)(2,1)} %copy.39), calls=%async_computation | async-start | bytes 32768 | tf_op jit(solution)/shard_map/all_to_all | solution.py:25
  24.9 63.0 %all-gather.6.cloned.1.call-start = ((), (), s32[]{:S(2)}) async-start(), calls=%async_computation.7 | async-start | bytes 1310720 | tf_op jit(solution)/shard_map/all_gather | solution.py:57
  64.8 19.1 %all-to-all-start.1 = ((bf16[16,4,512]{2,1,0:T(4,128)(2,1)}), bf16[16,4,512]{2,1,0:T(4,128)(2,1)S(1)}, u32[]{:S(2)}, u32[]{:S(2)}) async-start(bf16[16,4,512]{2,1,0:T(4,128)(2,1)} %reshape.262), calls=%async_computation.1 | async-start | bytes 131072 | tf_op jit(solution)/shard_map/all_to_all | solution.py:25
  87.9 23.3 %copy-start.3 = (bf16[4,2048]{1,0:T(4,128)(2,1)S(1)}, bf16[4,2048]{1,0:T(4,128)(2,1)}, u32[]{:S(2)}) copy-start(bf16[4,2048]{1,0:T(4,128)(2,1)} %param.15) | copy-start | bytes 49156
  87.9 24.0 %copy-start.8 = (f32[1,2048]{1,0:T(1,128)S(1)}, f32[1,2048]{1,0:T(1,128)}, u32[]{:S(2)}) copy-start(f32[1,2048]{1,0:T(1,128)} %param.24) | copy-start | bytes 24580
  90.4 31.4 %copy-start.6 = (bf16[1,96,256]{2,1,0:T(8,128)(2,1)S(1)}, bf16[1,96,256]{2,1,0:T(8,128)(2,1)}, u32[]{:S(2)}) copy-start(bf16[1,96,256]{2,1,0:T(8,128)(2,1)} %param.27) | copy-start | bytes 147460
  90.4 20.8 %all-to-all-start.2 = ((f32[8,4,2048]{2,1,0:T(4,128)}), f32[8,4,2048]{2,1,0:T(4,128)S(1)}, u32[]{:S(2)}, u32[]{:S(2)}) async-start(f32[8,4,2048]{2,1,0:T(4,128)} %broadcast_in_dim.26), calls=%async_computation.2 | async-start | bytes 524288 | tf_op jit(solution)/shard_map/all_to_all | solution.py:25
  111.2 20.4 %copy-start.4 = (bf16[1,256,96]{1,2,0:T(8,128)(2,1)S(1)}, bf16[1,256,96]{1,2,0:T(8,128)(2,1)}, u32[]{:S(2)}) copy-start(bf16[1,256,96]{1,2,0:T(8,128)(2,1)} %param.26) | copy-start | bytes 147460
  111.2 20.4 %copy-start.5 = (bf16[1,256,96]{1,2,0:T(8,128)(2,1)S(1)}, bf16[1,256,96]{1,2,0:T(8,128)(2,1)}, u32[]{:S(2)}) copy-start(bf16[1,256,96]{1,2,0:T(8,128)(2,1)} %param.25) | copy-start | bytes 147460
  115.6 26.3 %all-to-all-start.3 = ((bf16[64,2,512]{2,1,0:T(2,128)(2,1)}), bf16[64,2,512]{2,1,0:T(2,128)(2,1)S(1)}, u32[]{:S(2)}, u32[]{:S(2)}) async-start(bf16[64,2,512]{2,1,0:T(2,128)(2,1)} %reshape.284), calls=%async_computation.3 | async-start | bytes 262144 | tf_op jit(solution)/shard_map/all_to_all | solution.py:25
  151.9 29.6 %all-to-all-start.4 = ((bf16[64,2,512]{2,1,0:T(2,128)(2,1)}), bf16[64,2,512]{2,1,0:T(2,128)(2,1)S(1)}, u32[]{:S(2)}, u32[]{:S(2)}) async-start(bf16[64,2,512]{2,1,0:T(2,128)(2,1)} %reshape.286), calls=%async_computation.4 | async-start | bytes 262144 | tf_op jit(solution)/shard_map/all_to_all | solution.py:25
  167.1 63.6 %all-gather.8.cloned.1.call-start = ((), (), s32[]{:S(2)}) async-start(), calls=%async_computation.8 | async-start | bytes 1572864 | tf_op jit(solution)/shard_map/all_gather | solution.py:121
  204.8 10.3 %copy-start.7 = (f32[2048]{0:T(1024)S(1)}, f32[2048]{0:T(1024)}, u32[]{:S(2)}) copy-start(f32[2048]{0:T(1024)} %param.28) | copy-start | bytes 24580
  204.8 10.3 %copy-start.2 = (bf16[2048,256]{1,0:T(8,128)(2,1)S(1)}, bf16[2048,256]{1,0:T(8,128)(2,1)}, u32[]{:S(2)}) copy-start(bf16[2048,256]{1,0:T(8,128)(2,1)} %param.29) | copy-start | bytes 3145732
  230.6 1.6 copy-start.1
Sparse Core Ops, SparseCore 0:
  52.1 35.7 all-gather.5
  215.2 15.3 all-gather.7

commit v2 on v1

--- a/solution.py
+++ b/solution.py
@@ -49,15 +49,15 @@
     rows, width = tokens.shape
     head_dim = q_gain.shape[1]
     columns = w_qkv.shape[3]
+    units = w_gate.shape[2]
+    seg = width // (X * C)
+    part_width = width // C
     req = lax.axis_index(("y", "z"))
     ix, ic = lax.axis_index("x"), lax.axis_index("c")
 
-    qkv_block = lax.all_gather(w_qkv[0, :, 0], "y", axis=0, tiled=True)
-    out_part = lax.all_gather(w_out[0].T, "z", axis=0, tiled=True)
-    out_block = lax.all_gather(out_part, "y", axis=0, tiled=True)
-    gate_up = jnp.concatenate([w_gate[0].T, w_up[0].T], axis=0)
-    gate_up = lax.all_gather(gate_up, "x", axis=0)
-    down = lax.all_gather(w_down[0], "x", axis=0)
+    ffn = jnp.concatenate([w_gate[0].T, w_up[0].T, w_down[0]], axis=0)
+    ffn = lax.all_gather(ffn, ("y", "x"), axis=0).reshape(Y, X, -1, seg)
+    qkv_block = spread(w_qkv[0, :, 0], "y", Y).reshape(-1, columns)
 
     positions = lax.dynamic_slice_in_dim(lengths, req * rows, rows)
     starts = jnp.cumsum(positions) - positions
@@ -68,9 +68,17 @@
 
     depth = width // (Y * Z)
     sent = normed.reshape(rows, Y, Z, depth).transpose(2, 0, 1, 3).reshape(Z, rows, Y * depth)
-    arrived = swap(sent, "z").reshape(Z * rows, Y * depth)
-    part = jnp.dot(arrived, qkv_block, preferred_element_type=F32).astype(BF16)
+    block = w_out[0].T
+    block = jnp.concatenate([block[:, :head_dim], block[:, head_dim:]], axis=0)
+    sent = jnp.concatenate(
+        [sent, jnp.zeros((Z, 8 - rows, head_dim), BF16), jnp.broadcast_to(block[None], (Z,) + block.shape)], axis=1
+    )
+    arrived = swap(sent, "z")
+    batch = arrived[:, :rows].reshape(Z * rows, Y * depth)
+    out_block = arrived[:, 8:].reshape(Z, 2, -1, head_dim).transpose(1, 0, 2, 3).reshape(2, -1, head_dim)
+    part = jnp.dot(batch, qkv_block, preferred_element_type=F32).astype(BF16)
     qkv = jnp.sum(swap(part.reshape(Z, rows, columns), "z").astype(F32), axis=0)
+    out_block = spread(out_block, "y", Y)
 
     half = head_dim // 2
     frequency = ROPE_THETA ** (-2.0 * jnp.arange(half, dtype=F32) / head_dim)
@@ -94,40 +102,46 @@
     summed = jnp.einsum("rqs,sd->rqd", weight.astype(BF16), values, preferred_element_type=F32)
     summed = summed + own.astype(BF16).astype(F32)[..., None] * value.astype(F32)[:, None]
     attended = summed / total[..., None]
-    mixed = (attended * head_gate[..., None]).astype(BF16).reshape(rows, 2 * head_dim)
+    mixed = (attended * head_gate[..., None]).astype(BF16)
 
-    part = lax.dot_general(mixed, out_block, (((1,), (1,)), ((), ())), preferred_element_type=F32)
-    projected = jnp.sum(spread(part, ("x", "c"), X * C), axis=0)
-    stream = (tokens.astype(F32) + projected).astype(BF16)
-    normed_two = rms_scale(stream.astype(F32), post_gain[0]).astype(BF16)
+    part = jnp.einsum("rqd,yqnd->ryn", mixed, out_block, preferred_element_type=F32)
+    part = part.reshape(rows, Y, C, seg).transpose(0, 2, 1, 3).reshape(rows * C, 8, part_width // 8)
+    projected = jnp.sum(swap(part, ("x", "c")), axis=0)
 
     def mine(array):
-        row = lax.dynamic_slice_in_dim(array, ix, 1, 0).reshape(X, C, width // (X * C))
-        return lax.dynamic_slice_in_dim(row, ic, 1, 1).reshape(1, width // C)
+        row = lax.dynamic_slice_in_dim(array, ix, 1, 0).reshape(X, C, seg)
+        return lax.dynamic_slice_in_dim(row, ic, 1, 1).reshape(8, part_width // 8)
 
-    batch = spread(mine(normed_two), ("y", "z"), Y * Z).reshape(Y * Z, width // C)
-    gate_up = gate_up.transpose(1, 0, 2).reshape(gate_up.shape[1], width // C)
-    part = lax.dot_general(batch, gate_up, (((1,), (1,)), ((), ())), preferred_element_type=F32)
-    both = jnp.sum(lax.all_gather(part, "c", axis=0), axis=0)
-    units = w_gate.shape[2]
-    hidden = (jax.nn.silu(both[:, :units]) * both[:, units:]).astype(BF16)
-    down = down.transpose(1, 0, 2).reshape(units, width // C)
-    part = jnp.dot(hidden, down, preferred_element_type=F32).astype(BF16)
-    lowered = jnp.sum(swap(part.reshape(Y * Z, 1, width // C), ("y", "z")).astype(F32), axis=0)
-    piece = (mine(stream).astype(F32) + lowered).astype(BF16)
+    def half_of(gain):
+        return lax.dynamic_slice_in_dim(gain.reshape(X, C, seg), ic, 1, 1).reshape(8, part_width // 8)
 
-    piece = spread(piece, ("y", "z"), Y * Z).reshape(Y * Z, width // C)
-    piece = spread(piece, "x", X).reshape(X * Y * Z, width // C)
-    whole = lax.all_gather(piece, "c", axis=0)
+    stream = (mine(tokens).astype(F32) + projected).astype(BF16)
+    wide = stream.astype(F32)
+    squares = jnp.sum(lax.all_gather(jnp.sum(wide * wide).reshape(1, 1), "c", axis=0)) / width
+    normed_two = (wide * lax.rsqrt(squares + EPSILON) * half_of(post_gain[0])).astype(BF16)
+
+    batch = spread(normed_two, "z", Z).reshape(Z, X, seg)
+    part = jnp.einsum("bxk,yxfk->byf", batch, ffn[:, :, : 2 * units], preferred_element_type=F32)
+    part = part.reshape(Z, Y * 2 * units)
+    both = jnp.sum(lax.all_gather(part, "c", axis=0), axis=0).reshape(Z, Y, 2 * units)
+    hidden = (jax.nn.silu(both[..., :units]) * both[..., units:]).astype(BF16)
+    down = ffn[:, :, 2 * units : 3 * units]
+    part = jnp.einsum("byf,yxfk->bxk", hidden, down, preferred_element_type=F32).astype(BF16)
+    lowered = jnp.sum(swap(part.reshape(Z, 8, part_width // 8), "z").astype(F32), axis=0)
+    piece = (wide + lowered).astype(BF16)
+
+    piece = spread(piece, "z", Z).reshape(Z, part_width)
+    piece = spread(piece, ("y", "x"), Y * X).reshape(Y * X * Z, part_width)
+    whole = spread(piece, "c", C)
     mean_square = jnp.sum(jnp.square(whole.astype(F32)), axis=(0, 2)) / width
-    gain = final_gain.reshape(X, C, width // (X * C)).transpose(1, 0, 2).reshape(C, 1, width // C)
+    gain = final_gain.reshape(X, C, seg).transpose(1, 0, 2).reshape(C, 1, part_width)
     final = (whole.astype(F32) * lax.rsqrt(mean_square + EPSILON)[None, :, None] * gain).astype(BF16)
-    vocab = w_vocab.reshape(X, C, width // (X * C), w_vocab.shape[1]).transpose(1, 0, 2, 3)
-    vocab = vocab.reshape(C, width // C, w_vocab.shape[1])
+    vocab = w_vocab.reshape(X, C, seg, w_vocab.shape[1]).transpose(1, 0, 2, 3)
+    vocab = vocab.reshape(C, part_width, w_vocab.shape[1])
     logits = jnp.dot(final[0], vocab[0], preferred_element_type=F32)
     logits = logits + jnp.dot(final[1], vocab[1], preferred_element_type=F32)
-    logits = logits.astype(BF16).reshape(X, Y * Z, w_vocab.shape[1]).transpose(1, 0, 2)
-    return logits.reshape(X * Y * Z, w_vocab.shape[1])
+    logits = logits.astype(BF16).reshape(Y, X, Z, w_vocab.shape[1]).transpose(0, 2, 1, 3)
+    return logits.reshape(Y * X * Z, w_vocab.shape[1])
 
 
 def solution(mesh):

time: 242 us -> 201 us (0.83)
  blocking collectives: 96.2 us -> 58.1 us
  starting transfers between devices: 58.9 us -> 45.1 us
  waiting for transfers between devices: 50.5 us -> 59.7 us
  local copies, waits for them, and re-layouts: 7.77 us -> 11.3 us
  other arithmetic: 10.3 us -> 7.7 us
    all_gather x5 -> x1, blocking collectives: 64.9 us -> 3.37 us  [local(): lax.all_gather(part, 'c', axis=0)]
    all_to_all x5 -> x6, waiting for transfers between devices: 32.3 us -> 59.7 us  [swap(): return lax.all_to_all(values, axes, split_axis=0, concat_axis=0, tiled=True)]
    all_to_all x2 -> x4, blocking collectives: 31.3 us -> 51.8 us  [swap(): return lax.all_to_all(values, axes, split_axis=0, concat_axis=0, tiled=True)]
    all_gather x2 -> x1, waiting for transfers between devices: 18.2 us -> 0.02 us  [local(): ffn = lax.all_gather(ffn, ('y', 'x'), axis=0).reshape(Y, X, -1, seg)]
    all_to_all x5 -> x6, starting transfers between devices: 58.8 us -> 45 us  [swap(): return lax.all_to_all(values, axes, split_axis=0, concat_axis=0, tiled=True)]
    broadcast_in_dim x2 -> x0, other arithmetic: 2.88 us -> none  [spread(): return swap(jnp.broadcast_to(values[None], (count,) + values.shape), axes)]
    unnamed x0 -> x1, blocking collectives: none -> 2.86 us
  transfers between devices with their start and end apart: 7 -> 7, of which waited for: 5 -> 6; matrix products, arithmetic and copies ran while one was open for 2% -> 6% of each run, Pallas kernels for 0% -> 0%
where the time goes in v2:
time: 201 us; the launch traced here: 200 us
  waiting for transfers between devices  59.7 us (30%)
  blocking collectives  58.1 us (29%)
  starting transfers between devices  45.1 us (22%)
  between operations  14.5 us (7%)
  local copies, waits for them, and re-layouts  11.3 us (6%)
  other arithmetic  7.7 us (4%)
  matrix products  3.58 us (2%)
    all_to_all x6, waiting for transfers between devices, swap(): return lax.all_to_all(values, axes, split_axis=0, concat_axis=0, tiled=True)  59.7 us
    all_to_all x4, blocking collectives, swap(): return lax.all_to_all(values, axes, split_axis=0, concat_axis=0, tiled=True)  51.8 us
    all_to_all x6, starting transfers between devices, swap(): return lax.all_to_all(values, axes, split_axis=0, concat_axis=0, tiled=True)  45 us
  transfers between devices with their start and end apart: 7, of which 6 were waited for; matrix products, arithmetic and copies ran while one was open for 6% of the time, Pallas kernels for 0%

profile of v2, /device:TPU:1, one launch (start us, length us, event | category | flops | bytes accessed | tf_op | source)
XLA Modules:
  0.0 199.9 jit_solution(7150783157026090379)
XLA Ops:
  10.2 15.7 %all-to-all-start = ((bf16[16,72,128]{2,1,0:T(8,128)(2,1)}), bf16[16,72,128]{2,1,0:T(8,128)(2,1)S(1)}, u32[]{:S(2)}, u32[]{:S(2)}) async-start(bf16[16,72,128]{2,1,0:T(8,128)(2,1)} %pad_maximum_fusion), calls=%async_computation | async-start | bytes 589824 | tf_op jit(solution)/shard_map/all_to_all | solution.py:25
  26.0 1.5 pad_maximum_fusion.1
  27.9 11.8 %all-to-all-done = bf16[16,72,128]{2,1,0:T(8,128)(2,1)S(1)} async-done(((bf16[16,72,128]{2,1,0:T(8,128)(2,1)}), bf16[16,72,128]{2,1,0:T(8,128)(2,1)S(1)}, u32[]{:S(2)}, u32[]{:S(2)}) %all-to-all-start) | async-done | bytes 294944 | tf_op jit(solution)/shard_map/all_to_all | solution.py:25
  40.4 4.2 %all-to-all-start.1 = ((bf16[4,32,512]{2,1,0:T(8,128)(2,1)}), bf16[4,32,512]{2,1,0:T(8,128)(2,1)S(1)}, u32[]{:S(2)}, u32[]{:S(2)}) async-start(bf16[4,32,512]{2,1,0:T(8,128)(2,1)} %broadcast_in_dim.40), calls=%async_computation.1 | async-start | bytes 262144 | tf_op jit(solution)/shard_map/all_to_all | solution.py:25
  44.7 4.7 %all-to-all-done.1 = bf16[4,32,512]{2,1,0:T(8,128)(2,1)S(1)} async-done(((bf16[4,32,512]{2,1,0:T(8,128)(2,1)}), bf16[4,32,512]{2,1,0:T(8,128)(2,1)S(1)}, u32[]{:S(2)}, u32[]{:S(2)}) %all-to-all-start.1) | async-done | bytes 131104 | tf_op jit(solution)/shard_map/all_to_all | solution.py:25
  50.2 11.7 %all-to-all-start.2 = ((bf16[16,4,512]{2,1,0:T(4,128)(2,1)}), bf16[16,4,512]{2,1,0:T(4,128)(2,1)S(1)}, u32[]{:S(2)}, u32[]{:S(2)}) async-start(bf16[16,4,512]{2,1,0:T(4,128)(2,1)} %reshape.278), calls=%async_computation.2 | async-start | bytes 131072 | tf_op jit(solution)/shard_map/all_to_all | solution.py:25
  62.2 11.3 %all-to-all-done.2 = bf16[16,4,512]{2,1,0:T(4,128)(2,1)S(1)} async-done(((bf16[16,4,512]{2,1,0:T(4,128)(2,1)}), bf16[16,4,512]{2,1,0:T(4,128)(2,1)S(1)}, u32[]{:S(2)}, u32[]{:S(2)}) %all-to-all-start.2) | async-done | bytes 65568 | tf_op jit(solution)/shard_map/all_to_all | solution.py:25
  73.5 1.1 broadcast_in_dim.43
  74.6 3.7 %all-to-all-start.3 = ((bf16[4,2,512,128]{3,2,1,0:T(8,128)(2,1)}), bf16[4,2,512,128]{3,2,1,0:T(8,128)(2,1)S(1)}, u32[]{:S(2)}, u32[]{:S(2)}) async-start(bf16[4,2,512,128]{3,2,1,0:T(8,128)(2,1)} %broadcast_in_dim.43), calls=%async_computation.3 | async-start | bytes 2097152 | tf_op jit(solution)/shard_map/all_to_all | solution.py:25
  79.5 20.4 %all-to-all-done.3 = bf16[4,2,512,128]{3,2,1,0:T(8,128)(2,1)S(1)} async-done(((bf16[4,2,512,128]{3,2,1,0:T(8,128)(2,1)}), bf16[4,2,512,128]{3,2,1,0:T(8,128)(2,1)S(1)}, u32[]{:S(2)}, u32[]{:S(2)}) %all-to-all-start.3) | async-done | bytes 1048608 | tf_op jit(solution)/shard_map/all_to_all | solution.py:25
  101.1 6.1 %all-to-all-start.4 = ((f32[8,8,128]{2,1,0:T(8,128)}), f32[8,8,128]{2,1,0:T(8,128)S(1)}, u32[]{:S(2)}, u32[]{:S(2)}) async-start(f32[8,8,128]{2,1,0:T(8,128)} %reshape.282), calls=%async_computation.4 | async-start | bytes 65536 | tf_op jit(solution)/shard_map/all_to_all | solution.py:25
  108.4 1.3 dynamic-slice
  109.6 2.3 %all-to-all-done.4 = f32[8,8,128]{2,1,0:T(8,128)S(1)} async-done(((f32[8,8,128]{2,1,0:T(8,128)}), f32[8,8,128]{2,1,0:T(8,128)S(1)}, u32[]{:S(2)}, u32[]{:S(2)}) %all-to-all-start.4) | async-done | bytes 32800 | tf_op jit(solution)/shard_map/all_to_all | solution.py:25
  112.6 1.3 dynamic-update-slice
  113.9 2.9 %all-reduce = f32[2]{0:T(128)S(1)} all-reduce(f32[2]{0:T(128)S(1)} %dynamic-update-slice), channel_id=1, replica_groups=mesh['y'=4,'z'=16,'x'=4,'c'=2] {'c'}, use_global_device_ids=true, to_apply=%add | all-reduce | flops 2 | bytes 16
  118.1 16.3 %all_to_all.50 = bf16[16,8,128]{2,1,0:T(8,128)(2,1)S(1)} all-to-all(bf16[16,8,128]{2,1,0:T(8,128)(2,1)S(1)} %broadcast_in_dim.44), channel_id=1, replica_groups=mesh['y'=4,'z'=16,'x'=4,'c'=2] {'z'}, dimensions={0} | all-to-all | bytes 65536 | tf_op jit(solution)/shard_map/all_to_all | solution.py:25
  134.4 1.5 slice_bitcast_fusion
  136.6 3.4 %all-gather.1 = f32[32,768]{1,0:T(8,128)S(1)} all-gather(f32[16,768]{1,0:T(8,128)S(1)} %convolution_bitcast_fusion.1), channel_id=3, replica_groups=mesh['y'=4,'z'=16,'x'=4,'c'=2] {'c'}, dimensions={0}, use_global_device_ids=true | all-gather | bytes 147456 | tf_op jit(solution)/shard_map/all_gather | solution.py:126
  140.2 1.4 fusion.4
  141.6 14.1 %all_to_all.51 = bf16[16,8,128]{2,1,0:T(8,128)(2,1)S(1)} all-to-all(bf16[16,8,128]{2,1,0:T(8,128)(2,1)S(1)} %reshape.287), channel_id=1, replica_groups=mesh['y'=4,'z'=16,'x'=4,'c'=2] {'z'}, dimensions={0} | all-to-all | bytes 65536 | tf_op jit(solution)/shard_map/all_to_all | solution.py:25
  155.7 14.0 %all_to_all.52 = bf16[16,8,128]{2,1,0:T(8,128)(2,1)S(1)} all-to-all(bf16[16,8,128]{2,1,0:T(8,128)(2,1)S(1)} %broadcast_in_dim.45), channel_id=1, replica_groups=mesh['y'=4,'z'=16,'x'=4,'c'=2] {'z'}, dimensions={0} | all-to-all | bytes 65536 | tf_op jit(solution)/shard_map/all_to_all | solution.py:25
  170.6 3.6 %all-to-all-start.8 = ((bf16[16,16,1024]{2,1,0:T(8,128)(2,1)}), bf16[16,16,1024]{2,1,0:T(8,128)(2,1)S(1)}, u32[]{:S(2)}, u32[]{:S(2)}) async-start(bf16[16,16,1024]{2,1,0:T(8,128)(2,1)} %broadcast_in_dim.47), calls=%async_computation.8 | async-start | bytes 1048576 | tf_op jit(solution)/shard_map/all_to_all | solution.py:25
  174.3 9.2 %all-to-all-done.8 = bf16[16,16,1024]{2,1,0:T(8,128)(2,1)S(1)} async-done(((bf16[16,16,1024]{2,1,0:T(8,128)(2,1)}), bf16[16,16,1024]{2,1,0:T(8,128)(2,1)S(1)}, u32[]{:S(2)}, u32[]{:S(2)}) %all-to-all-start.8) | async-done | bytes 524320 | tf_op jit(solution)/shard_map/all_to_all | solution.py:25
  183.6 7.4 %all_to_all.53 = bf16[2,256,1024]{2,1,0:T(8,128)(2,1)S(1)} all-to-all(bf16[2,256,1024]{2,1,0:T(8,128)(2,1)S(1)} %broadcast_in_dim.49), channel_id=1, replica_groups=mesh['y'=4,'z'=16,'x'=4,'c'=2] {'c'}, dimensions={0} | all-to-all | bytes 2097152 | tf_op jit(solution)/shard_map/all_to_all | solution.py:25
  (101 shorter events, 14.5 us)
Async XLA Ops:
  6.5 55.4 %copy-start = (bf16[1,2048,2]{1,2,0:T(2,128)(2,1)S(1)}, bf16[1,2048,2]{1,2,0:T(2,128)(2,1)}, u32[]{:S(2)}) copy-start(bf16[1,2048,2]{1,2,0:T(2,128)(2,1)} %param.19) | copy-start | bytes 24580
  6.5 21.0 %copy-start.8 = (s32[256]{0:T(256)S(1)}, s32[256]{0:T(256)}, u32[]{:S(2)}) copy-start(s32[256]{0:T(256)} %param.16) | copy-start | bytes 3076
  6.5 33.2 %copy-start.3 = (bf16[1,32,1,512]{3,1,2,0:T(8,128)(2,1)S(1)}, bf16[1,32,1,512]{3,1,2,0:T(8,128)(2,1)}, u32[]{:S(2)}) copy-start(bf16[1,32,1,512]{3,1,2,0:T(8,128)(2,1)} %param.18) | copy-start | bytes 98308
  10.2 29.5 %all-to-all-start = ((bf16[16,72,128]{2,1,0:T(8,128)(2,1)}), bf16[16,72,128]{2,1,0:T(8,128)(2,1)S(1)}, u32[]{:S(2)}, u32[]{:S(2)}) async-start(bf16[16,72,128]{2,1,0:T(8,128)(2,1)} %pad_maximum_fusion), calls=%async_computation | async-start | bytes 589824 | tf_op jit(solution)/shard_map/all_to_all | solution.py:25
  26.0 108.4 %all-gather.4.cloned.1.call-start = ((), (), s32[]{:S(2)}) async-start(), calls=%async_computation.10 | async-start | bytes 2506752 | tf_op jit(solution)/shard_map/all_gather | solution.py:59
  40.4 9.0 %all-to-all-start.1 = ((bf16[4,32,512]{2,1,0:T(8,128)(2,1)}), bf16[4,32,512]{2,1,0:T(8,128)(2,1)S(1)}, u32[]{:S(2)}, u32[]{:S(2)}) async-start(bf16[4,32,512]{2,1,0:T(8,128)(2,1)} %broadcast_in_dim.40), calls=%async_computation.1 | async-start | bytes 262144 | tf_op jit(solution)/shard_map/all_to_all | solution.py:25
  50.2 23.3 %all-to-all-start.2 = ((bf16[16,4,512]{2,1,0:T(4,128)(2,1)}), bf16[16,4,512]{2,1,0:T(4,128)(2,1)S(1)}, u32[]{:S(2)}, u32[]{:S(2)}) async-start(bf16[16,4,512]{2,1,0:T(4,128)(2,1)} %reshape.278), calls=%async_computation.2 | async-start | bytes 131072 | tf_op jit(solution)/shard_map/all_to_all | solution.py:25
  62.1 16.4 %copy-start.6 = (f32[1,128]{1,0:T(1,128)S(1)}, f32[1,128]{1,0:T(1,128)}, u32[]{:S(2)}) copy-start(f32[1,128]{1,0:T(1,128)} %param.23) | copy-start | bytes 1540
  62.1 16.7 %copy-start.7 = (f32[1,128]{1,0:T(1,128)S(1)}, f32[1,128]{1,0:T(1,128)}, u32[]{:S(2)}) copy-start(f32[1,128]{1,0:T(1,128)} %param.22) | copy-start | bytes 1540
  62.1 17.0 %copy-start.9 = (bf16[1,2,1024,1,128]{4,2,3,1,0:T(8,128)(2,1)S(1)}, bf16[1,2,1024,1,128]{4,2,3,1,0:T(8,128)(2,1)}, u32[]{:S(2)}) copy-start(bf16[1,2,1024,1,128]{4,2,3,1,0:T(8,128)(2,1)} %param.17) | copy-start | bytes 1572868
  74.6 32.6 %copy-start.2 = (bf16[4,2048]{1,0:T(4,128)(2,1)S(1)}, bf16[4,2048]{1,0:T(4,128)(2,1)}, u32[]{:S(2)}) copy-start(bf16[4,2048]{1,0:T(4,128)(2,1)} %param.15) | copy-start | bytes 49156
  74.6 33.2 %copy-start.4 = (f32[1,2048]{1,0:T(1,128)S(1)}, f32[1,2048]{1,0:T(1,128)}, u32[]{:S(2)}) copy-start(f32[1,2048]{1,0:T(1,128)} %param.24) | copy-start | bytes 24580
  74.6 25.3 %all-to-all-start.3 = ((bf16[4,2,512,128]{3,2,1,0:T(8,128)(2,1)}), bf16[4,2,512,128]{3,2,1,0:T(8,128)(2,1)S(1)}, u32[]{:S(2)}, u32[]{:S(2)}) async-start(bf16[4,2,512,128]{3,2,1,0:T(8,128)(2,1)} %broadcast_in_dim.43), calls=%async_computation.3 | async-start | bytes 2097152 | tf_op jit(solution)/shard_map/all_to_all | solution.py:25
  101.1 10.9 %all-to-all-start.4 = ((f32[8,8,128]{2,1,0:T(8,128)}), f32[8,8,128]{2,1,0:T(8,128)S(1)}, u32[]{:S(2)}, u32[]{:S(2)}) async-start(f32[8,8,128]{2,1,0:T(8,128)} %reshape.282), calls=%async_computation.4 | async-start | bytes 65536 | tf_op jit(solution)/shard_map/all_to_all | solution.py:25
  136.6 37.6 %copy-start.5 = (f32[2048]{0:T(1024)S(1)}, f32[2048]{0:T(1024)}, u32[]{:S(2)}) copy-start(f32[2048]{0:T(1024)} %param.28) | copy-start | bytes 24580
  136.6 37.6 %copy-start.1 = (bf16[2048,256]{1,0:T(8,128)(2,1)S(1)}, bf16[2048,256]{1,0:T(8,128)(2,1)}, u32[]{:S(2)}) copy-start(bf16[2048,256]{1,0:T(8,128)(2,1)} %param.29) | copy-start | bytes 3145732
  170.6 12.8 %all-to-all-start.8 = ((bf16[16,16,1024]{2,1,0:T(8,128)(2,1)}), bf16[16,16,1024]{2,1,0:T(8,128)(2,1)S(1)}, u32[]{:S(2)}, u32[]{:S(2)}) async-start(bf16[16,16,1024]{2,1,0:T(8,128)(2,1)} %broadcast_in_dim.47), calls=%async_computation.8 | async-start | bytes 1048576 | tf_op jit(solution)/shard_map/all_to_all | solution.py:25
Sparse Core Ops, SparseCore 0:
  29.8 65.8 all-gather.3

commit v3 on v2

--- a/solution.py
+++ b/solution.py
@@ -56,8 +56,8 @@
     ix, ic = lax.axis_index("x"), lax.axis_index("c")
 
     ffn = jnp.concatenate([w_gate[0].T, w_up[0].T, w_down[0]], axis=0)
-    ffn = lax.all_gather(ffn, ("y", "x"), axis=0).reshape(Y, X, -1, seg)
-    qkv_block = spread(w_qkv[0, :, 0], "y", Y).reshape(-1, columns)
+    ffn = lax.all_gather(ffn, "x", axis=0).reshape(1, X, -1, seg)
+    qkv_block = lax.all_gather(w_qkv[0, :, 0], "y", axis=0, tiled=True)
 
     positions = lax.dynamic_slice_in_dim(lengths, req * rows, rows)
     starts = jnp.cumsum(positions) - positions
@@ -78,7 +78,7 @@
     out_block = arrived[:, 8:].reshape(Z, 2, -1, head_dim).transpose(1, 0, 2, 3).reshape(2, -1, head_dim)
     part = jnp.dot(batch, qkv_block, preferred_element_type=F32).astype(BF16)
     qkv = jnp.sum(swap(part.reshape(Z, rows, columns), "z").astype(F32), axis=0)
-    out_block = spread(out_block, "y", Y)
+    out_block = lax.all_gather(out_block, "y", axis=0)
 
     half = head_dim // 2
     frequency = ROPE_THETA ** (-2.0 * jnp.arange(half, dtype=F32) / head_dim)
@@ -116,19 +116,20 @@
         return lax.dynamic_slice_in_dim(gain.reshape(X, C, seg), ic, 1, 1).reshape(8, part_width // 8)
 
     stream = (mine(tokens).astype(F32) + projected).astype(BF16)
-    wide = stream.astype(F32)
-    squares = jnp.sum(lax.all_gather(jnp.sum(wide * wide).reshape(1, 1), "c", axis=0)) / width
-    normed_two = (wide * lax.rsqrt(squares + EPSILON) * half_of(post_gain[0])).astype(BF16)
 
-    batch = spread(normed_two, "z", Z).reshape(Z, X, seg)
-    part = jnp.einsum("bxk,yxfk->byf", batch, ffn[:, :, : 2 * units], preferred_element_type=F32)
-    part = part.reshape(Z, Y * 2 * units)
-    both = jnp.sum(lax.all_gather(part, "c", axis=0), axis=0).reshape(Z, Y, 2 * units)
-    hidden = (jax.nn.silu(both[..., :units]) * both[..., units:]).astype(BF16)
-    down = ffn[:, :, 2 * units : 3 * units]
-    part = jnp.einsum("byf,yxfk->bxk", hidden, down, preferred_element_type=F32).astype(BF16)
-    lowered = jnp.sum(swap(part.reshape(Z, 8, part_width // 8), "z").astype(F32), axis=0)
-    piece = (wide + lowered).astype(BF16)
+    batch = spread(stream, ("y", "z"), Y * Z).reshape(Y * Z, part_width)
+    wide = batch.astype(F32)
+    squares = jnp.sum(wide * wide, axis=-1, keepdims=True)
+    batch = (wide * half_of(post_gain[0]).reshape(1, part_width)).astype(BF16).reshape(Y * Z, X, seg)
+    part = jnp.einsum("bxk,xfk->bf", batch, ffn[0, :, : 2 * units], preferred_element_type=F32)
+    part = jnp.concatenate([part, jnp.broadcast_to(squares, (Y * Z, 256 - 2 * units))], axis=1)
+    both = jnp.sum(lax.all_gather(part, "c", axis=0), axis=0)
+    both = both[:, : 2 * units] * lax.rsqrt(both[:, 2 * units :][:, :1] / width + EPSILON)
+    hidden = (jax.nn.silu(both[:, :units]) * both[:, units:]).astype(BF16)
+    down = ffn[0, :, 2 * units :]
+    part = jnp.einsum("bf,xfk->bxk", hidden, down, preferred_element_type=F32).astype(BF16)
+    lowered = jnp.sum(swap(part.reshape((Y * Z), 8, part_width // 8), ("y", "z")).astype(F32), axis=0)
+    piece = (stream.astype(F32) + lowered).astype(BF16)
 
     piece = spread(piece, "z", Z).reshape(Z, part_width)
     piece = spread(piece, ("y", "x"), Y * X).reshape(Y * X * Z, part_width)

time: 201 us -> 212 us (1.055)
  blocking collectives: 58.1 us -> 77.4 us
  waiting for transfers between devices: 59.7 us -> 52 us
  starting transfers between devices: 45.1 us -> 51.8 us
  local copies, waits for them, and re-layouts: 11.3 us -> 6.89 us
    all_to_all x6 -> x5, waiting for transfers between devices: 59.7 us -> 29.3 us  [swap(): return lax.all_to_all(values, axes, split_axis=0, concat_axis=0, tiled=True)]
    all_gather x1, waiting for transfers between devices: 0.02 us -> 22.7 us  [local(): out_block = lax.all_gather(out_block, 'y', axis=0)]
    all_gather x1 -> x3, blocking collectives: 3.37 us -> 25.8 us  [the longest x1 10.9 us: local(): ffn = lax.all_gather(ffn, 'x', axis=0).reshape(1, X, -1, seg)]
    all_to_all x6 -> x5, starting transfers between devices: 45 us -> 51.7 us  [swap(): return lax.all_to_all(values, axes, split_axis=0, concat_axis=0, tiled=True)]
    unnamed x1 -> x0, blocking collectives: 2.86 us -> none
    unnamed x25 -> x29, local copies, waits for them, and re-layouts: 3.13 us -> 0.66 us
    all_to_all x4 -> x3, blocking collectives: 51.8 us -> 51.6 us  [swap(): return lax.all_to_all(values, axes, split_axis=0, concat_axis=0, tiled=True)]
  transfers between devices with their start and end apart: 7 -> 6, of which waited for: 6 -> 6; matrix products, arithmetic and copies ran while one was open for 6% -> 2% of each run, Pallas kernels for 0% -> 0%
where the time goes in v3:
time: 212 us; the launch traced here: 211 us
  blocking collectives  77.4 us (37%)
  waiting for transfers between devices  52 us (25%)
  starting transfers between devices  51.8 us (24%)
  between operations  13.8 us (7%)
  local copies, waits for them, and re-layouts  6.89 us (3%)
  other arithmetic  6.1 us (3%)
  matrix products  3.39 us (2%)
    all_to_all x5, starting transfers between devices, swap(): return lax.all_to_all(values, axes, split_axis=0, concat_axis=0, tiled=True)  51.7 us
    all_to_all x3, blocking collectives, swap(): return lax.all_to_all(values, axes, split_axis=0, concat_axis=0, tiled=True)  51.6 us
    all_to_all x5, waiting for transfers between devices, swap(): return lax.all_to_all(values, axes, split_axis=0, concat_axis=0, tiled=True)  29.3 us
    all_gather x1, waiting for transfers between devices, local(): out_block = lax.all_gather(out_block, 'y', axis=0)  22.7 us
    all_gather x1, blocking collectives, local(): ffn = lax.all_gather(ffn, 'x', axis=0).reshape(1, X, -1, seg)  10.9 us
    all_gather x1, blocking collectives, local(): qkv_block = lax.all_gather(w_qkv[0, :, 0], 'y', axis=0, tiled=True)  10 us
    all_gather x1, blocking collectives, local(): both = jnp.sum(lax.all_gather(part, 'c', axis=0), axis=0)  4.88 us
  transfers between devices with their start and end apart: 6, of which 6 were waited for; matrix products, arithmetic and copies ran while one was open for 2% of the time, Pallas kernels for 0%

profile of v3, /device:TPU:1, one launch (start us, length us, event | category | flops | bytes accessed | tf_op | source)
XLA Modules:
  0.0 211.3 jit_solution(15335214985497814821)
XLA Ops:
  6.5 0.9 fusion.22
  7.4 0.7 fusion.46
  8.2 0.8 fusion.24
  9.4 0.8 pad_maximum_fusion
  10.2 15.7 %all-to-all-start = ((bf16[16,72,128]{2,1,0:T(8,128)(2,1)}), bf16[16,72,128]{2,1,0:T(8,128)(2,1)S(1)}, u32[]{:S(2)}, u32[]{:S(2)}) async-start(bf16[16,72,128]{2,1,0:T(8,128)(2,1)} %pad_maximum_fusion), calls=%async_computation | async-start | bytes 589824 | tf_op jit(solution)/shard_map/all_to_all | solution.py:25
  26.2 10.0 %all-gather = bf16[1,128,1,512]{3,1,2,0:T(8,128)(2,1)S(1)} all-gather(bf16[1,32,1,512]{3,1,2,0:T(8,128)(2,1)S(1)} %copy-done.6), channel_id=2, replica_groups=mesh['y'=4,'z'=16,'x'=4,'c'=2] {'y'}, dimensions={1}, use_global_device_ids=true | all-gather | bytes 163840 | tf_op jit(solution)/shard_map/all_gather | solution.py:60
  36.4 3.3 %all-to-all-done = bf16[16,72,128]{2,1,0:T(8,128)(2,1)S(1)} async-done(((bf16[16,72,128]{2,1,0:T(8,128)(2,1)}), bf16[16,72,128]{2,1,0:T(8,128)(2,1)S(1)}, u32[]{:S(2)}, u32[]{:S(2)}) %all-to-all-start) | async-done | bytes 294944 | tf_op jit(solution)/shard_map/all_to_all | solution.py:25
  40.5 11.7 %all-to-all-start.1 = ((bf16[16,4,512]{2,1,0:T(4,128)(2,1)}), bf16[16,4,512]{2,1,0:T(4,128)(2,1)S(1)}, u32[]{:S(2)}, u32[]{:S(2)}) async-start(bf16[16,4,512]{2,1,0:T(4,128)(2,1)} %reshape.262), calls=%async_computation.1 | async-start | bytes 131072 | tf_op jit(solution)/shard_map/all_to_all | solution.py:25
  52.5 0.7 copy.49
  53.3 10.5 %all-to-all-done.1 = bf16[16,4,512]{2,1,0:T(4,128)(2,1)S(1)} async-done(((bf16[16,4,512]{2,1,0:T(4,128)(2,1)}), bf16[16,4,512]{2,1,0:T(4,128)(2,1)S(1)}, u32[]{:S(2)}, u32[]{:S(2)}) %all-to-all-start.1) | async-done | bytes 65568 | tf_op jit(solution)/shard_map/all_to_all | solution.py:25
  65.0 22.7 %all-gather.5.cloned.1.call-done = bf16[4,2,512,128]{3,2,1,0:T(8,128)(2,1)} async-done(((bf16[1,2,512,128]{3,2,1,0:T(8,128)(2,1)}), bf16[4,2,512,128]{3,2,1,0:T(8,128)(2,1)}) %all-gather.5.cloned.1.call-update) | async-done | bytes 1048592 | tf_op jit(solution)/shard_map/all_gather | solution.py:81
  87.7 1.7 convolution_bitcast_fusion.1
  90.1 5.8 %all-to-all-start.2 = ((f32[8,8,128]{2,1,0:T(8,128)}), f32[8,8,128]{2,1,0:T(8,128)S(1)}, u32[]{:S(2)}, u32[]{:S(2)}) async-start(f32[8,8,128]{2,1,0:T(8,128)} %reshape.266), calls=%async_computation.2 | async-start | bytes 65536 | tf_op jit(solution)/shard_map/all_to_all | solution.py:25
  95.9 4.7 %all-to-all-done.2 = f32[8,8,128]{2,1,0:T(8,128)S(1)} async-done(((f32[8,8,128]{2,1,0:T(8,128)}), f32[8,8,128]{2,1,0:T(8,128)S(1)}, u32[]{:S(2)}, u32[]{:S(2)}) %all-to-all-start.2) | async-done | bytes 32800 | tf_op jit(solution)/shard_map/all_to_all | solution.py:25
  101.3 14.4 %all-to-all-start.3 = ((bf16[64,8,128]{2,1,0:T(8,128)(2,1)}), bf16[64,8,128]{2,1,0:T(8,128)(2,1)S(1)}, u32[]{:S(2)}, u32[]{:S(2)}) async-start(bf16[64,8,128]{2,1,0:T(8,128)(2,1)} %broadcast_in_dim.34), calls=%async_computation.3 | async-start | bytes 262144 | tf_op jit(solution)/shard_map/all_to_all | solution.py:25
  117.1 10.9 %all-gather.1 = bf16[1152,256]{1,0:T(8,128)(2,1)S(1)} all-gather(bf16[288,256]{1,0:T(8,128)(2,1)S(1)} %pad_maximum_fusion.1), channel_id=3, replica_groups=mesh['y'=4,'z'=16,'x'=4,'c'=2] {'x'}, dimensions={0}, use_global_device_ids=true | all-gather | bytes 737280 | tf_op jit(solution)/shard_map/all_gather | solution.py:59
  128.0 1.6 all-to-all-done.3
  130.8 4.9 %all-gather.2 = f32[128,256]{1,0:T(8,128)S(1)} all-gather(f32[64,256]{1,0:T(8,128)S(1)} %pad_maximum_fusion.2), channel_id=4, replica_groups=mesh['y'=4,'z'=16,'x'=4,'c'=2] {'c'}, dimensions={0}, use_global_device_ids=true | all-gather | bytes 196608 | tf_op jit(solution)/shard_map/all_gather | solution.py:126
  136.4 27.9 %all_to_all.40 = bf16[64,8,128]{2,1,0:T(8,128)(2,1)S(1)} all-to-all(bf16[64,8,128]{2,1,0:T(8,128)(2,1)S(1)} %reshape.268), channel_id=1, replica_groups=mesh['y'=4,'z'=16,'x'=4,'c'=2] {'y','z'}, dimensions={0} | all-to-all | bytes 262144 | tf_op jit(solution)/shard_map/all_to_all | solution.py:25
  164.4 16.1 %all_to_all.41 = bf16[16,8,128]{2,1,0:T(8,128)(2,1)S(1)} all-to-all(bf16[16,8,128]{2,1,0:T(8,128)(2,1)S(1)} %broadcast_in_dim.36), channel_id=1, replica_groups=mesh['y'=4,'z'=16,'x'=4,'c'=2] {'z'}, dimensions={0} | all-to-all | bytes 65536 | tf_op jit(solution)/shard_map/all_to_all | solution.py:25
  180.6 0.9 broadcast_in_dim.38
  181.4 4.1 %all-to-all-start.6 = ((bf16[16,16,1024]{2,1,0:T(8,128)(2,1)}), bf16[16,16,1024]{2,1,0:T(8,128)(2,1)S(1)}, u32[]{:S(2)}, u32[]{:S(2)}) async-start(bf16[16,16,1024]{2,1,0:T(8,128)(2,1)} %broadcast_in_dim.38), calls=%async_computation.6 | async-start | bytes 1048576 | tf_op jit(solution)/shard_map/all_to_all | solution.py:25
  185.6 9.2 %all-to-all-done.6 = bf16[16,16,1024]{2,1,0:T(8,128)(2,1)S(1)} async-done(((bf16[16,16,1024]{2,1,0:T(8,128)(2,1)}), bf16[16,16,1024]{2,1,0:T(8,128)(2,1)S(1)}, u32[]{:S(2)}, u32[]{:S(2)}) %all-to-all-start.6) | async-done | bytes 524320 | tf_op jit(solution)/shard_map/all_to_all | solution.py:25
  194.9 7.6 %all_to_all.42 = bf16[2,256,1024]{2,1,0:T(8,128)(2,1)S(1)} all-to-all(bf16[2,256,1024]{2,1,0:T(8,128)(2,1)S(1)} %broadcast_in_dim.40), channel_id=1, replica_groups=mesh['y'=4,'z'=16,'x'=4,'c'=2] {'c'}, dimensions={0} | all-to-all | bytes 2097152 | tf_op jit(solution)/shard_map/all_to_all | solution.py:25
  (102 shorter events, 9.9 us)
Async XLA Ops:
  6.5 45.8 %copy-start = (bf16[1,2048,2]{1,2,0:T(2,128)(2,1)S(1)}, bf16[1,2048,2]{1,2,0:T(2,128)(2,1)}, u32[]{:S(2)}) copy-start(bf16[1,2048,2]{1,2,0:T(2,128)(2,1)} %param.19) | copy-start | bytes 24580
  6.5 19.4 %copy-start.11 = (s32[256]{0:T(256)S(1)}, s32[256]{0:T(256)}, u32[]{:S(2)}) copy-start(s32[256]{0:T(256)} %param.16) | copy-start | bytes 3076
  6.5 19.7 %copy-start.6 = (bf16[1,32,1,512]{3,1,2,0:T(8,128)(2,1)S(1)}, bf16[1,32,1,512]{3,1,2,0:T(8,128)(2,1)}, u32[]{:S(2)}) copy-start(bf16[1,32,1,512]{3,1,2,0:T(8,128)(2,1)} %param.18) | copy-start | bytes 98308
  9.3 43.0 %copy-start.2 = (bf16[4,2048]{1,0:T(4,128)(2,1)S(1)}, bf16[4,2048]{1,0:T(4,128)(2,1)}, u32[]{:S(2)}) copy-start(bf16[4,2048]{1,0:T(4,128)(2,1)} %param.15) | copy-start | bytes 49156
  10.2 29.5 %all-to-all-start = ((bf16[16,72,128]{2,1,0:T(8,128)(2,1)}), bf16[16,72,128]{2,1,0:T(8,128)(2,1)S(1)}, u32[]{:S(2)}, u32[]{:S(2)}) async-start(bf16[16,72,128]{2,1,0:T(8,128)(2,1)} %pad_maximum_fusion), calls=%async_computation | async-start | bytes 589824 | tf_op jit(solution)/shard_map/all_to_all | solution.py:25
  36.3 27.8 %copy-start.9 = (f32[1,128]{1,0:T(1,128)S(1)}, f32[1,128]{1,0:T(1,128)}, u32[]{:S(2)}) copy-start(f32[1,128]{1,0:T(1,128)} %param.23) | copy-start | bytes 1540
  36.3 28.1 %copy-start.10 = (f32[1,128]{1,0:T(1,128)S(1)}, f32[1,128]{1,0:T(1,128)}, u32[]{:S(2)}) copy-start(f32[1,128]{1,0:T(1,128)} %param.22) | copy-start | bytes 1540
  36.3 28.3 %copy-start.12 = (bf16[1,2,1024,1,128]{4,2,3,1,0:T(8,128)(2,1)S(1)}, bf16[1,2,1024,1,128]{4,2,3,1,0:T(8,128)(2,1)}, u32[]{:S(2)}) copy-start(bf16[1,2,1024,1,128]{4,2,3,1,0:T(8,128)(2,1)} %param.17) | copy-start | bytes 1572868
  40.5 23.3 %all-to-all-start.1 = ((bf16[16,4,512]{2,1,0:T(4,128)(2,1)}), bf16[16,4,512]{2,1,0:T(4,128)(2,1)S(1)}, u32[]{:S(2)}, u32[]{:S(2)}) async-start(bf16[16,4,512]{2,1,0:T(4,128)(2,1)} %reshape.262), calls=%async_computation.1 | async-start | bytes 131072 | tf_op jit(solution)/shard_map/all_to_all | solution.py:25
  52.2 35.4 %all-gather.5.cloned.1.call-start = ((), (), s32[]{:S(2)}) async-start(), calls=%async_computation.8 | async-start | bytes 1310720 | tf_op jit(solution)/shard_map/all_gather | solution.py:81
  65.0 51.3 %copy-start.7 = (f32[1,2048]{1,0:T(1,128)S(1)}, f32[1,2048]{1,0:T(1,128)}, u32[]{:S(2)}) copy-start(f32[1,2048]{1,0:T(1,128)} %param.24) | copy-start | bytes 24580
  87.6 29.4 %copy-start.3 = (bf16[1,96,256]{2,1,0:T(8,128)(2,1)S(1)}, bf16[1,96,256]{2,1,0:T(8,128)(2,1)}, u32[]{:S(2)}) copy-start(bf16[1,96,256]{2,1,0:T(8,128)(2,1)} %param.27) | copy-start | bytes 147460
  87.6 29.4 %copy-start.4 = (bf16[1,256,96]{1,2,0:T(8,128)(2,1)S(1)}, bf16[1,256,96]{1,2,0:T(8,128)(2,1)}, u32[]{:S(2)}) copy-start(bf16[1,256,96]{1,2,0:T(8,128)(2,1)} %param.26) | copy-start | bytes 147460
  87.7 29.4 %copy-start.5 = (bf16[1,256,96]{1,2,0:T(8,128)(2,1)S(1)}, bf16[1,256,96]{1,2,0:T(8,128)(2,1)}, u32[]{:S(2)}) copy-start(bf16[1,256,96]{1,2,0:T(8,128)(2,1)} %param.25) | copy-start | bytes 147460
  90.1 10.5 %all-to-all-start.2 = ((f32[8,8,128]{2,1,0:T(8,128)}), f32[8,8,128]{2,1,0:T(8,128)S(1)}, u32[]{:S(2)}, u32[]{:S(2)}) async-start(f32[8,8,128]{2,1,0:T(8,128)} %reshape.266), calls=%async_computation.2 | async-start | bytes 65536 | tf_op jit(solution)/shard_map/all_to_all | solution.py:25
  101.3 28.4 %all-to-all-start.3 = ((bf16[64,8,128]{2,1,0:T(8,128)(2,1)}), bf16[64,8,128]{2,1,0:T(8,128)(2,1)S(1)}, u32[]{:S(2)}, u32[]{:S(2)}) async-start(bf16[64,8,128]{2,1,0:T(8,128)(2,1)} %broadcast_in_dim.34), calls=%async_computation.3 | async-start | bytes 262144 | tf_op jit(solution)/shard_map/all_to_all | solution.py:25
  136.4 49.1 %copy-start.8 = (f32[2048]{0:T(1024)S(1)}, f32[2048]{0:T(1024)}, u32[]{:S(2)}) copy-start(f32[2048]{0:T(1024)} %param.28) | copy-start | bytes 24580
  136.4 49.1 %copy-start.1 = (bf16[2048,256]{1,0:T(8,128)(2,1)S(1)}, bf16[2048,256]{1,0:T(8,128)(2,1)}, u32[]{:S(2)}) copy-start(bf16[2048,256]{1,0:T(8,128)(2,1)} %param.29) | copy-start | bytes 3145732
  181.4 13.4 %all-to-all-start.6 = ((bf16[16,16,1024]{2,1,0:T(8,128)(2,1)}), bf16[16,16,1024]{2,1,0:T(8,128)(2,1)S(1)}, u32[]{:S(2)}, u32[]{:S(2)}) async-start(bf16[16,16,1024]{2,1,0:T(8,128)(2,1)} %broadcast_in_dim.38), calls=%async_computation.6 | async-start | bytes 1048576 | tf_op jit(solution)/shard_map/all_to_all | solution.py:25
Sparse Core Ops, SparseCore 0:
  55.2 32.4 all-gather.4

commit v4 on v2

--- a/solution.py
+++ b/solution.py
@@ -57,7 +57,7 @@
 
     ffn = jnp.concatenate([w_gate[0].T, w_up[0].T, w_down[0]], axis=0)
     ffn = lax.all_gather(ffn, ("y", "x"), axis=0).reshape(Y, X, -1, seg)
-    qkv_block = spread(w_qkv[0, :, 0], "y", Y).reshape(-1, columns)
+    qkv_block = lax.all_gather(w_qkv[0, :, 0], "y", axis=0, tiled=True)
 
     positions = lax.dynamic_slice_in_dim(lengths, req * rows, rows)
     starts = jnp.cumsum(positions) - positions
@@ -75,10 +75,9 @@
     )
     arrived = swap(sent, "z")
     batch = arrived[:, :rows].reshape(Z * rows, Y * depth)
-    out_block = arrived[:, 8:].reshape(Z, 2, -1, head_dim).transpose(1, 0, 2, 3).reshape(2, -1, head_dim)
+    out_block = arrived[:, 8:].reshape(Z, 2, -1, head_dim)
     part = jnp.dot(batch, qkv_block, preferred_element_type=F32).astype(BF16)
     qkv = jnp.sum(swap(part.reshape(Z, rows, columns), "z").astype(F32), axis=0)
-    out_block = spread(out_block, "y", Y)
 
     half = head_dim // 2
     frequency = ROPE_THETA ** (-2.0 * jnp.arange(half, dtype=F32) / head_dim)
@@ -104,31 +103,39 @@
     attended = summed / total[..., None]
     mixed = (attended * head_gate[..., None]).astype(BF16)
 
-    part = jnp.einsum("rqd,yqnd->ryn", mixed, out_block, preferred_element_type=F32)
-    part = part.reshape(rows, Y, C, seg).transpose(0, 2, 1, 3).reshape(rows * C, 8, part_width // 8)
+    def own_row(array):
+        return lax.dynamic_slice_in_dim(array, ix, 1, 0)
+
+    def own_core(array, axis):
+        return lax.dynamic_slice_in_dim(array, ic, 1, axis)
+
+    residual = own_core(own_row(tokens).reshape(Y, C, seg), 1).reshape(Y, 2, head_dim)
+    sent = jnp.broadcast_to(mixed.transpose(1, 0, 2).reshape(1, 2 * rows, head_dim), (Y, 2 * rows, head_dim))
+    sent = jnp.concatenate([sent, residual, jnp.zeros((Y, 6, head_dim), BF16)], axis=1)
+    arrived = swap(sent, "y")
+    everyone = arrived[:, : 2 * rows].reshape(Y, 2, rows, head_dim)
+    residual = arrived[:, 2 * rows : 2 * rows + 2].reshape(8, head_dim)
+    part = jnp.einsum("yqrd,zqnd->yrzn", everyone, out_block, preferred_element_type=F32)
+    part = part.reshape(Y, rows, C, seg).transpose(1, 2, 0, 3).reshape(rows * C, 8, head_dim)
     projected = jnp.sum(swap(part, ("x", "c")), axis=0)
+    stream = (residual.astype(F32) + projected).astype(BF16).reshape(Y, 2, head_dim)
 
-    def mine(array):
-        row = lax.dynamic_slice_in_dim(array, ix, 1, 0).reshape(X, C, seg)
-        return lax.dynamic_slice_in_dim(row, ic, 1, 1).reshape(8, part_width // 8)
-
-    def half_of(gain):
-        return lax.dynamic_slice_in_dim(gain.reshape(X, C, seg), ic, 1, 1).reshape(8, part_width // 8)
-
-    stream = (mine(tokens).astype(F32) + projected).astype(BF16)
-    wide = stream.astype(F32)
-    squares = jnp.sum(lax.all_gather(jnp.sum(wide * wide).reshape(1, 1), "c", axis=0)) / width
-    normed_two = (wide * lax.rsqrt(squares + EPSILON) * half_of(post_gain[0])).astype(BF16)
-
-    batch = spread(normed_two, "z", Z).reshape(Z, X, seg)
+    sent = jnp.broadcast_to(stream[:, None], (Y, Z, 2, head_dim)).reshape(Y * Z, 2, head_dim)
+    batch = swap(sent, ("y", "z")).reshape(Y, Z, seg).transpose(1, 0, 2)
+    stream = lax.dynamic_slice_in_dim(batch, lax.axis_index("z"), 1, 0).reshape(8, head_dim)
+    wide = batch.astype(F32)
+    squares = jnp.sum(wide * wide, axis=(1, 2)).reshape(Z, 1)
+    batch = (wide * own_core(post_gain.reshape(X, C, seg), 1).reshape(X, seg)).astype(BF16)
     part = jnp.einsum("bxk,yxfk->byf", batch, ffn[:, :, : 2 * units], preferred_element_type=F32)
-    part = part.reshape(Z, Y * 2 * units)
-    both = jnp.sum(lax.all_gather(part, "c", axis=0), axis=0).reshape(Z, Y, 2 * units)
+    part = jnp.concatenate([part.reshape(Z, -1), jnp.broadcast_to(squares, (Z, head_dim))], axis=1)
+    both = jnp.sum(lax.all_gather(part, "c", axis=0), axis=0)
+    scale = lax.rsqrt(both[:, -1:] / width + EPSILON)
+    both = (both[:, :-head_dim] * scale).reshape(Z, Y, 2 * units)
     hidden = (jax.nn.silu(both[..., :units]) * both[..., units:]).astype(BF16)
     down = ffn[:, :, 2 * units : 3 * units]
     part = jnp.einsum("byf,yxfk->bxk", hidden, down, preferred_element_type=F32).astype(BF16)
     lowered = jnp.sum(swap(part.reshape(Z, 8, part_width // 8), "z").astype(F32), axis=0)
-    piece = (wide + lowered).astype(BF16)
+    piece = (stream.astype(F32) + lowered).astype(BF16)
 
     piece = spread(piece, "z", Z).reshape(Z, part_width)
     piece = spread(piece, ("y", "x"), Y * X).reshape(Y * X * Z, part_width)

time: 201 us -> 175 us (0.87)
  waiting for transfers between devices: 59.7 us -> 49.3 us
  blocking collectives: 58.1 us -> 48.7 us
  local copies, waits for them, and re-layouts: 11.3 us -> 6.26 us
    all_to_all x4 -> x3, blocking collectives: 51.8 us -> 34.6 us  [swap(): return lax.all_to_all(values, axes, split_axis=0, concat_axis=0, tiled=True)]
    all_gather x1 -> x2, blocking collectives: 3.37 us -> 14.1 us  [the longest x1 10.5 us: local(): qkv_block = lax.all_gather(w_qkv[0, :, 0], 'y', axis=0, tiled=True)]
    all_to_all x6, waiting for transfers between devices: 59.7 us -> 49.3 us  [swap(): return lax.all_to_all(values, axes, split_axis=0, concat_axis=0, tiled=True)]
    unnamed x1 -> x0, blocking collectives: 2.86 us -> none
    unnamed x25 -> x23, local copies, waits for them, and re-layouts: 3.13 us -> 0.56 us
  transfers between devices with their start and end apart: 7 -> 7, of which waited for: 6 -> 6; matrix products, arithmetic and copies ran while one was open for 6% -> 4% of each run, Pallas kernels for 0% -> 0%
where the time goes in v4:
time: 175 us; the launch traced here: 174 us
  waiting for transfers between devices  49.3 us (28%)
  blocking collectives  48.7 us (28%)
  starting transfers between devices  43.3 us (25%)
  between operations  13.8 us (8%)
  other arithmetic  7.57 us (4%)
  local copies, waits for them, and re-layouts  6.26 us (4%)
  matrix products  4.86 us (3%)
    all_to_all x6, waiting for transfers between devices, swap(): return lax.all_to_all(values, axes, split_axis=0, concat_axis=0, tiled=True)  49.3 us
    all_to_all x6, starting transfers between devices, swap(): return lax.all_to_all(values, axes, split_axis=0, concat_axis=0, tiled=True)  43.3 us
    all_to_all x3, blocking collectives, swap(): return lax.all_to_all(values, axes, split_axis=0, concat_axis=0, tiled=True)  34.6 us
    all_gather x1, blocking collectives, local(): qkv_block = lax.all_gather(w_qkv[0, :, 0], 'y', axis=0, tiled=True)  10.5 us
    all_gather x1, blocking collectives, local(): both = jnp.sum(lax.all_gather(part, 'c', axis=0), axis=0)  3.55 us
  transfers between devices with their start and end apart: 7, of which 6 were waited for; matrix products, arithmetic and copies ran while one was open for 4% of the time, Pallas kernels for 0%

profile of v4, /device:TPU:1, one launch (start us, length us, event | category | flops | bytes accessed | tf_op | source)
XLA Modules:
  0.0 173.8 jit_solution(16561820330700685380)
XLA Ops:
  7.3 0.8 fusion.31
  8.2 0.8 fusion.33
  9.4 0.8 pad_maximum_fusion
  10.3 15.7 %all-to-all-start = ((bf16[16,72,128]{2,1,0:T(8,128)(2,1)}), bf16[16,72,128]{2,1,0:T(8,128)(2,1)S(1)}, u32[]{:S(2)}, u32[]{:S(2)}) async-start(bf16[16,72,128]{2,1,0:T(8,128)(2,1)} %pad_maximum_fusion), calls=%async_computation | async-start | bytes 589824 | tf_op jit(solution)/shard_map/all_to_all | solution.py:25
  26.1 1.5 pad_maximum_fusion.1
  28.0 10.5 %all-gather = bf16[1,128,1,512]{3,1,2,0:T(8,128)(2,1)S(1)} all-gather(bf16[1,32,1,512]{3,1,2,0:T(8,128)(2,1)S(1)} %copy-done.3), channel_id=2, replica_groups=mesh['y'=4,'z'=16,'x'=4,'c'=2] {'y'}, dimensions={1}, use_global_device_ids=true | all-gather | bytes 163840 | tf_op jit(solution)/shard_map/all_gather | solution.py:60
  38.7 1.1 all-to-all-done
  40.6 11.7 %all-to-all-start.1 = ((bf16[16,4,512]{2,1,0:T(4,128)(2,1)}), bf16[16,4,512]{2,1,0:T(4,128)(2,1)S(1)}, u32[]{:S(2)}, u32[]{:S(2)}) async-start(bf16[16,4,512]{2,1,0:T(4,128)(2,1)} %reshape.274), calls=%async_computation.1 | async-start | bytes 131072 | tf_op jit(solution)/shard_map/all_to_all | solution.py:25
  52.5 11.3 %all-to-all-done.1 = bf16[16,4,512]{2,1,0:T(4,128)(2,1)S(1)} async-done(((bf16[16,4,512]{2,1,0:T(4,128)(2,1)}), bf16[16,4,512]{2,1,0:T(4,128)(2,1)S(1)}, u32[]{:S(2)}, u32[]{:S(2)}) %all-to-all-start.1) | async-done | bytes 65568 | tf_op jit(solution)/shard_map/all_to_all | solution.py:25
  65.9 4.2 %all-to-all-start.2 = ((bf16[4,16,128]{2,1,0:T(8,128)(2,1)}), bf16[4,16,128]{2,1,0:T(8,128)(2,1)S(1)}, u32[]{:S(2)}, u32[]{:S(2)}) async-start(bf16[4,16,128]{2,1,0:T(8,128)(2,1)} %maximum_maximum_fusion), calls=%async_computation.2 | async-start | bytes 32768 | tf_op jit(solution)/shard_map/all_to_all | solution.py:25
  70.2 4.2 %all-to-all-done.2 = bf16[4,16,128]{2,1,0:T(8,128)(2,1)S(1)} async-done(((bf16[4,16,128]{2,1,0:T(8,128)(2,1)}), bf16[4,16,128]{2,1,0:T(8,128)(2,1)S(1)}, u32[]{:S(2)}, u32[]{:S(2)}) %all-to-all-start.2) | async-done | bytes 16416 | tf_op jit(solution)/shard_map/all_to_all | solution.py:25
  74.6 13.2 %all_to_all.45 = f32[8,8,128]{2,1,0:T(8,128)S(1)} all-to-all(f32[8,8,128]{2,1,0:T(8,128)S(1)} %reshape.280), channel_id=1, replica_groups=mesh['y'=4,'z'=16,'x'=4,'c'=2] {'x','c'}, dimensions={0} | all-to-all | bytes 65536 | tf_op jit(solution)/shard_map/all_to_all | solution.py:25
  88.4 4.6 %all-to-all-start.4 = ((bf16[64,2,128]{2,1,0:T(2,128)(2,1)}), bf16[64,2,128]{2,1,0:T(2,128)(2,1)S(1)}, u32[]{:S(2)}, u32[]{:S(2)}) async-start(bf16[64,2,128]{2,1,0:T(2,128)(2,1)} %bitcast.34), calls=%async_computation.4 | async-start | bytes 65536 | tf_op jit(solution)/shard_map/all_to_all | solution.py:25
  94.2 12.1 %all-to-all-done.4 = bf16[64,2,128]{2,1,0:T(2,128)(2,1)S(1)} async-done(((bf16[64,2,128]{2,1,0:T(2,128)(2,1)}), bf16[64,2,128]{2,1,0:T(2,128)(2,1)S(1)}, u32[]{:S(2)}, u32[]{:S(2)}) %all-to-all-start.4) | async-done | bytes 32800 | tf_op jit(solution)/shard_map/all_to_all | solution.py:25
  106.4 1.9 %fusion.6 = f32[16,4,192]{2,0,1:T(8,128)S(1)} fusion(bf16[4,4,288,256]{3,2,1,0:T(8,128)(2,1)} %bitcast.143, bf16[4,16,256]{2,1,0:T(8,128)(2,1)S(1)} %reshape.282, f32[4,256]{1,0:T(4,128)S(1)} %bitcast.159), kind=kOutput, calls=%fused_computation.10 | convolution fusion | flops 25214976 | bytes 1658880 | tf_op jit(solution)/shard_map/bxk,yxfk->byf/dot_general | solution.py:129
  108.6 3.5 %all-gather.2 = f32[32,896]{1,0:T(8,128)S(1)} all-gather(f32[16,896]{1,0:T(8,128)S(1)} %pad_maximum_fusion.2), channel_id=4, replica_groups=mesh['y'=4,'z'=16,'x'=4,'c'=2] {'c'}, dimensions={0}, use_global_device_ids=true | all-gather | bytes 172032 | tf_op jit(solution)/shard_map/all_gather | solution.py:131
  112.6 1.4 fusion.9
  114.7 3.5 %all-to-all-start.5 = ((bf16[16,8,128]{2,1,0:T(8,128)(2,1)}), bf16[16,8,128]{2,1,0:T(8,128)(2,1)S(1)}, u32[]{:S(2)}, u32[]{:S(2)}) async-start(bf16[16,8,128]{2,1,0:T(8,128)(2,1)} %reshape.287), calls=%async_computation.5 | async-start | bytes 65536 | tf_op jit(solution)/shard_map/all_to_all | solution.py:25
  118.2 11.4 %all-to-all-done.5 = bf16[16,8,128]{2,1,0:T(8,128)(2,1)S(1)} async-done(((bf16[16,8,128]{2,1,0:T(8,128)(2,1)}), bf16[16,8,128]{2,1,0:T(8,128)(2,1)S(1)}, u32[]{:S(2)}, u32[]{:S(2)}) %all-to-all-start.5) | async-done | bytes 32800 | tf_op jit(solution)/shard_map/all_to_all | solution.py:25
  129.6 14.0 %all_to_all.46 = bf16[16,8,128]{2,1,0:T(8,128)(2,1)S(1)} all-to-all(bf16[16,8,128]{2,1,0:T(8,128)(2,1)S(1)} %broadcast_in_dim.45), channel_id=1, replica_groups=mesh['y'=4,'z'=16,'x'=4,'c'=2] {'z'}, dimensions={0} | all-to-all | bytes 65536 | tf_op jit(solution)/shard_map/all_to_all | solution.py:25
  143.6 0.9 broadcast_in_dim.47
  144.5 3.6 %all-to-all-start.7 = ((bf16[16,16,1024]{2,1,0:T(8,128)(2,1)}), bf16[16,16,1024]{2,1,0:T(8,128)(2,1)S(1)}, u32[]{:S(2)}, u32[]{:S(2)}) async-start(bf16[16,16,1024]{2,1,0:T(8,128)(2,1)} %broadcast_in_dim.47), calls=%async_computation.7 | async-start | bytes 1048576 | tf_op jit(solution)/shard_map/all_to_all | solution.py:25
  148.2 9.2 %all-to-all-done.7 = bf16[16,16,1024]{2,1,0:T(8,128)(2,1)S(1)} async-done(((bf16[16,16,1024]{2,1,0:T(8,128)(2,1)}), bf16[16,16,1024]{2,1,0:T(8,128)(2,1)S(1)}, u32[]{:S(2)}, u32[]{:S(2)}) %all-to-all-start.7) | async-done | bytes 524320 | tf_op jit(solution)/shard_map/all_to_all | solution.py:25
  157.5 7.5 %all_to_all.47 = bf16[2,256,1024]{2,1,0:T(8,128)(2,1)S(1)} all-to-all(bf16[2,256,1024]{2,1,0:T(8,128)(2,1)S(1)} %broadcast_in_dim.49), channel_id=1, replica_groups=mesh['y'=4,'z'=16,'x'=4,'c'=2] {'c'}, dimensions={0} | all-to-all | bytes 2097152 | tf_op jit(solution)/shard_map/all_to_all | solution.py:25
  (108 shorter events, 10.6 us)
Async XLA Ops:
  6.5 45.9 %copy-start = (bf16[1,2048,2]{1,2,0:T(2,128)(2,1)S(1)}, bf16[1,2048,2]{1,2,0:T(2,128)(2,1)}, u32[]{:S(2)}) copy-start(bf16[1,2048,2]{1,2,0:T(2,128)(2,1)} %param.19) | copy-start | bytes 24580
  6.5 21.4 %copy-start.2 = (bf16[4,2048]{1,0:T(4,128)(2,1)S(1)}, bf16[4,2048]{1,0:T(4,128)(2,1)}, u32[]{:S(2)}) copy-start(bf16[4,2048]{1,0:T(4,128)(2,1)} %param.15) | copy-start | bytes 49156
  6.5 21.1 %copy-start.8 = (s32[256]{0:T(256)S(1)}, s32[256]{0:T(256)}, u32[]{:S(2)}) copy-start(s32[256]{0:T(256)} %param.16) | copy-start | bytes 3076
  6.5 21.4 %copy-start.3 = (bf16[1,32,1,512]{3,1,2,0:T(8,128)(2,1)S(1)}, bf16[1,32,1,512]{3,1,2,0:T(8,128)(2,1)}, u32[]{:S(2)}) copy-start(bf16[1,32,1,512]{3,1,2,0:T(8,128)(2,1)} %param.18) | copy-start | bytes 98308
  6.5 57.5 %copy-start.6 = (f32[1,128]{1,0:T(1,128)S(1)}, f32[1,128]{1,0:T(1,128)}, u32[]{:S(2)}) copy-start(f32[1,128]{1,0:T(1,128)} %param.23) | copy-start | bytes 1540
  6.5 57.9 %copy-start.7 = (f32[1,128]{1,0:T(1,128)S(1)}, f32[1,128]{1,0:T(1,128)}, u32[]{:S(2)}) copy-start(f32[1,128]{1,0:T(1,128)} %param.22) | copy-start | bytes 1540
  6.6 58.2 %copy-start.9 = (bf16[1,2,1024,1,128]{4,2,3,1,0:T(8,128)(2,1)S(1)}, bf16[1,2,1024,1,128]{4,2,3,1,0:T(8,128)(2,1)}, u32[]{:S(2)}) copy-start(bf16[1,2,1024,1,128]{4,2,3,1,0:T(8,128)(2,1)} %param.17) | copy-start | bytes 1572868
  10.3 29.5 %all-to-all-start = ((bf16[16,72,128]{2,1,0:T(8,128)(2,1)}), bf16[16,72,128]{2,1,0:T(8,128)(2,1)S(1)}, u32[]{:S(2)}, u32[]{:S(2)}) async-start(bf16[16,72,128]{2,1,0:T(8,128)(2,1)} %pad_maximum_fusion), calls=%async_computation | async-start | bytes 589824 | tf_op jit(solution)/shard_map/all_to_all | solution.py:25
  26.0 67.5 %copy-start.4 = (f32[1,2048]{1,0:T(1,128)S(1)}, f32[1,2048]{1,0:T(1,128)}, u32[]{:S(2)}) copy-start(f32[1,2048]{1,0:T(1,128)} %param.24) | copy-start | bytes 24580
  26.0 80.4 %all-gather.5.cloned.1.call-start = ((), (), s32[]{:S(2)}) async-start(), calls=%async_computation.9 | async-start | bytes 2506752 | tf_op jit(solution)/shard_map/all_gather | solution.py:59
  40.6 23.3 %all-to-all-start.1 = ((bf16[16,4,512]{2,1,0:T(4,128)(2,1)}), bf16[16,4,512]{2,1,0:T(4,128)(2,1)S(1)}, u32[]{:S(2)}, u32[]{:S(2)}) async-start(bf16[16,4,512]{2,1,0:T(4,128)(2,1)} %reshape.274), calls=%async_computation.1 | async-start | bytes 131072 | tf_op jit(solution)/shard_map/all_to_all | solution.py:25
  65.9 8.4 %all-to-all-start.2 = ((bf16[4,16,128]{2,1,0:T(8,128)(2,1)}), bf16[4,16,128]{2,1,0:T(8,128)(2,1)S(1)}, u32[]{:S(2)}, u32[]{:S(2)}) async-start(bf16[4,16,128]{2,1,0:T(8,128)(2,1)} %maximum_maximum_fusion), calls=%async_computation.2 | async-start | bytes 32768 | tf_op jit(solution)/shard_map/all_to_all | solution.py:25
  88.4 17.8 %all-to-all-start.4 = ((bf16[64,2,128]{2,1,0:T(2,128)(2,1)}), bf16[64,2,128]{2,1,0:T(2,128)(2,1)S(1)}, u32[]{:S(2)}, u32[]{:S(2)}) async-start(bf16[64,2,128]{2,1,0:T(2,128)(2,1)} %bitcast.34), calls=%async_computation.4 | async-start | bytes 65536 | tf_op jit(solution)/shard_map/all_to_all | solution.py:25
  108.3 39.7 %copy-start.5 = (f32[2048]{0:T(1024)S(1)}, f32[2048]{0:T(1024)}, u32[]{:S(2)}) copy-start(f32[2048]{0:T(1024)} %param.28) | copy-start | bytes 24580
  108.3 39.8 %copy-start.1 = (bf16[2048,256]{1,0:T(8,128)(2,1)S(1)}, bf16[2048,256]{1,0:T(8,128)(2,1)}, u32[]{:S(2)}) copy-start(bf16[2048,256]{1,0:T(8,128)(2,1)} %param.29) | copy-start | bytes 3145732
  114.7 15.0 %all-to-all-start.5 = ((bf16[16,8,128]{2,1,0:T(8,128)(2,1)}), bf16[16,8,128]{2,1,0:T(8,128)(2,1)S(1)}, u32[]{:S(2)}, u32[]{:S(2)}) async-start(bf16[16,8,128]{2,1,0:T(8,128)(2,1)} %reshape.287), calls=%async_computation.5 | async-start | bytes 65536 | tf_op jit(solution)/shard_map/all_to_all | solution.py:25
  144.5 12.9 %all-to-all-start.7 = ((bf16[16,16,1024]{2,1,0:T(8,128)(2,1)}), bf16[16,16,1024]{2,1,0:T(8,128)(2,1)S(1)}, u32[]{:S(2)}, u32[]{:S(2)}) async-start(bf16[16,16,1024]{2,1,0:T(8,128)(2,1)} %broadcast_in_dim.47), calls=%async_computation.7 | async-start | bytes 1048576 | tf_op jit(solution)/shard_map/all_to_all | solution.py:25
Sparse Core Ops, SparseCore 0:
  29.9 61.9 all-gather.4

commit v5 on v4

--- a/solution.py
+++ b/solution.py
@@ -109,20 +109,14 @@
     def own_core(array, axis):
         return lax.dynamic_slice_in_dim(array, ic, 1, axis)
 
-    residual = own_core(own_row(tokens).reshape(Y, C, seg), 1).reshape(Y, 2, head_dim)
-    sent = jnp.broadcast_to(mixed.transpose(1, 0, 2).reshape(1, 2 * rows, head_dim), (Y, 2 * rows, head_dim))
-    sent = jnp.concatenate([sent, residual, jnp.zeros((Y, 6, head_dim), BF16)], axis=1)
-    arrived = swap(sent, "y")
-    everyone = arrived[:, : 2 * rows].reshape(Y, 2, rows, head_dim)
-    residual = arrived[:, 2 * rows : 2 * rows + 2].reshape(8, head_dim)
+    residual = own_core(own_row(tokens).reshape(Y, C, seg), 1).reshape(8, head_dim)
+    everyone = spread(mixed.transpose(1, 0, 2).reshape(2 * rows, head_dim), "y", Y).reshape(Y, 2, rows, head_dim)
     part = jnp.einsum("yqrd,zqnd->yrzn", everyone, out_block, preferred_element_type=F32)
-    part = part.reshape(Y, rows, C, seg).transpose(1, 2, 0, 3).reshape(rows * C, 8, head_dim)
-    projected = jnp.sum(swap(part, ("x", "c")), axis=0)
-    stream = (residual.astype(F32) + projected).astype(BF16).reshape(Y, 2, head_dim)
+    part = swap(part.reshape(Y * rows * C, 2, head_dim), ("y", "x", "c"))
+    projected = jnp.sum(part.reshape(Y, X * C, 2, head_dim), axis=1).reshape(8, head_dim)
+    stream = (residual.astype(F32) + projected).astype(BF16)
 
-    sent = jnp.broadcast_to(stream[:, None], (Y, Z, 2, head_dim)).reshape(Y * Z, 2, head_dim)
-    batch = swap(sent, ("y", "z")).reshape(Y, Z, seg).transpose(1, 0, 2)
-    stream = lax.dynamic_slice_in_dim(batch, lax.axis_index("z"), 1, 0).reshape(8, head_dim)
+    batch = spread(stream, "z", Z).reshape(Z, X, seg)
     wide = batch.astype(F32)
     squares = jnp.sum(wide * wide, axis=(1, 2)).reshape(Z, 1)
     batch = (wide * own_core(post_gain.reshape(X, C, seg), 1).reshape(X, seg)).astype(BF16)
@@ -134,20 +128,22 @@
     hidden = (jax.nn.silu(both[..., :units]) * both[..., units:]).astype(BF16)
     down = ffn[:, :, 2 * units : 3 * units]
     part = jnp.einsum("byf,yxfk->bxk", hidden, down, preferred_element_type=F32).astype(BF16)
-    lowered = jnp.sum(swap(part.reshape(Z, 8, part_width // 8), "z").astype(F32), axis=0)
-    piece = (stream.astype(F32) + lowered).astype(BF16)
+    lowered = jnp.sum(spread(part.reshape(Z, 8, head_dim), "z", Z).astype(F32), axis=0)
+    piece = (wide.reshape(Z, 8, head_dim) + lowered).astype(BF16).reshape(Z, part_width)
 
-    piece = spread(piece, "z", Z).reshape(Z, part_width)
-    piece = spread(piece, ("y", "x"), Y * X).reshape(Y * X * Z, part_width)
-    whole = spread(piece, "c", C)
-    mean_square = jnp.sum(jnp.square(whole.astype(F32)), axis=(0, 2)) / width
-    gain = final_gain.reshape(X, C, seg).transpose(1, 0, 2).reshape(C, 1, part_width)
-    final = (whole.astype(F32) * lax.rsqrt(mean_square + EPSILON)[None, :, None] * gain).astype(BF16)
-    vocab = w_vocab.reshape(X, C, seg, w_vocab.shape[1]).transpose(1, 0, 2, 3)
-    vocab = vocab.reshape(C, part_width, w_vocab.shape[1])
-    logits = jnp.dot(final[0], vocab[0], preferred_element_type=F32)
-    logits = logits + jnp.dot(final[1], vocab[1], preferred_element_type=F32)
-    logits = logits.astype(BF16).reshape(Y, X, Z, w_vocab.shape[1]).transpose(0, 2, 1, 3)
+    near = spread(piece, ("y", "x"), Y * X).reshape(Y * X * Z, part_width)
+    far = lax.ppermute(near, "c", [(0, 1), (1, 0)])
+    near, far = near.astype(F32), far.astype(F32)
+    mean_square = (jnp.sum(near * near, axis=-1, keepdims=True) + jnp.sum(far * far, axis=-1, keepdims=True)) / width
+    scale = lax.rsqrt(mean_square + EPSILON)
+
+    def scored(half, core):
+        gain = lax.dynamic_slice_in_dim(final_gain.reshape(X, C, seg), core, 1, 1).reshape(1, part_width)
+        vocab = lax.dynamic_slice_in_dim(w_vocab.reshape(X, C, seg, -1), core, 1, 1).reshape(part_width, -1)
+        return jnp.dot((half * scale * gain).astype(BF16), vocab, preferred_element_type=F32)
+
+    logits = (scored(near, ic) + scored(far, 1 - ic)).astype(BF16)
+    logits = logits.reshape(Y, X, Z, w_vocab.shape[1]).transpose(0, 2, 1, 3)
     return logits.reshape(Y * X * Z, w_vocab.shape[1])
 
 

time: 175 us -> 173 us (0.989)
  waiting for transfers between devices: 49.3 us -> 36.4 us
  starting transfers between devices: 43.3 us -> 52.9 us
  blocking collectives: 48.7 us -> 51.7 us
    all_to_all x6 -> x5, waiting for transfers between devices: 49.3 us -> 35.3 us  [swap(): return lax.all_to_all(values, axes, split_axis=0, concat_axis=0, tiled=True)]
    ppermute x0 -> x1, starting transfers between devices: none -> 9.05 us  [local(): far = lax.ppermute(near, 'c', [(0, 1), (1, 0)])]
    all_to_all x3 -> x2, blocking collectives: 34.6 us -> 38.4 us  [swap(): return lax.all_to_all(values, axes, split_axis=0, concat_axis=0, tiled=True)]
    all_to_all x6 -> x5, starting transfers between devices: 43.3 us -> 43.8 us  [swap(): return lax.all_to_all(values, axes, split_axis=0, concat_axis=0, tiled=True)]
where the time goes in v5:
time: 173 us; the launch traced here: 172 us
  starting transfers between devices  52.9 us (31%)
  blocking collectives  51.7 us (30%)
  waiting for transfers between devices  36.4 us (21%)
  between operations  13.9 us (8%)
  local copies, waits for them, and re-layouts  7.66 us (4%)
  other arithmetic  6.15 us (4%)
  matrix products  3.62 us (2%)
    all_to_all x5, starting transfers between devices, swap(): return lax.all_to_all(values, axes, split_axis=0, concat_axis=0, tiled=True)  43.8 us
    all_to_all x2, blocking collectives, swap(): return lax.all_to_all(values, axes, split_axis=0, concat_axis=0, tiled=True)  38.4 us
    all_to_all x5, waiting for transfers between devices, swap(): return lax.all_to_all(values, axes, split_axis=0, concat_axis=0, tiled=True)  35.3 us
    all_gather x1, blocking collectives, local(): qkv_block = lax.all_gather(w_qkv[0, :, 0], 'y', axis=0, tiled=True)  10.3 us
    ppermute x1, starting transfers between devices, local(): far = lax.ppermute(near, 'c', [(0, 1), (1, 0)])  9.05 us
  transfers between devices with their start and end apart: 7, of which 6 were waited for; matrix products, arithmetic and copies ran while one was open for 4% of the time, Pallas kernels for 0%

profile of v5, /device:TPU:1, one launch (start us, length us, event | category | flops | bytes accessed | tf_op | source)
XLA Modules:
  0.0 172.3 jit_solution(6725744875364825116)
XLA Ops:
  6.6 0.8 fusion.44
  7.3 0.9 fusion.27
  8.2 0.8 fusion.29
  9.4 0.8 pad_maximum_fusion
  10.3 15.7 %all-to-all-start = ((bf16[16,72,128]{2,1,0:T(8,128)(2,1)}), bf16[16,72,128]{2,1,0:T(8,128)(2,1)S(1)}, u32[]{:S(2)}, u32[]{:S(2)}) async-start(bf16[16,72,128]{2,1,0:T(8,128)(2,1)} %pad_maximum_fusion), calls=%async_computation | async-start | bytes 589824 | tf_op jit(solution)/shard_map/all_to_all | solution.py:25
  27.1 10.3 %all-gather = bf16[1,128,1,512]{3,1,2,0:T(8,128)(2,1)S(1)} all-gather(bf16[1,32,1,512]{3,1,2,0:T(8,128)(2,1)S(1)} %copy-done.6), channel_id=2, replica_groups=mesh['y'=4,'z'=16,'x'=4,'c'=2] {'y'}, dimensions={1}, use_global_device_ids=true | all-gather | bytes 163840 | tf_op jit(solution)/shard_map/all_gather | solution.py:60
  37.6 2.2 %all-to-all-done = bf16[16,72,128]{2,1,0:T(8,128)(2,1)S(1)} async-done(((bf16[16,72,128]{2,1,0:T(8,128)(2,1)}), bf16[16,72,128]{2,1,0:T(8,128)(2,1)S(1)}, u32[]{:S(2)}, u32[]{:S(2)}) %all-to-all-start) | async-done | bytes 294944 | tf_op jit(solution)/shard_map/all_to_all | solution.py:25
  40.6 11.7 %all-to-all-start.1 = ((bf16[16,4,512]{2,1,0:T(4,128)(2,1)}), bf16[16,4,512]{2,1,0:T(4,128)(2,1)S(1)}, u32[]{:S(2)}, u32[]{:S(2)}) async-start(bf16[16,4,512]{2,1,0:T(4,128)(2,1)} %reshape.292), calls=%async_computation.1 | async-start | bytes 131072 | tf_op jit(solution)/shard_map/all_to_all | solution.py:25
  52.5 11.4 %all-to-all-done.1 = bf16[16,4,512]{2,1,0:T(4,128)(2,1)S(1)} async-done(((bf16[16,4,512]{2,1,0:T(4,128)(2,1)}), bf16[16,4,512]{2,1,0:T(4,128)(2,1)S(1)}, u32[]{:S(2)}, u32[]{:S(2)}) %all-to-all-start.1) | async-done | bytes 65568 | tf_op jit(solution)/shard_map/all_to_all | solution.py:25
  65.9 4.2 %all-to-all-start.2 = ((bf16[4,8,128]{2,1,0:T(8,128)(2,1)}), bf16[4,8,128]{2,1,0:T(8,128)(2,1)S(1)}, u32[]{:S(2)}, u32[]{:S(2)}) async-start(bf16[4,8,128]{2,1,0:T(8,128)(2,1)} %broadcast_in_dim.37), calls=%async_computation.2 | async-start | bytes 16384 | tf_op jit(solution)/shard_map/all_to_all | solution.py:25
  70.1 4.1 %all-to-all-done.2 = bf16[4,8,128]{2,1,0:T(8,128)(2,1)S(1)} async-done(((bf16[4,8,128]{2,1,0:T(8,128)(2,1)}), bf16[4,8,128]{2,1,0:T(8,128)(2,1)S(1)}, u32[]{:S(2)}, u32[]{:S(2)}) %all-to-all-start.2) | async-done | bytes 8224 | tf_op jit(solution)/shard_map/all_to_all | solution.py:25
  74.5 0.7 reshape.296
  75.2 8.7 %all-to-all-start.3 = ((f32[32,2,128]{2,1,0:T(2,128)}), f32[32,2,128]{2,1,0:T(2,128)S(1)}, u32[]{:S(2)}, u32[]{:S(2)}) async-start(f32[32,2,128]{2,1,0:T(2,128)} %reshape.296), calls=%async_computation.3 | async-start | bytes 65536 | tf_op jit(solution)/shard_map/all_to_all | solution.py:25
  84.0 7.2 %all-to-all-done.3 = f32[32,2,128]{2,1,0:T(2,128)S(1)} async-done(((f32[32,2,128]{2,1,0:T(2,128)}), f32[32,2,128]{2,1,0:T(2,128)S(1)}, u32[]{:S(2)}, u32[]{:S(2)}) %all-to-all-start.3) | async-done | bytes 32800 | tf_op jit(solution)/shard_map/all_to_all | solution.py:25
  91.9 3.5 %all-to-all-start.4 = ((bf16[16,8,128]{2,1,0:T(8,128)(2,1)}), bf16[16,8,128]{2,1,0:T(8,128)(2,1)S(1)}, u32[]{:S(2)}, u32[]{:S(2)}) async-start(bf16[16,8,128]{2,1,0:T(8,128)(2,1)} %broadcast_in_dim.38), calls=%async_computation.4 | async-start | bytes 65536 | tf_op jit(solution)/shard_map/all_to_all | solution.py:25
  96.5 10.3 %all-to-all-done.4 = bf16[16,8,128]{2,1,0:T(8,128)(2,1)S(1)} async-done(((bf16[16,8,128]{2,1,0:T(8,128)(2,1)}), bf16[16,8,128]{2,1,0:T(8,128)(2,1)S(1)}, u32[]{:S(2)}, u32[]{:S(2)}) %all-to-all-start.4) | async-done | bytes 32800 | tf_op jit(solution)/shard_map/all_to_all | solution.py:25
  107.1 1.5 slice_bitcast_fusion
  109.4 2.9 %all-gather.2 = f32[32,896]{1,0:T(8,128)S(1)} all-gather(f32[16,896]{1,0:T(8,128)S(1)} %pad_maximum_fusion.2), channel_id=4, replica_groups=mesh['y'=4,'z'=16,'x'=4,'c'=2] {'c'}, dimensions={0}, use_global_device_ids=true | all-gather | bytes 172032 | tf_op jit(solution)/shard_map/all_gather | solution.py:125
  112.8 1.4 fusion.1
  114.4 26.6 %all_to_all.35 = bf16[16,16,8,128]{3,2,1,0:T(8,128)(2,1)S(1)} all-to-all(bf16[16,16,8,128]{3,2,1,0:T(8,128)(2,1)S(1)} %broadcast_in_dim.41), channel_id=1, replica_groups=mesh['y'=4,'z'=16,'x'=4,'c'=2] {'z'}, dimensions={0} | all-to-all | bytes 1048576 | tf_op jit(solution)/shard_map/all_to_all | solution.py:25
  141.2 11.8 %all_to_all.36 = bf16[16,16,1024]{2,1,0:T(8,128)(2,1)S(1)} all-to-all(bf16[16,16,1024]{2,1,0:T(8,128)(2,1)S(1)} %broadcast_in_dim.43), channel_id=1, replica_groups=mesh['y'=4,'z'=16,'x'=4,'c'=2] {'y','x'}, dimensions={0} | all-to-all | bytes 1048576 | tf_op jit(solution)/shard_map/all_to_all | solution.py:25
  152.9 9.0 %collective-permute-start = (bf16[256,1024]{1,0:T(8,128)(2,1)S(1)}, bf16[256,1024]{1,0:T(8,128)(2,1)S(1)}, u32[]{:S(2)}, u32[]{:S(2)}) collective-permute-start(bf16[256,1024]{1,0:T(8,128)(2,1)S(1)} %bitcast.123), channel_id=1, source_target_pairs={{0,1},{1,0},{2,3},{3,2},{4,5},{5,4},{6,7},{7,6},{8,9},{9,8},{10,11... | collective-permute-start | bytes 1572872 | tf_op jit(solution)/shard_map/ppermute | solution.py:135
  162.4 1.1 collective-permute-done
  164.7 0.7 reshape.308
  (109 shorter events, 9.9 us)
Async XLA Ops:
  6.5 45.8 %copy-start = (bf16[1,2048,2]{1,2,0:T(2,128)(2,1)S(1)}, bf16[1,2048,2]{1,2,0:T(2,128)(2,1)}, u32[]{:S(2)}) copy-start(bf16[1,2048,2]{1,2,0:T(2,128)(2,1)} %param.19) | copy-start | bytes 24580
  6.5 19.6 %copy-start.3 = (bf16[1,96,256]{2,1,0:T(8,128)(2,1)S(1)}, bf16[1,96,256]{2,1,0:T(8,128)(2,1)}, u32[]{:S(2)}) copy-start(bf16[1,96,256]{2,1,0:T(8,128)(2,1)} %param.27) | copy-start | bytes 147460
  6.5 19.6 %copy-start.4 = (bf16[1,256,96]{1,2,0:T(8,128)(2,1)S(1)}, bf16[1,256,96]{1,2,0:T(8,128)(2,1)}, u32[]{:S(2)}) copy-start(bf16[1,256,96]{1,2,0:T(8,128)(2,1)} %param.26) | copy-start | bytes 147460
  6.5 19.6 %copy-start.5 = (bf16[1,256,96]{1,2,0:T(8,128)(2,1)S(1)}, bf16[1,256,96]{1,2,0:T(8,128)(2,1)}, u32[]{:S(2)}) copy-start(bf16[1,256,96]{1,2,0:T(8,128)(2,1)} %param.25) | copy-start | bytes 147460
  6.5 20.3 %copy-start.11 = (s32[256]{0:T(256)S(1)}, s32[256]{0:T(256)}, u32[]{:S(2)}) copy-start(s32[256]{0:T(256)} %param.16) | copy-start | bytes 3076
  6.5 20.5 %copy-start.6 = (bf16[1,32,1,512]{3,1,2,0:T(8,128)(2,1)S(1)}, bf16[1,32,1,512]{3,1,2,0:T(8,128)(2,1)}, u32[]{:S(2)}) copy-start(bf16[1,32,1,512]{3,1,2,0:T(8,128)(2,1)} %param.18) | copy-start | bytes 98308
  7.3 56.7 %copy-start.9 = (f32[1,128]{1,0:T(1,128)S(1)}, f32[1,128]{1,0:T(1,128)}, u32[]{:S(2)}) copy-start(f32[1,128]{1,0:T(1,128)} %param.23) | copy-start | bytes 1540
  9.0 55.4 %copy-start.10 = (f32[1,128]{1,0:T(1,128)S(1)}, f32[1,128]{1,0:T(1,128)}, u32[]{:S(2)}) copy-start(f32[1,128]{1,0:T(1,128)} %param.22) | copy-start | bytes 1540
  9.0 55.8 %copy-start.12 = (bf16[1,2,1024,1,128]{4,2,3,1,0:T(8,128)(2,1)S(1)}, bf16[1,2,1024,1,128]{4,2,3,1,0:T(8,128)(2,1)}, u32[]{:S(2)}) copy-start(bf16[1,2,1024,1,128]{4,2,3,1,0:T(8,128)(2,1)} %param.17) | copy-start | bytes 1572868
  9.4 60.6 %copy-start.2 = (bf16[4,2048]{1,0:T(4,128)(2,1)S(1)}, bf16[4,2048]{1,0:T(4,128)(2,1)}, u32[]{:S(2)}) copy-start(bf16[4,2048]{1,0:T(4,128)(2,1)} %param.15) | copy-start | bytes 49156
  10.3 29.5 %all-to-all-start = ((bf16[16,72,128]{2,1,0:T(8,128)(2,1)}), bf16[16,72,128]{2,1,0:T(8,128)(2,1)S(1)}, u32[]{:S(2)}, u32[]{:S(2)}) async-start(bf16[16,72,128]{2,1,0:T(8,128)(2,1)} %pad_maximum_fusion), calls=%async_computation | async-start | bytes 589824 | tf_op jit(solution)/shard_map/all_to_all | solution.py:25
  26.0 81.1 %all-gather.5.cloned.1.call-start = ((), (), s32[]{:S(2)}) async-start(), calls=%async_computation.7 | async-start | bytes 2506752 | tf_op jit(solution)/shard_map/all_gather | solution.py:59
  37.4 58.4 %copy-start.7 = (f32[1,2048]{1,0:T(1,128)S(1)}, f32[1,2048]{1,0:T(1,128)}, u32[]{:S(2)}) copy-start(f32[1,2048]{1,0:T(1,128)} %param.24) | copy-start | bytes 24580
  40.6 23.3 %all-to-all-start.1 = ((bf16[16,4,512]{2,1,0:T(4,128)(2,1)}), bf16[16,4,512]{2,1,0:T(4,128)(2,1)S(1)}, u32[]{:S(2)}, u32[]{:S(2)}) async-start(bf16[16,4,512]{2,1,0:T(4,128)(2,1)} %reshape.292), calls=%async_computation.1 | async-start | bytes 131072 | tf_op jit(solution)/shard_map/all_to_all | solution.py:25
  65.9 8.3 %all-to-all-start.2 = ((bf16[4,8,128]{2,1,0:T(8,128)(2,1)}), bf16[4,8,128]{2,1,0:T(8,128)(2,1)S(1)}, u32[]{:S(2)}, u32[]{:S(2)}) async-start(bf16[4,8,128]{2,1,0:T(8,128)(2,1)} %broadcast_in_dim.37), calls=%async_computation.2 | async-start | bytes 16384 | tf_op jit(solution)/shard_map/all_to_all | solution.py:25
  75.2 16.0 %all-to-all-start.3 = ((f32[32,2,128]{2,1,0:T(2,128)}), f32[32,2,128]{2,1,0:T(2,128)S(1)}, u32[]{:S(2)}, u32[]{:S(2)}) async-start(f32[32,2,128]{2,1,0:T(2,128)} %reshape.296), calls=%async_computation.3 | async-start | bytes 65536 | tf_op jit(solution)/shard_map/all_to_all | solution.py:25
  91.9 15.0 %all-to-all-start.4 = ((bf16[16,8,128]{2,1,0:T(8,128)(2,1)}), bf16[16,8,128]{2,1,0:T(8,128)(2,1)S(1)}, u32[]{:S(2)}, u32[]{:S(2)}) async-start(bf16[16,8,128]{2,1,0:T(8,128)(2,1)} %broadcast_in_dim.38), calls=%async_computation.4 | async-start | bytes 65536 | tf_op jit(solution)/shard_map/all_to_all | solution.py:25
  114.3 47.7 %copy-start.8 = (f32[2048]{0:T(1024)S(1)}, f32[2048]{0:T(1024)}, u32[]{:S(2)}) copy-start(f32[2048]{0:T(1024)} %param.28) | copy-start | bytes 24580
  114.3 47.7 %copy-start.1 = (bf16[2048,256]{1,0:T(8,128)(2,1)S(1)}, bf16[2048,256]{1,0:T(8,128)(2,1)}, u32[]{:S(2)}) copy-start(bf16[2048,256]{1,0:T(8,128)(2,1)} %param.29) | copy-start | bytes 3145732
  152.9 10.6 %collective-permute-start = (bf16[256,1024]{1,0:T(8,128)(2,1)S(1)}, bf16[256,1024]{1,0:T(8,128)(2,1)S(1)}, u32[]{:S(2)}, u32[]{:S(2)}) collective-permute-start(bf16[256,1024]{1,0:T(8,128)(2,1)S(1)} %bitcast.123), channel_id=1, source_target_pairs={{0,1},{1,0},{2,3},{3,2},{4,5},{5,4},{6,7},{7,6},{8,9},{9,8},{10,11... | collective-permute-start | bytes 1572872 | tf_op jit(solution)/shard_map/ppermute | solution.py:135
Sparse Core Ops, SparseCore 0:
  29.9 62.0 all-gather.4

commit v6 on v5

--- a/solution.py
+++ b/solution.py
@@ -66,6 +66,23 @@
     normed = rms_scale(tokens.astype(F32), in_gain[0]).astype(BF16)
     head_gate = jax.nn.sigmoid(jnp.dot(normed, w_headgate[0], preferred_element_type=F32))
 
+    half = head_dim // 2
+    frequency = ROPE_THETA ** (-2.0 * jnp.arange(half, dtype=F32) / head_dim)
+    angles = positions.astype(F32)[:, None] * frequency[None, :]
+    cosine, sine = jnp.cos(angles), jnp.sin(angles)
+
+    def own_row(array):
+        return lax.dynamic_slice_in_dim(array, ix, 1, 0)
+
+    def own_core(array, axis):
+        return lax.dynamic_slice_in_dim(array, ic, 1, axis)
+
+    residual = own_core(own_row(tokens).reshape(Y, C, seg), 1).reshape(8, head_dim)
+    post_half = own_core(post_gain.reshape(X, C, seg), 1).reshape(X, seg)
+    slot = jnp.arange(kv_cache.shape[2], dtype=jnp.int32)
+    inside = (slot[None, :] >= starts[:, None]) & (slot[None, :] < limits[:, None])
+    inside = inside.astype(F32)
+
     depth = width // (Y * Z)
     sent = normed.reshape(rows, Y, Z, depth).transpose(2, 0, 1, 3).reshape(Z, rows, Y * depth)
     block = w_out[0].T
@@ -74,15 +91,15 @@
         [sent, jnp.zeros((Z, 8 - rows, head_dim), BF16), jnp.broadcast_to(block[None], (Z,) + block.shape)], axis=1
     )
     arrived = swap(sent, "z")
+    arrived, qkv_block, head_gate, cosine, sine, residual, post_half, inside = lax.optimization_barrier(
+        (arrived, qkv_block, head_gate, cosine, sine, residual, post_half, inside)
+    )
     batch = arrived[:, :rows].reshape(Z * rows, Y * depth)
-    out_block = arrived[:, 8:].reshape(Z, 2, -1, head_dim)
+    out_block = arrived[:, 8:].reshape(Z, 2, -1, head_dim).transpose(1, 0, 2, 3).reshape(2, -1, head_dim)
     part = jnp.dot(batch, qkv_block, preferred_element_type=F32).astype(BF16)
-    qkv = jnp.sum(swap(part.reshape(Z, rows, columns), "z").astype(F32), axis=0)
+    part, out_block = lax.optimization_barrier((swap(part.reshape(Z, rows, columns), "z"), out_block))
+    qkv = jnp.sum(part.astype(F32), axis=0)
 
-    half = head_dim // 2
-    frequency = ROPE_THETA ** (-2.0 * jnp.arange(half, dtype=F32) / head_dim)
-    angles = positions.astype(F32)[:, None] * frequency[None, :]
-    cosine, sine = jnp.cos(angles), jnp.sin(angles)
     query = qkv[:, : 2 * head_dim].reshape(rows, 2, head_dim)
     query = rotate(rms_scale(query, q_gain[0]), cosine[:, None], sine[:, None]).astype(BF16)
     key = qkv[:, 2 * head_dim : 3 * head_dim]
@@ -91,11 +108,8 @@
 
     scale = head_dim ** (-0.5)
     keys, values = kv_cache[0, 0, :, 0], kv_cache[0, 1, :, 0]
-    slots = keys.shape[0]
     score = jnp.einsum("rqd,sd->rqs", query, keys, preferred_element_type=F32) * scale
-    slot = jnp.arange(slots, dtype=jnp.int32)
-    inside = (slot[None, :] >= starts[:, None]) & (slot[None, :] < limits[:, None])
-    weight = jnp.where(inside[:, None, :], jnp.exp(score), 0.0)
+    weight = jnp.where(inside[:, None, :] > 0.0, jnp.exp(score), 0.0)
     own = jnp.exp(jnp.sum(query.astype(F32) * key.astype(F32)[:, None], axis=-1) * scale)
     total = jnp.sum(weight, axis=-1) + own
     summed = jnp.einsum("rqs,sd->rqd", weight.astype(BF16), values, preferred_element_type=F32)
@@ -103,15 +117,8 @@
     attended = summed / total[..., None]
     mixed = (attended * head_gate[..., None]).astype(BF16)
 
-    def own_row(array):
-        return lax.dynamic_slice_in_dim(array, ix, 1, 0)
-
-    def own_core(array, axis):
-        return lax.dynamic_slice_in_dim(array, ic, 1, axis)
-
-    residual = own_core(own_row(tokens).reshape(Y, C, seg), 1).reshape(8, head_dim)
     everyone = spread(mixed.transpose(1, 0, 2).reshape(2 * rows, head_dim), "y", Y).reshape(Y, 2, rows, head_dim)
-    part = jnp.einsum("yqrd,zqnd->yrzn", everyone, out_block, preferred_element_type=F32)
+    part = jnp.einsum("yqrd,qnd->yrn", everyone, out_block, preferred_element_type=F32)
     part = swap(part.reshape(Y * rows * C, 2, head_dim), ("y", "x", "c"))
     projected = jnp.sum(part.reshape(Y, X * C, 2, head_dim), axis=1).reshape(8, head_dim)
     stream = (residual.astype(F32) + projected).astype(BF16)
@@ -119,7 +126,7 @@
     batch = spread(stream, "z", Z).reshape(Z, X, seg)
     wide = batch.astype(F32)
     squares = jnp.sum(wide * wide, axis=(1, 2)).reshape(Z, 1)
-    batch = (wide * own_core(post_gain.reshape(X, C, seg), 1).reshape(X, seg)).astype(BF16)
+    batch = (wide * post_half).astype(BF16)
     part = jnp.einsum("bxk,yxfk->byf", batch, ffn[:, :, : 2 * units], preferred_element_type=F32)
     part = jnp.concatenate([part.reshape(Z, -1), jnp.broadcast_to(squares, (Z, head_dim))], axis=1)
     both = jnp.sum(lax.all_gather(part, "c", axis=0), axis=0)
@@ -128,9 +135,10 @@
     hidden = (jax.nn.silu(both[..., :units]) * both[..., units:]).astype(BF16)
     down = ffn[:, :, 2 * units : 3 * units]
     part = jnp.einsum("byf,yxfk->bxk", hidden, down, preferred_element_type=F32).astype(BF16)
-    lowered = jnp.sum(spread(part.reshape(Z, 8, head_dim), "z", Z).astype(F32), axis=0)
-    piece = (wide.reshape(Z, 8, head_dim) + lowered).astype(BF16).reshape(Z, part_width)
+    lowered = jnp.sum(swap(part.reshape(Z, 8, head_dim), "z").astype(F32), axis=0)
+    piece = (stream.astype(F32) + lowered).astype(BF16)
 
+    piece = spread(piece, "z", Z).reshape(Z, part_width)
     near = spread(piece, ("y", "x"), Y * X).reshape(Y * X * Z, part_width)
     far = lax.ppermute(near, "c", [(0, 1), (1, 0)])
     near, far = near.astype(F32), far.astype(F32)

time: 173 us -> 170 us (0.983)
  blocking collectives: 51.7 us -> 92.1 us
  waiting for transfers between devices: 36.4 us -> 14 us
  starting transfers between devices: 52.9 us -> 33.2 us
  local copies, waits for them, and re-layouts: 7.66 us -> 5.69 us
    all_to_all x2 -> x6, blocking collectives: 38.4 us -> 78.5 us  [swap(): return lax.all_to_all(values, axes, split_axis=0, concat_axis=0, tiled=True)]
    all_to_all x5 -> x2, waiting for transfers between devices: 35.3 us -> 12.9 us  [swap(): return lax.all_to_all(values, axes, split_axis=0, concat_axis=0, tiled=True)]
    all_to_all x5 -> x2, starting transfers between devices: 43.8 us -> 27.5 us  [swap(): return lax.all_to_all(values, axes, split_axis=0, concat_axis=0, tiled=True)]
    ppermute x1, starting transfers between devices: 9.05 us -> 5.65 us  [local(): far = lax.ppermute(near, 'c', [(0, 1), (1, 0)])]
  transfers between devices with their start and end apart: 7 -> 4, of which waited for: 6 -> 3; matrix products, arithmetic and copies ran while one was open for 4% -> 5% of each run, Pallas kernels for 0% -> 0%
where the time goes in v6:
time: 170 us
  blocking collectives  92.1 us (54%)
  starting transfers between devices  33.2 us (20%)
  waiting for transfers between devices  14 us (8%)
  between operations  13.8 us (8%)
  other arithmetic  7.11 us (4%)
  local copies, waits for them, and re-layouts  5.69 us (3%)
  matrix products  3.59 us (2%)
    all_to_all x6, blocking collectives, swap(): return lax.all_to_all(values, axes, split_axis=0, concat_axis=0, tiled=True)  78.5 us
    all_to_all x2, starting transfers between devices, swap(): return lax.all_to_all(values, axes, split_axis=0, concat_axis=0, tiled=True)  27.5 us
    all_to_all x2, waiting for transfers between devices, swap(): return lax.all_to_all(values, axes, split_axis=0, concat_axis=0, tiled=True)  12.9 us
    all_gather x1, blocking collectives, local(): qkv_block = lax.all_gather(w_qkv[0, :, 0], 'y', axis=0, tiled=True)  10.4 us
    ppermute x1, starting transfers between devices, local(): far = lax.ppermute(near, 'c', [(0, 1), (1, 0)])  5.65 us
  transfers between devices with their start and end apart: 4, of which 3 were waited for; matrix products, arithmetic and copies ran while one was open for 5% of the time, Pallas kernels for 0%

profile of v6, /device:TPU:1, one launch (start us, length us, event | category | flops | bytes accessed | tf_op | source)
XLA Modules:
  0.0 169.6 jit_solution(18086799229553333827)
XLA Ops:
  6.6 1.5 pad_maximum_fusion.1
  8.2 0.7 fusion.44
  8.9 0.8 fusion.26
  9.7 0.8 fusion.28
  11.0 0.8 pad_maximum_fusion
  11.8 15.7 %all-to-all-start = ((bf16[16,72,128]{2,1,0:T(8,128)(2,1)}), bf16[16,72,128]{2,1,0:T(8,128)(2,1)S(1)}, u32[]{:S(2)}, u32[]{:S(2)}) async-start(bf16[16,72,128]{2,1,0:T(8,128)(2,1)} %pad_maximum_fusion), calls=%async_computation | async-start | bytes 589824 | tf_op jit(solution)/shard_map/all_to_all | solution.py:25
  28.1 0.7 reduce.11
  29.2 10.4 %all-gather = bf16[1,128,1,512]{3,1,2,0:T(8,128)(2,1)S(1)} all-gather(bf16[1,32,1,512]{3,1,2,0:T(8,128)(2,1)S(1)} %copy-done.3), channel_id=2, replica_groups=mesh['y'=4,'z'=16,'x'=4,'c'=2] {'y'}, dimensions={1}, use_global_device_ids=true | all-gather | bytes 163840 | tf_op jit(solution)/shard_map/all_gather | solution.py:60
  40.0 1.4 all-to-all-done
  41.5 0.7 reshape.218
  42.2 11.8 %all-to-all-start.1 = ((bf16[16,4,512]{2,1,0:T(4,128)(2,1)}), bf16[16,4,512]{2,1,0:T(4,128)(2,1)S(1)}, u32[]{:S(2)}, u32[]{:S(2)}) async-start(bf16[16,4,512]{2,1,0:T(4,128)(2,1)} %reshape.218), calls=%async_computation.1 | async-start | bytes 131072 | tf_op jit(solution)/shard_map/all_to_all | solution.py:25
  54.0 11.5 %all-to-all-done.1 = bf16[16,4,512]{2,1,0:T(4,128)(2,1)S(1)} async-done(((bf16[16,4,512]{2,1,0:T(4,128)(2,1)}), bf16[16,4,512]{2,1,0:T(4,128)(2,1)S(1)}, u32[]{:S(2)}, u32[]{:S(2)}) %all-to-all-start.1) | async-done | bytes 65568 | tf_op jit(solution)/shard_map/all_to_all | solution.py:25
  66.9 8.2 %all_to_all.40 = bf16[4,8,128]{2,1,0:T(8,128)(2,1)S(1)} all-to-all(bf16[4,8,128]{2,1,0:T(8,128)(2,1)S(1)} %broadcast_in_dim.35), channel_id=1, replica_groups=mesh['y'=4,'z'=16,'x'=4,'c'=2] {'y'}, dimensions={0} | all-to-all | bytes 16384 | tf_op jit(solution)/shard_map/all_to_all | solution.py:25
  75.3 16.3 %all_to_all.41 = f32[32,2,128]{2,1,0:T(2,128)S(1)} all-to-all(f32[32,2,128]{2,1,0:T(2,128)S(1)} %reshape.223), channel_id=1, replica_groups=mesh['y'=4,'z'=16,'x'=4,'c'=2] {'y','x','c'}, dimensions={0} | all-to-all | bytes 65536 | tf_op jit(solution)/shard_map/all_to_all | solution.py:25
  91.6 14.0 %all_to_all.42 = bf16[16,8,128]{2,1,0:T(8,128)(2,1)S(1)} all-to-all(bf16[16,8,128]{2,1,0:T(8,128)(2,1)S(1)} %broadcast_in_dim.36), channel_id=1, replica_groups=mesh['y'=4,'z'=16,'x'=4,'c'=2] {'z'}, dimensions={0} | all-to-all | bytes 65536 | tf_op jit(solution)/shard_map/all_to_all | solution.py:25
  105.9 1.5 slice_bitcast_fusion
  108.1 3.3 %all-gather.2 = f32[32,896]{1,0:T(8,128)S(1)} all-gather(f32[16,896]{1,0:T(8,128)S(1)} %pad_maximum_fusion.2), channel_id=4, replica_groups=mesh['y'=4,'z'=16,'x'=4,'c'=2] {'c'}, dimensions={0}, use_global_device_ids=true | all-gather | bytes 172032 | tf_op jit(solution)/shard_map/all_gather | solution.py:132
  111.9 1.5 fusion.1
  113.5 14.1 %all_to_all.43 = bf16[16,8,128]{2,1,0:T(8,128)(2,1)S(1)} all-to-all(bf16[16,8,128]{2,1,0:T(8,128)(2,1)S(1)} %reshape.228), channel_id=1, replica_groups=mesh['y'=4,'z'=16,'x'=4,'c'=2] {'z'}, dimensions={0} | all-to-all | bytes 65536 | tf_op jit(solution)/shard_map/all_to_all | solution.py:25
  127.6 14.0 %all_to_all.44 = bf16[16,8,128]{2,1,0:T(8,128)(2,1)S(1)} all-to-all(bf16[16,8,128]{2,1,0:T(8,128)(2,1)S(1)} %broadcast_in_dim.38), channel_id=1, replica_groups=mesh['y'=4,'z'=16,'x'=4,'c'=2] {'z'}, dimensions={0} | all-to-all | bytes 65536 | tf_op jit(solution)/shard_map/all_to_all | solution.py:25
  141.7 11.9 %all_to_all.45 = bf16[16,16,1024]{2,1,0:T(8,128)(2,1)S(1)} all-to-all(bf16[16,16,1024]{2,1,0:T(8,128)(2,1)S(1)} %broadcast_in_dim.40), channel_id=1, replica_groups=mesh['y'=4,'z'=16,'x'=4,'c'=2] {'y','x'}, dimensions={0} | all-to-all | bytes 1048576 | tf_op jit(solution)/shard_map/all_to_all | solution.py:25
  153.6 5.6 %collective-permute-start = (bf16[256,1024]{1,0:T(8,128)(2,1)S(1)}, bf16[256,1024]{1,0:T(8,128)(2,1)S(1)}, u32[]{:S(2)}, u32[]{:S(2)}) collective-permute-start(bf16[256,1024]{1,0:T(8,128)(2,1)S(1)} %bitcast.121), channel_id=1, source_target_pairs={{0,1},{1,0},{2,3},{3,2},{4,5},{5,4},{6,7},{7,6},{8,9},{9,8},{10,11... | collective-permute-start | bytes 1572872 | tf_op jit(solution)/shard_map/ppermute | solution.py:143
  159.7 1.1 collective-permute-done
  162.0 0.7 reshape.235
  (105 shorter events, 6.7 us)
Async XLA Ops:
  6.5 33.2 %copy-start = (bf16[1,2048,2]{1,2,0:T(2,128)(2,1)S(1)}, bf16[1,2048,2]{1,2,0:T(2,128)(2,1)}, u32[]{:S(2)}) copy-start(bf16[1,2048,2]{1,2,0:T(2,128)(2,1)} %param.19) | copy-start | bytes 24580
  6.5 22.6 %copy-start.2 = (bf16[4,2048]{1,0:T(4,128)(2,1)S(1)}, bf16[4,2048]{1,0:T(4,128)(2,1)}, u32[]{:S(2)}) copy-start(bf16[4,2048]{1,0:T(4,128)(2,1)} %param.15) | copy-start | bytes 49156
  6.5 21.6 %copy-start.4 = (f32[1,2048]{1,0:T(1,128)S(1)}, f32[1,2048]{1,0:T(1,128)}, u32[]{:S(2)}) copy-start(f32[1,2048]{1,0:T(1,128)} %param.24) | copy-start | bytes 24580
  6.5 22.3 %copy-start.8 = (s32[256]{0:T(256)S(1)}, s32[256]{0:T(256)}, u32[]{:S(2)}) copy-start(s32[256]{0:T(256)} %param.16) | copy-start | bytes 3076
  6.5 22.7 %copy-start.3 = (bf16[1,32,1,512]{3,1,2,0:T(8,128)(2,1)S(1)}, bf16[1,32,1,512]{3,1,2,0:T(8,128)(2,1)}, u32[]{:S(2)}) copy-start(bf16[1,32,1,512]{3,1,2,0:T(8,128)(2,1)} %param.18) | copy-start | bytes 98308
  6.5 99.3 %all-gather.5.cloned.1.call-start = ((), (), s32[]{:S(2)}) async-start(), calls=%async_computation.8 | async-start | bytes 2506752 | tf_op jit(solution)/shard_map/all_gather | solution.py:59
  11.0 54.7 %copy-start.6 = (f32[1,128]{1,0:T(1,128)S(1)}, f32[1,128]{1,0:T(1,128)}, u32[]{:S(2)}) copy-start(f32[1,128]{1,0:T(1,128)} %param.23) | copy-start | bytes 1540
  11.0 55.1 %copy-start.7 = (f32[1,128]{1,0:T(1,128)S(1)}, f32[1,128]{1,0:T(1,128)}, u32[]{:S(2)}) copy-start(f32[1,128]{1,0:T(1,128)} %param.22) | copy-start | bytes 1540
  11.0 55.4 %copy-start.9 = (bf16[1,2,1024,1,128]{4,2,3,1,0:T(8,128)(2,1)S(1)}, bf16[1,2,1024,1,128]{4,2,3,1,0:T(8,128)(2,1)}, u32[]{:S(2)}) copy-start(bf16[1,2,1024,1,128]{4,2,3,1,0:T(8,128)(2,1)} %param.17) | copy-start | bytes 1572868
  11.8 29.5 %all-to-all-start = ((bf16[16,72,128]{2,1,0:T(8,128)(2,1)}), bf16[16,72,128]{2,1,0:T(8,128)(2,1)S(1)}, u32[]{:S(2)}, u32[]{:S(2)}) async-start(bf16[16,72,128]{2,1,0:T(8,128)(2,1)} %pad_maximum_fusion), calls=%async_computation | async-start | bytes 589824 | tf_op jit(solution)/shard_map/all_to_all | solution.py:25
  42.2 23.4 %all-to-all-start.1 = ((bf16[16,4,512]{2,1,0:T(4,128)(2,1)}), bf16[16,4,512]{2,1,0:T(4,128)(2,1)S(1)}, u32[]{:S(2)}, u32[]{:S(2)}) async-start(bf16[16,4,512]{2,1,0:T(4,128)(2,1)} %reshape.218), calls=%async_computation.1 | async-start | bytes 131072 | tf_op jit(solution)/shard_map/all_to_all | solution.py:25
  111.8 47.4 %copy-start.5 = (f32[2048]{0:T(1024)S(1)}, f32[2048]{0:T(1024)}, u32[]{:S(2)}) copy-start(f32[2048]{0:T(1024)} %param.28) | copy-start | bytes 24580
  111.8 47.5 %copy-start.1 = (bf16[2048,256]{1,0:T(8,128)(2,1)S(1)}, bf16[2048,256]{1,0:T(8,128)(2,1)}, u32[]{:S(2)}) copy-start(bf16[2048,256]{1,0:T(8,128)(2,1)} %param.29) | copy-start | bytes 3145732
  153.6 7.2 %collective-permute-start = (bf16[256,1024]{1,0:T(8,128)(2,1)S(1)}, bf16[256,1024]{1,0:T(8,128)(2,1)S(1)}, u32[]{:S(2)}, u32[]{:S(2)}) collective-permute-start(bf16[256,1024]{1,0:T(8,128)(2,1)S(1)} %bitcast.121), channel_id=1, source_target_pairs={{0,1},{1,0},{2,3},{3,2},{4,5},{5,4},{6,7},{7,6},{8,9},{9,8},{10,11... | collective-permute-start | bytes 1572872 | tf_op jit(solution)/shard_map/ppermute | solution.py:143
Sparse Core Ops, SparseCore 0:
  10.4 65.3 all-gather.4

commit v7 on v6

--- a/solution.py
+++ b/solution.py
@@ -1,6 +1,8 @@
 import jax
 import jax.numpy as jnp
 from jax import lax
+from jax.experimental import pallas as pl
+from jax.experimental.pallas import tpu as pltpu
 from jax.sharding import Mesh
 from jax.sharding import PartitionSpec as P
 
@@ -27,6 +29,62 @@
 
 def spread(values, axes, count):
     return swap(jnp.broadcast_to(values[None], (count,) + values.shape), axes)
+
+
+def first_kernel(tokens, gain, block, gate, up, down, sent, ffn, normed, token_buf, gain_buf, block_buf, sems):
+    rows, width = token_buf.shape
+    units = gate.shape[0]
+    loads = [
+        pltpu.make_async_copy(source, target, sems.at[i])
+        for i, (source, target) in enumerate(((tokens, token_buf), (gain, gain_buf), (block, block_buf)))
+    ]
+    moves = [
+        pltpu.make_async_copy(source, ffn.at[pl.ds(i * units, units)], sems.at[3 + i])
+        for i, source in enumerate((gate, up, down))
+    ]
+    for copy in loads + moves:
+        copy.start()
+    for copy in loads:
+        copy.wait()
+    wide = token_buf[...].astype(F32)
+    scale = lax.rsqrt(jnp.sum(wide * wide, axis=-1, keepdims=True) / width + EPSILON)
+    wide = wide * scale * gain_buf[...]
+    normed[...] = wide.astype(BF16)
+    span, depth = width // Y, width // (Y * Z)
+    empty = jnp.zeros((8 - rows, Y * depth), F32)
+    left, right = block_buf[:, : Y * depth], block_buf[:, Y * depth :]
+    for z in range(Z):
+        mine = [wide[:, y * span + z * depth : y * span + (z + 1) * depth] for y in range(Y)]
+        head = jnp.concatenate([jnp.concatenate(mine, axis=1), empty], axis=0).astype(BF16)
+        sent[z, :8] = head
+        sent[z, 8 : 8 + depth] = left
+        sent[z, 8 + depth :] = right
+    for copy in moves:
+        copy.wait()
+
+
+def first(tokens, gain, block, gate, up, down):
+    rows, width = tokens.shape
+    depth = width // (Y * Z)
+    anywhere = pl.BlockSpec(memory_space=pl.ANY)
+    local = pl.BlockSpec(memory_space=pltpu.VMEM)
+    return pl.pallas_call(
+        first_kernel,
+        out_shape=(
+            jax.ShapeDtypeStruct((Z, 8 + 2 * depth, Y * depth), BF16),
+            jax.ShapeDtypeStruct((3 * gate.shape[0], gate.shape[1]), BF16),
+            jax.ShapeDtypeStruct((rows, width), BF16),
+        ),
+        in_specs=[anywhere] * 6,
+        out_specs=(local, anywhere, local),
+        scratch_shapes=[
+            pltpu.VMEM((rows, width), BF16),
+            pltpu.VMEM((1, width), F32),
+            pltpu.VMEM(block.shape, BF16),
+            pltpu.SemaphoreType.DMA((6,)),
+        ],
+        name="first",
+    )(tokens, gain, block, gate, up, down)
 
 
 def local(
@@ -55,7 +113,7 @@
     req = lax.axis_index(("y", "z"))
     ix, ic = lax.axis_index("x"), lax.axis_index("c")
 
-    ffn = jnp.concatenate([w_gate[0].T, w_up[0].T, w_down[0]], axis=0)
+    sent, ffn, normed = first(tokens, in_gain, w_out[0].T, w_gate[0].T, w_up[0].T, w_down[0])
     ffn = lax.all_gather(ffn, ("y", "x"), axis=0).reshape(Y, X, -1, seg)
     qkv_block = lax.all_gather(w_qkv[0, :, 0], "y", axis=0, tiled=True)
 
@@ -63,7 +121,6 @@
     starts = jnp.cumsum(positions) - positions
     limits = starts + positions
 
-    normed = rms_scale(tokens.astype(F32), in_gain[0]).astype(BF16)
     head_gate = jax.nn.sigmoid(jnp.dot(normed, w_headgate[0], preferred_element_type=F32))
 
     half = head_dim // 2
@@ -78,26 +135,20 @@
         return lax.dynamic_slice_in_dim(array, ic, 1, axis)
 
     residual = own_core(own_row(tokens).reshape(Y, C, seg), 1).reshape(8, head_dim)
-    post_half = own_core(post_gain.reshape(X, C, seg), 1).reshape(X, seg)
     slot = jnp.arange(kv_cache.shape[2], dtype=jnp.int32)
     inside = (slot[None, :] >= starts[:, None]) & (slot[None, :] < limits[:, None])
     inside = inside.astype(F32)
 
     depth = width // (Y * Z)
-    sent = normed.reshape(rows, Y, Z, depth).transpose(2, 0, 1, 3).reshape(Z, rows, Y * depth)
-    block = w_out[0].T
-    block = jnp.concatenate([block[:, :head_dim], block[:, head_dim:]], axis=0)
-    sent = jnp.concatenate(
-        [sent, jnp.zeros((Z, 8 - rows, head_dim), BF16), jnp.broadcast_to(block[None], (Z,) + block.shape)], axis=1
-    )
-    arrived = swap(sent, "z")
-    arrived, qkv_block, head_gate, cosine, sine, residual, post_half, inside = lax.optimization_barrier(
-        (arrived, qkv_block, head_gate, cosine, sine, residual, post_half, inside)
-    )
+    arrived, post_gain = lax.optimization_barrier((swap(sent, "z"), post_gain))
+    post_half = own_core(post_gain.reshape(X, C, seg), 1).reshape(X, seg)
     batch = arrived[:, :rows].reshape(Z * rows, Y * depth)
     out_block = arrived[:, 8:].reshape(Z, 2, -1, head_dim).transpose(1, 0, 2, 3).reshape(2, -1, head_dim)
     part = jnp.dot(batch, qkv_block, preferred_element_type=F32).astype(BF16)
-    part, out_block = lax.optimization_barrier((swap(part.reshape(Z, rows, columns), "z"), out_block))
+    part = swap(part.reshape(Z, rows, columns), "z")
+    part, out_block, head_gate, cosine, sine, residual, post_half, inside = lax.optimization_barrier(
+        (part, out_block, head_gate, cosine, sine, residual, post_half, inside)
+    )
     qkv = jnp.sum(part.astype(F32), axis=0)
 
     query = qkv[:, : 2 * head_dim].reshape(rows, 2, head_dim)
@@ -123,18 +174,20 @@
     projected = jnp.sum(part.reshape(Y, X * C, 2, head_dim), axis=1).reshape(8, head_dim)
     stream = (residual.astype(F32) + projected).astype(BF16)
 
-    batch = spread(stream, "z", Z).reshape(Z, X, seg)
+    gate_up = ffn[:, :, : 2 * units].transpose(0, 2, 1, 3).reshape(Y * 2 * units, part_width)
+    down = ffn[:, :, 2 * units :].transpose(0, 2, 1, 3).reshape(Y * units, part_width)
+    batch, gate_up, down = lax.optimization_barrier((spread(stream, "z", Z), gate_up, down))
+    batch = batch.reshape(Z, X, seg)
     wide = batch.astype(F32)
     squares = jnp.sum(wide * wide, axis=(1, 2)).reshape(Z, 1)
-    batch = (wide * post_half).astype(BF16)
-    part = jnp.einsum("bxk,yxfk->byf", batch, ffn[:, :, : 2 * units], preferred_element_type=F32)
-    part = jnp.concatenate([part.reshape(Z, -1), jnp.broadcast_to(squares, (Z, head_dim))], axis=1)
+    batch = (wide * post_half).astype(BF16).reshape(Z, part_width)
+    part = lax.dot_general(batch, gate_up, (((1,), (1,)), ((), ())), preferred_element_type=F32)
+    part = jnp.concatenate([part, jnp.broadcast_to(squares, (Z, head_dim))], axis=1)
     both = jnp.sum(lax.all_gather(part, "c", axis=0), axis=0)
     scale = lax.rsqrt(both[:, -1:] / width + EPSILON)
     both = (both[:, :-head_dim] * scale).reshape(Z, Y, 2 * units)
     hidden = (jax.nn.silu(both[..., :units]) * both[..., units:]).astype(BF16)
-    down = ffn[:, :, 2 * units : 3 * units]
-    part = jnp.einsum("byf,yxfk->bxk", hidden, down, preferred_element_type=F32).astype(BF16)
+    part = jnp.dot(hidden.reshape(Z, Y * units), down, preferred_element_type=F32).astype(BF16)
     lowered = jnp.sum(swap(part.reshape(Z, 8, head_dim), "z").astype(F32), axis=0)
     piece = (stream.astype(F32) + lowered).astype(BF16)
 

time: 170 us -> 174 us (1.024)
  blocking collectives: 92.1 us -> 80.8 us
  Pallas kernels: 0 us -> 6.35 us
  waiting for transfers between devices: 14 us -> 18.4 us
  local copies, waits for them, and re-layouts: 5.69 us -> 9.93 us
  starting transfers between devices: 33.2 us -> 37.1 us
  other arithmetic: 7.11 us -> 3.73 us
    all_to_all x6 -> x5, blocking collectives: 78.5 us -> 67.4 us  [swap(): return lax.all_to_all(values, axes, split_axis=0, concat_axis=0, tiled=True)]
    pallas_call x0 -> x1, Pallas kernels: none -> 6.35 us  [first(): pl.pallas_call(first_kernel, out_shape=(jax.ShapeDtypeStruct((Z, 8 + 2 *...]
    all_to_all x2 -> x3, waiting for transfers between devices: 12.9 us -> 16.6 us  [swap(): return lax.all_to_all(values, axes, split_axis=0, concat_axis=0, tiled=True)]
    all_to_all x2 -> x3, starting transfers between devices: 27.5 us -> 30.8 us  [swap(): return lax.all_to_all(values, axes, split_axis=0, concat_axis=0, tiled=True)]
    concatenate x4 -> x1, other arithmetic: 2.39 us -> 0.01 us  [local(): jnp.concatenate([part, jnp.broadcast_to(squares, (Z, head_dim))], axis=1)]
    slice x2, local copies, waits for them, and re-layouts: 0.8 us -> 2.71 us  [the longest x1 1.52 us: local(): ffn[:, :, :2 * units].transpose(0, 2, 1, 3)]
    unnamed x23 -> x22, local copies, waits for them, and re-layouts: 0.57 us -> 2.38 us
  transfers between devices with their start and end apart: 4 -> 5, of which waited for: 3 -> 3; matrix products, arithmetic and copies ran while one was open for 5% -> 8% of each run, Pallas kernels for 0% -> 0%
where the time goes in v7:
time: 174 us; the launch traced here: 173 us
  blocking collectives  80.8 us (46%)
  starting transfers between devices  37.1 us (21%)
  waiting for transfers between devices  18.4 us (11%)
  between operations  13.8 us (8%)
  local copies, waits for them, and re-layouts  9.93 us (6%)
  Pallas kernels  6.35 us (4%)
  other arithmetic  3.73 us (2%)
  matrix products  3.04 us (2%)
    all_to_all x5, blocking collectives, swap(): return lax.all_to_all(values, axes, split_axis=0, concat_axis=0, tiled=True)  67.4 us
    all_to_all x3, starting transfers between devices, swap(): return lax.all_to_all(values, axes, split_axis=0, concat_axis=0, tiled=True)  30.8 us
    all_to_all x3, waiting for transfers between devices, swap(): return lax.all_to_all(values, axes, split_axis=0, concat_axis=0, tiled=True)  16.6 us
    all_gather x1, blocking collectives, local(): qkv_block = lax.all_gather(w_qkv[0, :, 0], 'y', axis=0, tiled=True)  10.5 us
    pallas_call x1, Pallas kernels, first(): pl.pallas_call(first_kernel, out_shape=(jax.ShapeDtypeStruct((Z, 8 + 2 *...  6.35 us
    ppermute x1, starting transfers between devices, local(): far = lax.ppermute(near, 'c', [(0, 1), (1, 0)])  6.2 us
  transfers between devices with their start and end apart: 5, of which 3 were waited for; matrix products, arithmetic and copies ran while one was open for 8% of the time, Pallas kernels for 0%

profile of v7, /device:TPU:1, one launch (start us, length us, event | category | flops | bytes accessed | tf_op | source)
XLA Modules:
  0.0 173.1 jit_solution(7753094616709108361)
XLA Ops:
  6.5 6.3 %first.1 = (bf16[16,72,128]{2,1,0:T(8,128)(2,1)}, bf16[288,256]{1,0:T(8,128)(2,1)}, bf16[4,2048]{1,0:T(4,128)(2,1)}) custom-call(bf16[4,2048]{1,0:T(4,128)(2,1)} %tokens.1, f32[1,2048]{1,0:T(1,128)} %gain.1, bf16[32,256]{1,0:T(8,128)(2,1)} %bitcast.146, bf16[96,256]{1,0:T(8,128)(2,1)} %bitcast.140, bf16[96,256]{1,0:T(8,128)(2,1)} %bitcast.141, ...), custom_call_target="tpu_custom_call" | custom-call | tf_op jit(solution)/shard_map/first/pallas_call | solution.py:71
  12.9 15.8 %all-to-all-start = ((bf16[16,72,128]{2,1,0:T(8,128)(2,1)}), bf16[16,72,128]{2,1,0:T(8,128)(2,1)S(1)}, u32[]{:S(2)}, u32[]{:S(2)}) async-start(bf16[16,72,128]{2,1,0:T(8,128)(2,1)} %get-tuple-element.21), calls=%async_computation | async-start | bytes 589824 | tf_op jit(solution)/shard_map/all_to_all | solution.py:27
  28.7 0.7 all-gather.5.cloned.1.call-update
  29.4 0.8 dynamic-slice_bitcast_fusion
  30.4 0.8 dynamic-slice_reduce_fusion
  31.2 10.5 %all-gather = bf16[1,128,1,512]{3,1,2,0:T(8,128)(2,1)S(1)} all-gather(bf16[1,32,1,512]{3,1,2,0:T(8,128)(2,1)} %param.18), channel_id=2, replica_groups=mesh['y'=4,'z'=16,'x'=4,'c'=2] {'y'}, dimensions={1}, use_global_device_ids=true | all-gather | bytes 163840 | tf_op jit(solution)/shard_map/all_gather | solution.py:118
  41.7 0.8 bitcast_subtract_fusion
  42.5 0.8 fusion.10
  44.2 11.6 %all-to-all-start.1 = ((bf16[16,4,512]{2,1,0:T(4,128)(2,1)}), bf16[16,4,512]{2,1,0:T(4,128)(2,1)S(1)}, u32[]{:S(2)}, u32[]{:S(2)}) async-start(bf16[16,4,512]{2,1,0:T(4,128)(2,1)} %reshape.206), calls=%async_computation.1 | async-start | bytes 131072 | tf_op jit(solution)/shard_map/all_to_all | solution.py:27
  57.1 10.3 %all-to-all-done.1 = bf16[16,4,512]{2,1,0:T(4,128)(2,1)S(1)} async-done(((bf16[16,4,512]{2,1,0:T(4,128)(2,1)}), bf16[16,4,512]{2,1,0:T(4,128)(2,1)S(1)}, u32[]{:S(2)}, u32[]{:S(2)}) %all-to-all-start.1) | async-done | bytes 65568 | tf_op jit(solution)/shard_map/all_to_all | solution.py:27
  68.7 7.6 %all_to_all.40 = bf16[4,8,128]{2,1,0:T(8,128)(2,1)S(1)} all-to-all(bf16[4,8,128]{2,1,0:T(8,128)(2,1)S(1)} %broadcast_in_dim.29), channel_id=1, replica_groups=mesh['y'=4,'z'=16,'x'=4,'c'=2] {'y'}, dimensions={0} | all-to-all | bytes 16384 | tf_op jit(solution)/shard_map/all_to_all | solution.py:27
  76.5 18.5 %all_to_all.41 = f32[32,2,128]{2,1,0:T(2,128)S(1)} all-to-all(f32[32,2,128]{2,1,0:T(2,128)S(1)} %reshape.217), channel_id=1, replica_groups=mesh['y'=4,'z'=16,'x'=4,'c'=2] {'y','x','c'}, dimensions={0} | all-to-all | bytes 65536 | tf_op jit(solution)/shard_map/all_to_all | solution.py:27
  95.6 3.5 %all-to-all-start.4 = ((bf16[16,8,128]{2,1,0:T(8,128)(2,1)}), bf16[16,8,128]{2,1,0:T(8,128)(2,1)S(1)}, u32[]{:S(2)}, u32[]{:S(2)}) async-start(bf16[16,8,128]{2,1,0:T(8,128)(2,1)} %broadcast_in_dim.30), calls=%async_computation.4 | async-start | bytes 65536 | tf_op jit(solution)/shard_map/all_to_all | solution.py:27
  99.2 1.2 slice.75
  100.4 1.5 slice.74
  101.9 1.2 copy.40
  104.3 6.3 %all-to-all-done.4 = bf16[16,8,128]{2,1,0:T(8,128)(2,1)S(1)} async-done(((bf16[16,8,128]{2,1,0:T(8,128)(2,1)}), bf16[16,8,128]{2,1,0:T(8,128)(2,1)S(1)}, u32[]{:S(2)}, u32[]{:S(2)}) %all-to-all-start.4) | async-done | bytes 32800 | tf_op jit(solution)/shard_map/all_to_all | solution.py:27
  111.4 2.9 %all-gather.2 = f32[32,896]{1,0:T(8,128)S(1)} all-gather(f32[16,896]{1,0:T(8,128)S(1)} %pad_maximum_fusion), channel_id=4, replica_groups=mesh['y'=4,'z'=16,'x'=4,'c'=2] {'c'}, dimensions={0}, use_global_device_ids=true | all-gather | bytes 172032 | tf_op jit(solution)/shard_map/all_gather | solution.py:186
  115.1 15.6 %all_to_all.42 = bf16[16,8,128]{2,1,0:T(8,128)(2,1)S(1)} all-to-all(bf16[16,8,128]{2,1,0:T(8,128)(2,1)S(1)} %bitcast.137), channel_id=1, replica_groups=mesh['y'=4,'z'=16,'x'=4,'c'=2] {'z'}, dimensions={0} | all-to-all | bytes 65536 | tf_op jit(solution)/shard_map/all_to_all | solution.py:27
  130.8 14.0 %all_to_all.43 = bf16[16,8,128]{2,1,0:T(8,128)(2,1)S(1)} all-to-all(bf16[16,8,128]{2,1,0:T(8,128)(2,1)S(1)} %broadcast_in_dim.32), channel_id=1, replica_groups=mesh['y'=4,'z'=16,'x'=4,'c'=2] {'z'}, dimensions={0} | all-to-all | bytes 65536 | tf_op jit(solution)/shard_map/all_to_all | solution.py:27
  144.8 11.8 %all_to_all.44 = bf16[16,16,1024]{2,1,0:T(8,128)(2,1)S(1)} all-to-all(bf16[16,16,1024]{2,1,0:T(8,128)(2,1)S(1)} %broadcast_in_dim.34), channel_id=1, replica_groups=mesh['y'=4,'z'=16,'x'=4,'c'=2] {'y','x'}, dimensions={0} | all-to-all | bytes 1048576 | tf_op jit(solution)/shard_map/all_to_all | solution.py:27
  156.6 6.2 %collective-permute-start = (bf16[256,1024]{1,0:T(8,128)(2,1)S(1)}, bf16[256,1024]{1,0:T(8,128)(2,1)S(1)}, u32[]{:S(2)}, u32[]{:S(2)}) collective-permute-start(bf16[256,1024]{1,0:T(8,128)(2,1)S(1)} %bitcast.122), channel_id=1, source_target_pairs={{0,1},{1,0},{2,3},{3,2},{4,5},{5,4},{6,7},{7,6},{8,9},{9,8},{10,11... | collective-permute-start | bytes 1572872 | tf_op jit(solution)/shard_map/ppermute | solution.py:196
  163.2 1.1 collective-permute-done
  165.6 0.7 reshape.232
  (91 shorter events, 9.0 us)
Async XLA Ops:
  6.5 35.9 %copy-start = (bf16[1,2048,2]{1,2,0:T(2,128)(2,1)S(1)}, bf16[1,2048,2]{1,2,0:T(2,128)(2,1)}, u32[]{:S(2)}) copy-start(bf16[1,2048,2]{1,2,0:T(2,128)(2,1)} %param.19) | copy-start | bytes 24580
  6.5 49.9 %copy-start.2 = (f32[1,2048]{1,0:T(1,128)S(1)}, f32[1,2048]{1,0:T(1,128)}, u32[]{:S(2)}) copy-start(f32[1,2048]{1,0:T(1,128)} %param.24) | copy-start | bytes 24580
  6.5 61.0 %copy-start.4 = (f32[1,128]{1,0:T(1,128)S(1)}, f32[1,128]{1,0:T(1,128)}, u32[]{:S(2)}) copy-start(f32[1,128]{1,0:T(1,128)} %param.23) | copy-start | bytes 1540
  6.5 61.3 %copy-start.5 = (f32[1,128]{1,0:T(1,128)S(1)}, f32[1,128]{1,0:T(1,128)}, u32[]{:S(2)}) copy-start(f32[1,128]{1,0:T(1,128)} %param.22) | copy-start | bytes 1540
  6.5 61.6 %copy-start.6 = (bf16[1,2,1024,1,128]{4,2,3,1,0:T(8,128)(2,1)S(1)}, bf16[1,2,1024,1,128]{4,2,3,1,0:T(8,128)(2,1)}, u32[]{:S(2)}) copy-start(bf16[1,2,1024,1,128]{4,2,3,1,0:T(8,128)(2,1)} %param.17) | copy-start | bytes 1572868
  12.9 30.5 %all-to-all-start = ((bf16[16,72,128]{2,1,0:T(8,128)(2,1)}), bf16[16,72,128]{2,1,0:T(8,128)(2,1)S(1)}, u32[]{:S(2)}, u32[]{:S(2)}) async-start(bf16[16,72,128]{2,1,0:T(8,128)(2,1)} %get-tuple-element.21), calls=%async_computation | async-start | bytes 589824 | tf_op jit(solution)/shard_map/all_to_all | solution.py:27
  28.7 70.5 %all-gather.5.cloned.1.call-start = ((), (), s32[]{:S(2)}) async-start(), calls=%async_computation.8 | async-start | bytes 2506752 | tf_op jit(solution)/shard_map/all_gather | solution.py:117
  44.2 23.1 %all-to-all-start.1 = ((bf16[16,4,512]{2,1,0:T(4,128)(2,1)}), bf16[16,4,512]{2,1,0:T(4,128)(2,1)S(1)}, u32[]{:S(2)}, u32[]{:S(2)}) async-start(bf16[16,4,512]{2,1,0:T(4,128)(2,1)} %reshape.206), calls=%async_computation.1 | async-start | bytes 131072 | tf_op jit(solution)/shard_map/all_to_all | solution.py:27
  95.6 15.0 %all-to-all-start.4 = ((bf16[16,8,128]{2,1,0:T(8,128)(2,1)}), bf16[16,8,128]{2,1,0:T(8,128)(2,1)S(1)}, u32[]{:S(2)}, u32[]{:S(2)}) async-start(bf16[16,8,128]{2,1,0:T(8,128)(2,1)} %broadcast_in_dim.30), calls=%async_computation.4 | async-start | bytes 65536 | tf_op jit(solution)/shard_map/all_to_all | solution.py:27
  114.3 48.5 %copy-start.3 = (f32[2048]{0:T(1024)S(1)}, f32[2048]{0:T(1024)}, u32[]{:S(2)}) copy-start(f32[2048]{0:T(1024)} %param.28) | copy-start | bytes 24580
  114.5 48.3 %copy-start.1 = (bf16[2048,256]{1,0:T(8,128)(2,1)S(1)}, bf16[2048,256]{1,0:T(8,128)(2,1)}, u32[]{:S(2)}) copy-start(bf16[2048,256]{1,0:T(8,128)(2,1)} %param.29) | copy-start | bytes 3145732
  156.6 7.7 %collective-permute-start = (bf16[256,1024]{1,0:T(8,128)(2,1)S(1)}, bf16[256,1024]{1,0:T(8,128)(2,1)S(1)}, u32[]{:S(2)}, u32[]{:S(2)}) collective-permute-start(bf16[256,1024]{1,0:T(8,128)(2,1)S(1)} %bitcast.122), channel_id=1, source_target_pairs={{0,1},{1,0},{2,3},{3,2},{4,5},{5,4},{6,7},{7,6},{8,9},{9,8},{10,11... | collective-permute-start | bytes 1572872 | tf_op jit(solution)/shard_map/ppermute | solution.py:196
Sparse Core Ops, SparseCore 0:
  32.5 61.9 all-gather.4

commit v8 on v6

--- a/solution.py
+++ b/solution.py
@@ -7,6 +7,8 @@
 EPSILON = 1e-06
 ROPE_THETA = 1000000.0
 Y, Z, X, C = 4, 16, 4, 2
+ZH, ZL = 4, 4
+DEPTH = ("zh", "zl")
 F32, BF16 = jnp.float32, jnp.bfloat16
 
 
@@ -52,7 +54,7 @@
     units = w_gate.shape[2]
     seg = width // (X * C)
     part_width = width // C
-    req = lax.axis_index(("y", "z"))
+    req = lax.axis_index(("y",) + DEPTH)
     ix, ic = lax.axis_index("x"), lax.axis_index("c")
 
     ffn = jnp.concatenate([w_gate[0].T, w_up[0].T, w_down[0]], axis=0)
@@ -63,7 +65,10 @@
     starts = jnp.cumsum(positions) - positions
     limits = starts + positions
 
-    normed = rms_scale(tokens.astype(F32), in_gain[0]).astype(BF16)
+    token_wide = tokens.astype(F32)
+    gained = (token_wide * in_gain[0]).astype(BF16)
+    in_scale = lax.rsqrt(jnp.mean(token_wide * token_wide, axis=-1, keepdims=True) + EPSILON)
+    normed = (token_wide * in_scale * in_gain[0]).astype(BF16)
     head_gate = jax.nn.sigmoid(jnp.dot(normed, w_headgate[0], preferred_element_type=F32))
 
     half = head_dim // 2
@@ -78,27 +83,28 @@
         return lax.dynamic_slice_in_dim(array, ic, 1, axis)
 
     residual = own_core(own_row(tokens).reshape(Y, C, seg), 1).reshape(8, head_dim)
-    post_half = own_core(post_gain.reshape(X, C, seg), 1).reshape(X, seg)
     slot = jnp.arange(kv_cache.shape[2], dtype=jnp.int32)
     inside = (slot[None, :] >= starts[:, None]) & (slot[None, :] < limits[:, None])
     inside = inside.astype(F32)
 
     depth = width // (Y * Z)
-    sent = normed.reshape(rows, Y, Z, depth).transpose(2, 0, 1, 3).reshape(Z, rows, Y * depth)
+    sent = gained.reshape(rows, Y, Z, depth).transpose(2, 0, 1, 3).reshape(Z, rows, Y * depth)
     block = w_out[0].T
     block = jnp.concatenate([block[:, :head_dim], block[:, head_dim:]], axis=0)
     sent = jnp.concatenate(
         [sent, jnp.zeros((Z, 8 - rows, head_dim), BF16), jnp.broadcast_to(block[None], (Z,) + block.shape)], axis=1
     )
-    arrived = swap(sent, "z")
-    arrived, qkv_block, head_gate, cosine, sine, residual, post_half, inside = lax.optimization_barrier(
-        (arrived, qkv_block, head_gate, cosine, sine, residual, post_half, inside)
-    )
+    arrived = swap(sent, DEPTH)
+    arrived, qkv_block, post_gain = lax.optimization_barrier((arrived, qkv_block, post_gain))
+    post_half = own_core(post_gain.reshape(X, C, seg), 1).reshape(X, seg)
     batch = arrived[:, :rows].reshape(Z * rows, Y * depth)
     out_block = arrived[:, 8:].reshape(Z, 2, -1, head_dim).transpose(1, 0, 2, 3).reshape(2, -1, head_dim)
     part = jnp.dot(batch, qkv_block, preferred_element_type=F32).astype(BF16)
-    part, out_block = lax.optimization_barrier((swap(part.reshape(Z, rows, columns), "z"), out_block))
-    qkv = jnp.sum(part.astype(F32), axis=0)
+    part = swap(part.reshape(Z, rows, columns), DEPTH)
+    part, out_block, in_scale, head_gate, cosine, sine, residual, post_half, inside = lax.optimization_barrier(
+        (part, out_block, in_scale, head_gate, cosine, sine, residual, post_half, inside)
+    )
+    qkv = jnp.sum(part.astype(F32), axis=0) * in_scale
 
     query = qkv[:, : 2 * head_dim].reshape(rows, 2, head_dim)
     query = rotate(rms_scale(query, q_gain[0]), cosine[:, None], sine[:, None]).astype(BF16)
@@ -123,7 +129,7 @@
     projected = jnp.sum(part.reshape(Y, X * C, 2, head_dim), axis=1).reshape(8, head_dim)
     stream = (residual.astype(F32) + projected).astype(BF16)
 
-    batch = spread(stream, "z", Z).reshape(Z, X, seg)
+    batch = spread(stream, DEPTH, Z).reshape(Z, X, seg)
     wide = batch.astype(F32)
     squares = jnp.sum(wide * wide, axis=(1, 2)).reshape(Z, 1)
     batch = (wide * post_half).astype(BF16)
@@ -135,10 +141,10 @@
     hidden = (jax.nn.silu(both[..., :units]) * both[..., units:]).astype(BF16)
     down = ffn[:, :, 2 * units : 3 * units]
     part = jnp.einsum("byf,yxfk->bxk", hidden, down, preferred_element_type=F32).astype(BF16)
-    lowered = jnp.sum(swap(part.reshape(Z, 8, head_dim), "z").astype(F32), axis=0)
-    piece = (stream.astype(F32) + lowered).astype(BF16)
+    part = jnp.sum(spread(part.reshape(Z, 8, head_dim), "zh", ZH).astype(F32), axis=0).astype(BF16)
+    lowered = jnp.sum(spread(part, "zl", ZL).astype(F32), axis=0)
+    piece = (wide.reshape(Z, 8, head_dim) + lowered).astype(BF16).reshape(Z, part_width)
 
-    piece = spread(piece, "z", Z).reshape(Z, part_width)
     near = spread(piece, ("y", "x"), Y * X).reshape(Y * X * Z, part_width)
     far = lax.ppermute(near, "c", [(0, 1), (1, 0)])
     near, far = near.astype(F32), far.astype(F32)
@@ -156,8 +162,8 @@
 
 
 def solution(mesh):
-    fine = Mesh(mesh.devices.reshape(Y, Z, X, C), ("y", "z", "x", "c"))
-    req, head = ("y", "z"), ("x", "c")
+    fine = Mesh(mesh.devices.reshape(Y, ZH, ZL, X, C), ("y", "zh", "zl", "x", "c"))
+    req, head = ("y",) + DEPTH, ("x", "c")
     in_specs = (
         P(req, None),
         P(),

time: 170 us -> 167 us (0.982)
  blocking collectives: 92.1 us -> 88.2 us
    all_to_all x6, blocking collectives: 78.5 us -> 74.9 us  [swap(): return lax.all_to_all(values, axes, split_axis=0, concat_axis=0, tiled=True)]
where the time goes in v8:
time: 167 us; the launch traced here: 166 us
  blocking collectives  88.2 us (53%)
  starting transfers between devices  34.2 us (20%)
  waiting for transfers between devices  14.3 us (9%)
  between operations  13.9 us (8%)
  other arithmetic  6.32 us (4%)
  local copies, waits for them, and re-layouts  5.71 us (3%)
  matrix products  3.58 us (2%)
    all_to_all x6, blocking collectives, swap(): return lax.all_to_all(values, axes, split_axis=0, concat_axis=0, tiled=True)  74.9 us
    all_to_all x2, starting transfers between devices, swap(): return lax.all_to_all(values, axes, split_axis=0, concat_axis=0, tiled=True)  27.4 us
    all_to_all x2, waiting for transfers between devices, swap(): return lax.all_to_all(values, axes, split_axis=0, concat_axis=0, tiled=True)  13.2 us
    all_gather x1, blocking collectives, local(): qkv_block = lax.all_gather(w_qkv[0, :, 0], 'y', axis=0, tiled=True)  10 us
    ppermute x1, starting transfers between devices, local(): far = lax.ppermute(near, 'c', [(0, 1), (1, 0)])  6.69 us
  transfers between devices with their start and end apart: 4, of which 3 were waited for; matrix products, arithmetic and copies ran while one was open for 5% of the time, Pallas kernels for 0%

profile of v8, /device:TPU:1, one launch (start us, length us, event | category | flops | bytes accessed | tf_op | source)
XLA Modules:
  0.0 166.2 jit_solution(17356336349606417543)
XLA Ops:
  6.6 1.5 pad_maximum_fusion.1
  8.2 0.7 fusion.49
  8.9 0.8 fusion.27
  10.2 0.8 pad_maximum_fusion
  11.0 15.7 %all-to-all-start = ((bf16[16,72,128]{2,1,0:T(8,128)(2,1)}), bf16[16,72,128]{2,1,0:T(8,128)(2,1)S(1)}, u32[]{:S(2)}, u32[]{:S(2)}) async-start(bf16[16,72,128]{2,1,0:T(8,128)(2,1)} %pad_maximum_fusion), calls=%async_computation | async-start | bytes 589824 | tf_op jit(solution)/shard_map/all_to_all | solution.py:27
  27.1 10.0 %all-gather = bf16[1,128,1,512]{3,1,2,0:T(8,128)(2,1)S(1)} all-gather(bf16[1,32,1,512]{3,1,2,0:T(8,128)(2,1)S(1)} %copy-done.3), channel_id=2, replica_groups=mesh['y'=4,'zh'=4,'zl'=4,'x'=4,'c'=2] {'y'}, dimensions={1}, use_global_device_ids=true | all-gather | bytes 163840 | tf_op jit(solution)/shard_map/all_gather | solution.py:62
  37.5 3.0 %all-to-all-done = bf16[16,72,128]{2,1,0:T(8,128)(2,1)S(1)} async-done(((bf16[16,72,128]{2,1,0:T(8,128)(2,1)}), bf16[16,72,128]{2,1,0:T(8,128)(2,1)S(1)}, u32[]{:S(2)}, u32[]{:S(2)}) %all-to-all-start) | async-done | bytes 294944 | tf_op jit(solution)/shard_map/all_to_all | solution.py:27
  40.7 0.7 reshape.224
  41.4 11.7 %all-to-all-start.1 = ((bf16[16,4,512]{2,1,0:T(4,128)(2,1)}), bf16[16,4,512]{2,1,0:T(4,128)(2,1)S(1)}, u32[]{:S(2)}, u32[]{:S(2)}) async-start(bf16[16,4,512]{2,1,0:T(4,128)(2,1)} %reshape.224), calls=%async_computation.1 | async-start | bytes 131072 | tf_op jit(solution)/shard_map/all_to_all | solution.py:27
  53.3 0.5 broadcast.164
  53.8 0.6 reduce.12
  54.5 10.2 %all-to-all-done.1 = bf16[16,4,512]{2,1,0:T(4,128)(2,1)S(1)} async-done(((bf16[16,4,512]{2,1,0:T(4,128)(2,1)}), bf16[16,4,512]{2,1,0:T(4,128)(2,1)S(1)}, u32[]{:S(2)}, u32[]{:S(2)}) %all-to-all-start.1) | async-done | bytes 65568 | tf_op jit(solution)/shard_map/all_to_all | solution.py:27
  66.1 8.2 %all_to_all.40 = bf16[4,8,128]{2,1,0:T(8,128)(2,1)S(1)} all-to-all(bf16[4,8,128]{2,1,0:T(8,128)(2,1)S(1)} %broadcast_in_dim.39), channel_id=1, replica_groups=mesh['y'=4,'zh'=4,'zl'=4,'x'=4,'c'=2] {'y'}, dimensions={0} | all-to-all | bytes 16384 | tf_op jit(solution)/shard_map/all_to_all | solution.py:27
  74.5 15.7 %all_to_all.41 = f32[32,2,128]{2,1,0:T(2,128)S(1)} all-to-all(f32[32,2,128]{2,1,0:T(2,128)S(1)} %reshape.235), channel_id=1, replica_groups=mesh['y'=4,'zh'=4,'zl'=4,'x'=4,'c'=2] {'y','x','c'}, dimensions={0} | all-to-all | bytes 65536 | tf_op jit(solution)/shard_map/all_to_all | solution.py:27
  90.3 14.1 %all_to_all.42 = bf16[16,8,128]{2,1,0:T(8,128)(2,1)S(1)} all-to-all(bf16[16,8,128]{2,1,0:T(8,128)(2,1)S(1)} %broadcast_in_dim.40), channel_id=1, replica_groups=mesh['y'=4,'zh'=4,'zl'=4,'x'=4,'c'=2] {'zh','zl'}, dimensions={0} | all-to-all | bytes 65536 | tf_op jit(solution)/shard_map/all_to_all | solution.py:27
  104.6 1.5 slice_bitcast_fusion
  106.9 3.3 %all-gather.2 = f32[32,896]{1,0:T(8,128)S(1)} all-gather(f32[16,896]{1,0:T(8,128)S(1)} %pad_maximum_fusion.2), channel_id=4, replica_groups=mesh['y'=4,'zh'=4,'zl'=4,'x'=4,'c'=2] {'c'}, dimensions={0}, use_global_device_ids=true | all-gather | bytes 172032 | tf_op jit(solution)/shard_map/all_gather | solution.py:138
  110.7 1.4 fusion.1
  112.2 14.9 %all_to_all.43 = bf16[4,16,8,128]{3,2,1,0:T(8,128)(2,1)S(1)} all-to-all(bf16[4,16,8,128]{3,2,1,0:T(8,128)(2,1)S(1)} %broadcast_in_dim.43), channel_id=1, replica_groups=mesh['y'=4,'zh'=4,'zl'=4,'x'=4,'c'=2] {'zh'}, dimensions={0} | all-to-all | bytes 262144 | tf_op jit(solution)/shard_map/all_to_all | solution.py:27
  127.1 9.9 %all_to_all.44 = bf16[4,16,8,128]{3,2,1,0:T(8,128)(2,1)S(1)} all-to-all(bf16[4,16,8,128]{3,2,1,0:T(8,128)(2,1)S(1)} %broadcast_in_dim.44), channel_id=1, replica_groups=mesh['y'=4,'zh'=4,'zl'=4,'x'=4,'c'=2] {'zl'}, dimensions={0} | all-to-all | bytes 262144 | tf_op jit(solution)/shard_map/all_to_all | solution.py:27
  137.2 12.0 %all_to_all.45 = bf16[16,16,1024]{2,1,0:T(8,128)(2,1)S(1)} all-to-all(bf16[16,16,1024]{2,1,0:T(8,128)(2,1)S(1)} %broadcast_in_dim.46), channel_id=1, replica_groups=mesh['y'=4,'zh'=4,'zl'=4,'x'=4,'c'=2] {'y','x'}, dimensions={0} | all-to-all | bytes 1048576 | tf_op jit(solution)/shard_map/all_to_all | solution.py:27
  149.2 6.7 %collective-permute-start = (bf16[256,1024]{1,0:T(8,128)(2,1)S(1)}, bf16[256,1024]{1,0:T(8,128)(2,1)S(1)}, u32[]{:S(2)}, u32[]{:S(2)}) collective-permute-start(bf16[256,1024]{1,0:T(8,128)(2,1)S(1)} %bitcast.123), channel_id=1, source_target_pairs={{0,1},{1,0},{2,3},{3,2},{4,5},{5,4},{6,7},{7,6},{8,9},{9,8},{10,11... | collective-permute-start | bytes 1572872 | tf_op jit(solution)/shard_map/ppermute | solution.py:149
  156.3 1.1 collective-permute-done
  158.6 0.7 reshape.246
  (109 shorter events, 6.4 us)
Async XLA Ops:
  6.5 30.8 %copy-start = (bf16[1,2048,2]{1,2,0:T(2,128)(2,1)S(1)}, bf16[1,2048,2]{1,2,0:T(2,128)(2,1)}, u32[]{:S(2)}) copy-start(bf16[1,2048,2]{1,2,0:T(2,128)(2,1)} %param.19) | copy-start | bytes 24580
  6.5 30.8 %copy-start.2 = (bf16[4,2048]{1,0:T(4,128)(2,1)S(1)}, bf16[4,2048]{1,0:T(4,128)(2,1)}, u32[]{:S(2)}) copy-start(bf16[4,2048]{1,0:T(4,128)(2,1)} %param.15) | copy-start | bytes 49156
  6.5 30.8 %copy-start.6 = (f32[1,2048]{1,0:T(1,128)S(1)}, f32[1,2048]{1,0:T(1,128)}, u32[]{:S(2)}) copy-start(f32[1,2048]{1,0:T(1,128)} %param.21) | copy-start | bytes 24580
  6.5 20.3 %copy-start.9 = (s32[256]{0:T(256)S(1)}, s32[256]{0:T(256)}, u32[]{:S(2)}) copy-start(s32[256]{0:T(256)} %param.16) | copy-start | bytes 3076
  6.5 20.5 %copy-start.3 = (bf16[1,32,1,512]{3,1,2,0:T(8,128)(2,1)S(1)}, bf16[1,32,1,512]{3,1,2,0:T(8,128)(2,1)}, u32[]{:S(2)}) copy-start(bf16[1,32,1,512]{3,1,2,0:T(8,128)(2,1)} %param.18) | copy-start | bytes 98308
  6.5 98.1 %all-gather.5.cloned.1.call-start = ((), (), s32[]{:S(2)}) async-start(), calls=%async_computation.8 | async-start | bytes 2506752 | tf_op jit(solution)/shard_map/all_gather | solution.py:61
  10.1 43.7 %copy-start.4 = (f32[1,2048]{1,0:T(1,128)S(1)}, f32[1,2048]{1,0:T(1,128)}, u32[]{:S(2)}) copy-start(f32[1,2048]{1,0:T(1,128)} %param.24) | copy-start | bytes 24580
  10.2 54.7 %copy-start.7 = (f32[1,128]{1,0:T(1,128)S(1)}, f32[1,128]{1,0:T(1,128)}, u32[]{:S(2)}) copy-start(f32[1,128]{1,0:T(1,128)} %param.23) | copy-start | bytes 1540
  10.2 55.0 %copy-start.8 = (f32[1,128]{1,0:T(1,128)S(1)}, f32[1,128]{1,0:T(1,128)}, u32[]{:S(2)}) copy-start(f32[1,128]{1,0:T(1,128)} %param.22) | copy-start | bytes 1540
  10.2 55.4 %copy-start.10 = (bf16[1,2,1024,1,128]{4,2,3,1,0:T(8,128)(2,1)S(1)}, bf16[1,2,1024,1,128]{4,2,3,1,0:T(8,128)(2,1)}, u32[]{:S(2)}) copy-start(bf16[1,2,1024,1,128]{4,2,3,1,0:T(8,128)(2,1)} %param.17) | copy-start | bytes 1572868
  11.0 29.5 %all-to-all-start = ((bf16[16,72,128]{2,1,0:T(8,128)(2,1)}), bf16[16,72,128]{2,1,0:T(8,128)(2,1)S(1)}, u32[]{:S(2)}, u32[]{:S(2)}) async-start(bf16[16,72,128]{2,1,0:T(8,128)(2,1)} %pad_maximum_fusion), calls=%async_computation | async-start | bytes 589824 | tf_op jit(solution)/shard_map/all_to_all | solution.py:27
  41.4 23.3 %all-to-all-start.1 = ((bf16[16,4,512]{2,1,0:T(4,128)(2,1)}), bf16[16,4,512]{2,1,0:T(4,128)(2,1)S(1)}, u32[]{:S(2)}, u32[]{:S(2)}) async-start(bf16[16,4,512]{2,1,0:T(4,128)(2,1)} %reshape.224), calls=%async_computation.1 | async-start | bytes 131072 | tf_op jit(solution)/shard_map/all_to_all | solution.py:27
  112.1 43.8 %copy-start.5 = (f32[2048]{0:T(1024)S(1)}, f32[2048]{0:T(1024)}, u32[]{:S(2)}) copy-start(f32[2048]{0:T(1024)} %param.28) | copy-start | bytes 24580
  112.1 43.8 %copy-start.1 = (bf16[2048,256]{1,0:T(8,128)(2,1)S(1)}, bf16[2048,256]{1,0:T(8,128)(2,1)}, u32[]{:S(2)}) copy-start(bf16[2048,256]{1,0:T(8,128)(2,1)} %param.29) | copy-start | bytes 3145732
  149.2 8.2 %collective-permute-start = (bf16[256,1024]{1,0:T(8,128)(2,1)S(1)}, bf16[256,1024]{1,0:T(8,128)(2,1)S(1)}, u32[]{:S(2)}, u32[]{:S(2)}) collective-permute-start(bf16[256,1024]{1,0:T(8,128)(2,1)S(1)} %bitcast.123), channel_id=1, source_target_pairs={{0,1},{1,0},{2,3},{3,2},{4,5},{5,4},{6,7},{7,6},{8,9},{9,8},{10,11... | collective-permute-start | bytes 1572872 | tf_op jit(solution)/shard_map/ppermute | solution.py:149
Sparse Core Ops, SparseCore 0:
  10.4 65.4 all-gather.4

commit v9 on v8

--- a/solution.py
+++ b/solution.py
@@ -129,17 +129,19 @@
     projected = jnp.sum(part.reshape(Y, X * C, 2, head_dim), axis=1).reshape(8, head_dim)
     stream = (residual.astype(F32) + projected).astype(BF16)
 
-    batch = spread(stream, DEPTH, Z).reshape(Z, X, seg)
+    gate_up = ffn[:, :, : 2 * units].transpose(1, 0, 2, 3)
+    down = ffn[:, :, 2 * units :]
+    batch, gate_up, down = lax.optimization_barrier((spread(stream, DEPTH, Z), gate_up, down))
+    batch = batch.reshape(Z, X, seg)
     wide = batch.astype(F32)
     squares = jnp.sum(wide * wide, axis=(1, 2)).reshape(Z, 1)
     batch = (wide * post_half).astype(BF16)
-    part = jnp.einsum("bxk,yxfk->byf", batch, ffn[:, :, : 2 * units], preferred_element_type=F32)
+    part = jnp.einsum("bxk,xyfk->byf", batch, gate_up, preferred_element_type=F32)
     part = jnp.concatenate([part.reshape(Z, -1), jnp.broadcast_to(squares, (Z, head_dim))], axis=1)
     both = jnp.sum(lax.all_gather(part, "c", axis=0), axis=0)
     scale = lax.rsqrt(both[:, -1:] / width + EPSILON)
     both = (both[:, :-head_dim] * scale).reshape(Z, Y, 2 * units)
     hidden = (jax.nn.silu(both[..., :units]) * both[..., units:]).astype(BF16)
-    down = ffn[:, :, 2 * units : 3 * units]
     part = jnp.einsum("byf,yxfk->bxk", hidden, down, preferred_element_type=F32).astype(BF16)
     part = jnp.sum(spread(part.reshape(Z, 8, head_dim), "zh", ZH).astype(F32), axis=0).astype(BF16)
     lowered = jnp.sum(spread(part, "zl", ZL).astype(F32), axis=0)

time: 167 us -> 164 us (0.982)
  blocking collectives: 88.2 us -> 74 us
  waiting for transfers between devices: 14.3 us -> 21.8 us
  starting transfers between devices: 34.2 us -> 38 us
  local copies, waits for them, and re-layouts: 5.71 us -> 7.63 us
    all_to_all x6 -> x5, blocking collectives: 74.9 us -> 60.6 us  [swap(): return lax.all_to_all(values, axes, split_axis=0, concat_axis=0, tiled=True)]
    all_to_all x2 -> x3, waiting for transfers between devices: 13.2 us -> 20.7 us  [swap(): return lax.all_to_all(values, axes, split_axis=0, concat_axis=0, tiled=True)]
    all_to_all x2 -> x3, starting transfers between devices: 27.4 us -> 31.1 us  [swap(): return lax.all_to_all(values, axes, split_axis=0, concat_axis=0, tiled=True)]
  transfers between devices with their start and end apart: 4 -> 5, of which waited for: 3 -> 4; matrix products, arithmetic and copies ran while one was open for 5% -> 5% of each run, Pallas kernels for 0% -> 0%
where the time goes in v9:
time: 164 us; the launch traced here: 163 us
  blocking collectives  74 us (45%)
  starting transfers between devices  38 us (23%)
  waiting for transfers between devices  21.8 us (13%)
  between operations  13.9 us (8%)
  local copies, waits for them, and re-layouts  7.63 us (5%)
  other arithmetic  5.45 us (3%)
  matrix products  2.43 us (1%)
    all_to_all x5, blocking collectives, swap(): return lax.all_to_all(values, axes, split_axis=0, concat_axis=0, tiled=True)  60.6 us
    all_to_all x3, starting transfers between devices, swap(): return lax.all_to_all(values, axes, split_axis=0, concat_axis=0, tiled=True)  31.1 us
    all_to_all x3, waiting for transfers between devices, swap(): return lax.all_to_all(values, axes, split_axis=0, concat_axis=0, tiled=True)  20.7 us
    all_gather x1, blocking collectives, local(): qkv_block = lax.all_gather(w_qkv[0, :, 0], 'y', axis=0, tiled=True)  10.4 us
    ppermute x1, starting transfers between devices, local(): far = lax.ppermute(near, 'c', [(0, 1), (1, 0)])  6.94 us
  transfers between devices with their start and end apart: 5, of which 4 were waited for; matrix products, arithmetic and copies ran while one was open for 5% of the time, Pallas kernels for 0%

profile of v9, /device:TPU:1, one launch (start us, length us, event | category | flops | bytes accessed | tf_op | source)
XLA Modules:
  0.0 163.3 jit_solution(16647899689913125924)
XLA Ops:
  6.6 0.8 fusion.48
  7.4 0.8 fusion.26
  8.6 0.8 pad_maximum_fusion
  9.5 15.9 %all-to-all-start = ((bf16[16,72,128]{2,1,0:T(8,128)(2,1)}), bf16[16,72,128]{2,1,0:T(8,128)(2,1)S(1)}, u32[]{:S(2)}, u32[]{:S(2)}) async-start(bf16[16,72,128]{2,1,0:T(8,128)(2,1)} %pad_maximum_fusion), calls=%async_computation | async-start | bytes 589824 | tf_op jit(solution)/shard_map/all_to_all | solution.py:27
  25.5 0.7 pad_maximum_fusion.1
  26.5 10.4 %all-gather = bf16[1,128,1,512]{3,1,2,0:T(8,128)(2,1)S(1)} all-gather(bf16[1,32,1,512]{3,1,2,0:T(8,128)(2,1)S(1)} %copy-done.6), channel_id=2, replica_groups=mesh['y'=4,'zh'=4,'zl'=4,'x'=4,'c'=2] {'y'}, dimensions={1}, use_global_device_ids=true | all-gather | bytes 163840 | tf_op jit(solution)/shard_map/all_gather | solution.py:62
  37.3 1.9 %all-to-all-done = bf16[16,72,128]{2,1,0:T(8,128)(2,1)S(1)} async-done(((bf16[16,72,128]{2,1,0:T(8,128)(2,1)}), bf16[16,72,128]{2,1,0:T(8,128)(2,1)S(1)}, u32[]{:S(2)}, u32[]{:S(2)}) %all-to-all-start) | async-done | bytes 294944 | tf_op jit(solution)/shard_map/all_to_all | solution.py:27
  39.3 0.7 reshape.224
  40.0 11.7 %all-to-all-start.1 = ((bf16[16,4,512]{2,1,0:T(4,128)(2,1)}), bf16[16,4,512]{2,1,0:T(4,128)(2,1)S(1)}, u32[]{:S(2)}, u32[]{:S(2)}) async-start(bf16[16,4,512]{2,1,0:T(4,128)(2,1)} %reshape.224), calls=%async_computation.1 | async-start | bytes 131072 | tf_op jit(solution)/shard_map/all_to_all | solution.py:27
  53.0 10.3 %all-to-all-done.1 = bf16[16,4,512]{2,1,0:T(4,128)(2,1)S(1)} async-done(((bf16[16,4,512]{2,1,0:T(4,128)(2,1)}), bf16[16,4,512]{2,1,0:T(4,128)(2,1)S(1)}, u32[]{:S(2)}, u32[]{:S(2)}) %all-to-all-start.1) | async-done | bytes 65568 | tf_op jit(solution)/shard_map/all_to_all | solution.py:27
  64.7 8.2 %all_to_all.40 = bf16[4,8,128]{2,1,0:T(8,128)(2,1)S(1)} all-to-all(bf16[4,8,128]{2,1,0:T(8,128)(2,1)S(1)} %broadcast_in_dim.39), channel_id=1, replica_groups=mesh['y'=4,'zh'=4,'zl'=4,'x'=4,'c'=2] {'y'}, dimensions={0} | all-to-all | bytes 16384 | tf_op jit(solution)/shard_map/all_to_all | solution.py:27
  73.0 15.8 %all_to_all.41 = f32[32,2,128]{2,1,0:T(2,128)S(1)} all-to-all(f32[32,2,128]{2,1,0:T(2,128)S(1)} %reshape.235), channel_id=1, replica_groups=mesh['y'=4,'zh'=4,'zl'=4,'x'=4,'c'=2] {'y','x','c'}, dimensions={0} | all-to-all | bytes 65536 | tf_op jit(solution)/shard_map/all_to_all | solution.py:27
  88.8 0.6 broadcast_in_dim.40
  89.5 3.5 %all-to-all-start.4 = ((bf16[16,8,128]{2,1,0:T(8,128)(2,1)}), bf16[16,8,128]{2,1,0:T(8,128)(2,1)S(1)}, u32[]{:S(2)}, u32[]{:S(2)}) async-start(bf16[16,8,128]{2,1,0:T(8,128)(2,1)} %broadcast_in_dim.40), calls=%async_computation.4 | async-start | bytes 65536 | tf_op jit(solution)/shard_map/all_to_all | solution.py:27
  93.0 1.5 slice_bitcast_fusion
  94.5 1.2 slice.85
  95.8 8.6 %all-to-all-done.4 = bf16[16,8,128]{2,1,0:T(8,128)(2,1)S(1)} async-done(((bf16[16,8,128]{2,1,0:T(8,128)(2,1)}), bf16[16,8,128]{2,1,0:T(8,128)(2,1)S(1)}, u32[]{:S(2)}, u32[]{:S(2)}) %all-to-all-start.4) | async-done | bytes 32800 | tf_op jit(solution)/shard_map/all_to_all | solution.py:27
  105.3 3.1 %all-gather.2 = f32[32,896]{1,0:T(8,128)S(1)} all-gather(f32[16,896]{1,0:T(8,128)S(1)} %pad_maximum_fusion.2), channel_id=4, replica_groups=mesh['y'=4,'zh'=4,'zl'=4,'x'=4,'c'=2] {'c'}, dimensions={0}, use_global_device_ids=true | all-gather | bytes 172032 | tf_op jit(solution)/shard_map/all_gather | solution.py:141
  109.2 14.9 %all_to_all.42 = bf16[4,16,8,128]{3,2,1,0:T(8,128)(2,1)S(1)} all-to-all(bf16[4,16,8,128]{3,2,1,0:T(8,128)(2,1)S(1)} %broadcast_in_dim.43), channel_id=1, replica_groups=mesh['y'=4,'zh'=4,'zl'=4,'x'=4,'c'=2] {'zh'}, dimensions={0} | all-to-all | bytes 262144 | tf_op jit(solution)/shard_map/all_to_all | solution.py:27
  124.2 10.0 %all_to_all.43 = bf16[4,16,8,128]{3,2,1,0:T(8,128)(2,1)S(1)} all-to-all(bf16[4,16,8,128]{3,2,1,0:T(8,128)(2,1)S(1)} %broadcast_in_dim.44), channel_id=1, replica_groups=mesh['y'=4,'zh'=4,'zl'=4,'x'=4,'c'=2] {'zl'}, dimensions={0} | all-to-all | bytes 262144 | tf_op jit(solution)/shard_map/all_to_all | solution.py:27
  134.3 11.7 %all_to_all.44 = bf16[16,16,1024]{2,1,0:T(8,128)(2,1)S(1)} all-to-all(bf16[16,16,1024]{2,1,0:T(8,128)(2,1)S(1)} %broadcast_in_dim.46), channel_id=1, replica_groups=mesh['y'=4,'zh'=4,'zl'=4,'x'=4,'c'=2] {'y','x'}, dimensions={0} | all-to-all | bytes 1048576 | tf_op jit(solution)/shard_map/all_to_all | solution.py:27
  146.1 6.9 %collective-permute-start = (bf16[256,1024]{1,0:T(8,128)(2,1)S(1)}, bf16[256,1024]{1,0:T(8,128)(2,1)S(1)}, u32[]{:S(2)}, u32[]{:S(2)}) collective-permute-start(bf16[256,1024]{1,0:T(8,128)(2,1)S(1)} %bitcast.122), channel_id=1, source_target_pairs={{0,1},{1,0},{2,3},{3,2},{4,5},{5,4},{6,7},{7,6},{8,9},{9,8},{10,11... | collective-permute-start | bytes 1572872 | tf_op jit(solution)/shard_map/ppermute | solution.py:151
  153.4 1.1 collective-permute-done
  155.8 0.7 reshape.246
  (118 shorter events, 7.8 us)
Async XLA Ops:
  6.5 30.5 %copy-start = (bf16[1,2048,2]{1,2,0:T(2,128)(2,1)S(1)}, bf16[1,2048,2]{1,2,0:T(2,128)(2,1)}, u32[]{:S(2)}) copy-start(bf16[1,2048,2]{1,2,0:T(2,128)(2,1)} %param.19) | copy-start | bytes 24580
  6.5 19.9 %copy-start.5 = (bf16[4,2048]{1,0:T(4,128)(2,1)S(1)}, bf16[4,2048]{1,0:T(4,128)(2,1)}, u32[]{:S(2)}) copy-start(bf16[4,2048]{1,0:T(4,128)(2,1)} %param.15) | copy-start | bytes 49156
  6.5 30.5 %copy-start.9 = (f32[1,2048]{1,0:T(1,128)S(1)}, f32[1,2048]{1,0:T(1,128)}, u32[]{:S(2)}) copy-start(f32[1,2048]{1,0:T(1,128)} %param.21) | copy-start | bytes 24580
  6.5 18.9 %copy-start.4 = (bf16[1,256,96]{1,2,0:T(8,128)(2,1)S(1)}, bf16[1,256,96]{1,2,0:T(8,128)(2,1)}, u32[]{:S(2)}) copy-start(bf16[1,256,96]{1,2,0:T(8,128)(2,1)} %param.25) | copy-start | bytes 147460
  6.5 18.9 %copy-start.3 = (bf16[1,256,96]{1,2,0:T(8,128)(2,1)S(1)}, bf16[1,256,96]{1,2,0:T(8,128)(2,1)}, u32[]{:S(2)}) copy-start(bf16[1,256,96]{1,2,0:T(8,128)(2,1)} %param.26) | copy-start | bytes 147460
  6.5 18.9 %copy-start.2 = (bf16[1,96,256]{2,1,0:T(8,128)(2,1)S(1)}, bf16[1,96,256]{2,1,0:T(8,128)(2,1)}, u32[]{:S(2)}) copy-start(bf16[1,96,256]{2,1,0:T(8,128)(2,1)} %param.27) | copy-start | bytes 147460
  6.6 19.6 %copy-start.12 = (s32[256]{0:T(256)S(1)}, s32[256]{0:T(256)}, u32[]{:S(2)}) copy-start(s32[256]{0:T(256)} %param.16) | copy-start | bytes 3076
  6.6 20.0 %copy-start.6 = (bf16[1,32,1,512]{3,1,2,0:T(8,128)(2,1)S(1)}, bf16[1,32,1,512]{3,1,2,0:T(8,128)(2,1)}, u32[]{:S(2)}) copy-start(bf16[1,32,1,512]{3,1,2,0:T(8,128)(2,1)} %param.18) | copy-start | bytes 98308
  8.6 43.7 %copy-start.7 = (f32[1,2048]{1,0:T(1,128)S(1)}, f32[1,2048]{1,0:T(1,128)}, u32[]{:S(2)}) copy-start(f32[1,2048]{1,0:T(1,128)} %param.24) | copy-start | bytes 24580
  9.5 54.0 %copy-start.10 = (f32[1,128]{1,0:T(1,128)S(1)}, f32[1,128]{1,0:T(1,128)}, u32[]{:S(2)}) copy-start(f32[1,128]{1,0:T(1,128)} %param.23) | copy-start | bytes 1540
  9.5 54.3 %copy-start.11 = (f32[1,128]{1,0:T(1,128)S(1)}, f32[1,128]{1,0:T(1,128)}, u32[]{:S(2)}) copy-start(f32[1,128]{1,0:T(1,128)} %param.22) | copy-start | bytes 1540
  9.5 54.6 %copy-start.13 = (bf16[1,2,1024,1,128]{4,2,3,1,0:T(8,128)(2,1)S(1)}, bf16[1,2,1024,1,128]{4,2,3,1,0:T(8,128)(2,1)}, u32[]{:S(2)}) copy-start(bf16[1,2,1024,1,128]{4,2,3,1,0:T(8,128)(2,1)} %param.17) | copy-start | bytes 1572868
  9.5 29.6 %all-to-all-start = ((bf16[16,72,128]{2,1,0:T(8,128)(2,1)}), bf16[16,72,128]{2,1,0:T(8,128)(2,1)S(1)}, u32[]{:S(2)}, u32[]{:S(2)}) async-start(bf16[16,72,128]{2,1,0:T(8,128)(2,1)} %pad_maximum_fusion), calls=%async_computation | async-start | bytes 589824 | tf_op jit(solution)/shard_map/all_to_all | solution.py:27
  25.4 67.6 %all-gather.5.cloned.1.call-start = ((), (), s32[]{:S(2)}) async-start(), calls=%async_computation.8 | async-start | bytes 2506752 | tf_op jit(solution)/shard_map/all_gather | solution.py:61
  40.0 23.3 %all-to-all-start.1 = ((bf16[16,4,512]{2,1,0:T(4,128)(2,1)}), bf16[16,4,512]{2,1,0:T(4,128)(2,1)S(1)}, u32[]{:S(2)}, u32[]{:S(2)}) async-start(bf16[16,4,512]{2,1,0:T(4,128)(2,1)} %reshape.224), calls=%async_computation.1 | async-start | bytes 131072 | tf_op jit(solution)/shard_map/all_to_all | solution.py:27
  89.5 14.9 %all-to-all-start.4 = ((bf16[16,8,128]{2,1,0:T(8,128)(2,1)}), bf16[16,8,128]{2,1,0:T(8,128)(2,1)S(1)}, u32[]{:S(2)}, u32[]{:S(2)}) async-start(bf16[16,8,128]{2,1,0:T(8,128)(2,1)} %broadcast_in_dim.40), calls=%async_computation.4 | async-start | bytes 65536 | tf_op jit(solution)/shard_map/all_to_all | solution.py:27
  109.1 43.9 %copy-start.8 = (f32[2048]{0:T(1024)S(1)}, f32[2048]{0:T(1024)}, u32[]{:S(2)}) copy-start(f32[2048]{0:T(1024)} %param.28) | copy-start | bytes 24580
  109.2 43.9 %copy-start.1 = (bf16[2048,256]{1,0:T(8,128)(2,1)S(1)}, bf16[2048,256]{1,0:T(8,128)(2,1)}, u32[]{:S(2)}) copy-start(bf16[2048,256]{1,0:T(8,128)(2,1)} %param.29) | copy-start | bytes 3145732
  146.1 8.5 %collective-permute-start = (bf16[256,1024]{1,0:T(8,128)(2,1)S(1)}, bf16[256,1024]{1,0:T(8,128)(2,1)S(1)}, u32[]{:S(2)}, u32[]{:S(2)}) collective-permute-start(bf16[256,1024]{1,0:T(8,128)(2,1)S(1)} %bitcast.122), channel_id=1, source_target_pairs={{0,1},{1,0},{2,3},{3,2},{4,5},{5,4},{6,7},{7,6},{8,9},{9,8},{10,11... | collective-permute-start | bytes 1572872 | tf_op jit(solution)/shard_map/ppermute | solution.py:151
Sparse Core Ops, SparseCore 0:
  29.2 62.1 all-gather.4

commit v10 on v9

--- a/solution.py
+++ b/solution.py
@@ -85,25 +85,21 @@
     residual = own_core(own_row(tokens).reshape(Y, C, seg), 1).reshape(8, head_dim)
     slot = jnp.arange(kv_cache.shape[2], dtype=jnp.int32)
     inside = (slot[None, :] >= starts[:, None]) & (slot[None, :] < limits[:, None])
-    inside = inside.astype(F32)
 
     depth = width // (Y * Z)
     sent = gained.reshape(rows, Y, Z, depth).transpose(2, 0, 1, 3).reshape(Z, rows, Y * depth)
     block = w_out[0].T
-    block = jnp.concatenate([block[:, :head_dim], block[:, head_dim:]], axis=0)
-    sent = jnp.concatenate(
-        [sent, jnp.zeros((Z, 8 - rows, head_dim), BF16), jnp.broadcast_to(block[None], (Z,) + block.shape)], axis=1
+    halves = [jnp.broadcast_to(block[None, :, q * head_dim : (q + 1) * head_dim], (Z, block.shape[0], head_dim)) for q in (0, 1)]
+    sent = jnp.concatenate([sent, jnp.zeros((Z, 8 - rows, head_dim), BF16)] + halves, axis=1)
+    arrived = swap(sent, DEPTH)
+    arrived, qkv_block, in_scale, head_gate, cosine, sine, residual, inside = lax.optimization_barrier(
+        (arrived, qkv_block, in_scale, head_gate, cosine, sine, residual, inside)
     )
-    arrived = swap(sent, DEPTH)
-    arrived, qkv_block, post_gain = lax.optimization_barrier((arrived, qkv_block, post_gain))
-    post_half = own_core(post_gain.reshape(X, C, seg), 1).reshape(X, seg)
     batch = arrived[:, :rows].reshape(Z * rows, Y * depth)
     out_block = arrived[:, 8:].reshape(Z, 2, -1, head_dim).transpose(1, 0, 2, 3).reshape(2, -1, head_dim)
     part = jnp.dot(batch, qkv_block, preferred_element_type=F32).astype(BF16)
-    part = swap(part.reshape(Z, rows, columns), DEPTH)
-    part, out_block, in_scale, head_gate, cosine, sine, residual, post_half, inside = lax.optimization_barrier(
-        (part, out_block, in_scale, head_gate, cosine, sine, residual, post_half, inside)
-    )
+    part, out_block = lax.optimization_barrier((part.reshape(Z, rows, columns), out_block))
+    part = swap(part, DEPTH)
     qkv = jnp.sum(part.astype(F32), axis=0) * in_scale
 
     query = qkv[:, : 2 * head_dim].reshape(rows, 2, head_dim)
@@ -115,7 +111,7 @@
     scale = head_dim ** (-0.5)
     keys, values = kv_cache[0, 0, :, 0], kv_cache[0, 1, :, 0]
     score = jnp.einsum("rqd,sd->rqs", query, keys, preferred_element_type=F32) * scale
-    weight = jnp.where(inside[:, None, :] > 0.0, jnp.exp(score), 0.0)
+    weight = jnp.where(inside[:, None, :], jnp.exp(score), 0.0)
     own = jnp.exp(jnp.sum(query.astype(F32) * key.astype(F32)[:, None], axis=-1) * scale)
     total = jnp.sum(weight, axis=-1) + own
     summed = jnp.einsum("rqs,sd->rqd", weight.astype(BF16), values, preferred_element_type=F32)
@@ -129,9 +125,11 @@
     projected = jnp.sum(part.reshape(Y, X * C, 2, head_dim), axis=1).reshape(8, head_dim)
     stream = (residual.astype(F32) + projected).astype(BF16)
 
+    stream, post_gain = lax.optimization_barrier((stream, post_gain))
+    post_half = own_core(post_gain.reshape(X, C, seg), 1).reshape(X, seg)
     gate_up = ffn[:, :, : 2 * units].transpose(1, 0, 2, 3)
     down = ffn[:, :, 2 * units :]
-    batch, gate_up, down = lax.optimization_barrier((spread(stream, DEPTH, Z), gate_up, down))
+    batch, gate_up, down, post_half = lax.optimization_barrier((spread(stream, DEPTH, Z), gate_up, down, post_half))
     batch = batch.reshape(Z, X, seg)
     wide = batch.astype(F32)
     squares = jnp.sum(wide * wide, axis=(1, 2)).reshape(Z, 1)

time: 164 us -> 164 us (level)
  blocking collectives: 74 us -> 96.6 us
  waiting for transfers between devices: 21.8 us -> 10.4 us
  starting transfers between devices: 38 us -> 27.3 us
    all_to_all x5 -> x6, blocking collectives: 60.6 us -> 83.3 us  [swap(): return lax.all_to_all(values, axes, split_axis=0, concat_axis=0, tiled=True)]
    all_to_all x3 -> x2, starting transfers between devices: 31.1 us -> 19.4 us  [swap(): return lax.all_to_all(values, axes, split_axis=0, concat_axis=0, tiled=True)]
    all_to_all x3 -> x2, waiting for transfers between devices: 20.7 us -> 9.26 us  [swap(): return lax.all_to_all(values, axes, split_axis=0, concat_axis=0, tiled=True)]
  transfers between devices with their start and end apart: 5 -> 4, of which waited for: 4 -> 3; matrix products, arithmetic and copies ran while one was open for 5% -> 5% of each run, Pallas kernels for 0% -> 0%
where the time goes in v10:
time: 164 us; the launch traced here: 163 us
  blocking collectives  96.6 us (59%)
  starting transfers between devices  27.3 us (17%)
  between operations  13.9 us (8%)
  waiting for transfers between devices  10.4 us (6%)
  local copies, waits for them, and re-layouts  6.97 us (4%)
  other arithmetic  5.44 us (3%)
  matrix products  2.43 us (1%)
    all_to_all x6, blocking collectives, swap(): return lax.all_to_all(values, axes, split_axis=0, concat_axis=0, tiled=True)  83.3 us
    all_to_all x2, starting transfers between devices, swap(): return lax.all_to_all(values, axes, split_axis=0, concat_axis=0, tiled=True)  19.4 us
    all_gather x1, blocking collectives, local(): qkv_block = lax.all_gather(w_qkv[0, :, 0], 'y', axis=0, tiled=True)  10.4 us
    all_to_all x2, waiting for transfers between devices, swap(): return lax.all_to_all(values, axes, split_axis=0, concat_axis=0, tiled=True)  9.26 us
    ppermute x1, starting transfers between devices, local(): far = lax.ppermute(near, 'c', [(0, 1), (1, 0)])  7.84 us
  transfers between devices with their start and end apart: 4, of which 3 were waited for; matrix products, arithmetic and copies ran while one was open for 5% of the time, Pallas kernels for 0%

profile of v10, /device:TPU:1, one launch (start us, length us, event | category | flops | bytes accessed | tf_op | source)
XLA Modules:
  0.0 163.0 jit_solution(13107783377533839267)
XLA Ops:
  6.6 0.8 fusion.47
  7.4 0.8 fusion.26
  8.6 0.8 pad_maximum_fusion
  9.5 15.9 %all-to-all-start = ((bf16[16,72,128]{2,1,0:T(8,128)(2,1)}), bf16[16,72,128]{2,1,0:T(8,128)(2,1)S(1)}, u32[]{:S(2)}, u32[]{:S(2)}) async-start(bf16[16,72,128]{2,1,0:T(8,128)(2,1)} %pad_maximum_fusion), calls=%async_computation | async-start | bytes 589824 | tf_op jit(solution)/shard_map/all_to_all | solution.py:27
  25.4 0.7 pad_maximum_fusion.1
  26.8 10.4 %all-gather = bf16[1,128,1,512]{3,1,2,0:T(8,128)(2,1)S(1)} all-gather(bf16[1,32,1,512]{3,1,2,0:T(8,128)(2,1)S(1)} %copy-done.6), channel_id=2, replica_groups=mesh['y'=4,'zh'=4,'zl'=4,'x'=4,'c'=2] {'y'}, dimensions={1}, use_global_device_ids=true | all-gather | bytes 163840 | tf_op jit(solution)/shard_map/all_gather | solution.py:62
  37.4 1.7 %all-to-all-done = bf16[16,72,128]{2,1,0:T(8,128)(2,1)S(1)} async-done(((bf16[16,72,128]{2,1,0:T(8,128)(2,1)}), bf16[16,72,128]{2,1,0:T(8,128)(2,1)S(1)}, u32[]{:S(2)}, u32[]{:S(2)}) %all-to-all-start) | async-done | bytes 294944 | tf_op jit(solution)/shard_map/all_to_all | solution.py:27
  39.4 23.1 %all_to_all.40 = bf16[16,4,512]{2,1,0:T(4,128)(2,1)S(1)} all-to-all(bf16[16,4,512]{2,1,0:T(4,128)(2,1)S(1)} %reshape.228), channel_id=1, replica_groups=mesh['y'=4,'zh'=4,'zl'=4,'x'=4,'c'=2] {'zh','zl'}, dimensions={0} | all-to-all | bytes 131072 | tf_op jit(solution)/shard_map/all_to_all | solution.py:27
  63.8 8.2 %all_to_all.41 = bf16[4,8,128]{2,1,0:T(8,128)(2,1)S(1)} all-to-all(bf16[4,8,128]{2,1,0:T(8,128)(2,1)S(1)} %broadcast_in_dim.42), channel_id=1, replica_groups=mesh['y'=4,'zh'=4,'zl'=4,'x'=4,'c'=2] {'y'}, dimensions={0} | all-to-all | bytes 16384 | tf_op jit(solution)/shard_map/all_to_all | solution.py:27
  72.2 15.9 %all_to_all.42 = f32[32,2,128]{2,1,0:T(2,128)S(1)} all-to-all(f32[32,2,128]{2,1,0:T(2,128)S(1)} %reshape.233), channel_id=1, replica_groups=mesh['y'=4,'zh'=4,'zl'=4,'x'=4,'c'=2] {'y','x','c'}, dimensions={0} | all-to-all | bytes 65536 | tf_op jit(solution)/shard_map/all_to_all | solution.py:27
  88.2 0.6 broadcast_in_dim.43
  88.8 3.5 %all-to-all-start.4 = ((bf16[16,8,128]{2,1,0:T(8,128)(2,1)}), bf16[16,8,128]{2,1,0:T(8,128)(2,1)S(1)}, u32[]{:S(2)}, u32[]{:S(2)}) async-start(bf16[16,8,128]{2,1,0:T(8,128)(2,1)} %broadcast_in_dim.43), calls=%async_computation.4 | async-start | bytes 65536 | tf_op jit(solution)/shard_map/all_to_all | solution.py:27
  92.3 0.5 broadcast.164
  92.8 0.6 reduce.12
  93.5 1.5 slice_bitcast_fusion
  95.0 1.2 slice.85
  96.3 7.5 %all-to-all-done.4 = bf16[16,8,128]{2,1,0:T(8,128)(2,1)S(1)} async-done(((bf16[16,8,128]{2,1,0:T(8,128)(2,1)}), bf16[16,8,128]{2,1,0:T(8,128)(2,1)S(1)}, u32[]{:S(2)}, u32[]{:S(2)}) %all-to-all-start.4) | async-done | bytes 32800 | tf_op jit(solution)/shard_map/all_to_all | solution.py:27
  104.8 2.9 %all-gather.2 = f32[32,896]{1,0:T(8,128)S(1)} all-gather(f32[16,896]{1,0:T(8,128)S(1)} %pad_maximum_fusion.2), channel_id=4, replica_groups=mesh['y'=4,'zh'=4,'zl'=4,'x'=4,'c'=2] {'c'}, dimensions={0}, use_global_device_ids=true | all-gather | bytes 172032 | tf_op jit(solution)/shard_map/all_gather | solution.py:139
  108.5 15.2 %all_to_all.43 = bf16[4,16,8,128]{3,2,1,0:T(8,128)(2,1)S(1)} all-to-all(bf16[4,16,8,128]{3,2,1,0:T(8,128)(2,1)S(1)} %broadcast_in_dim.46), channel_id=1, replica_groups=mesh['y'=4,'zh'=4,'zl'=4,'x'=4,'c'=2] {'zh'}, dimensions={0} | all-to-all | bytes 262144 | tf_op jit(solution)/shard_map/all_to_all | solution.py:27
  123.8 9.2 %all_to_all.44 = bf16[4,16,8,128]{3,2,1,0:T(8,128)(2,1)S(1)} all-to-all(bf16[4,16,8,128]{3,2,1,0:T(8,128)(2,1)S(1)} %broadcast_in_dim.47), channel_id=1, replica_groups=mesh['y'=4,'zh'=4,'zl'=4,'x'=4,'c'=2] {'zl'}, dimensions={0} | all-to-all | bytes 262144 | tf_op jit(solution)/shard_map/all_to_all | solution.py:27
  133.1 11.7 %all_to_all.45 = bf16[16,16,1024]{2,1,0:T(8,128)(2,1)S(1)} all-to-all(bf16[16,16,1024]{2,1,0:T(8,128)(2,1)S(1)} %broadcast_in_dim.49), channel_id=1, replica_groups=mesh['y'=4,'zh'=4,'zl'=4,'x'=4,'c'=2] {'y','x'}, dimensions={0} | all-to-all | bytes 1048576 | tf_op jit(solution)/shard_map/all_to_all | solution.py:27
  144.8 7.8 %collective-permute-start = (bf16[256,1024]{1,0:T(8,128)(2,1)S(1)}, bf16[256,1024]{1,0:T(8,128)(2,1)S(1)}, u32[]{:S(2)}, u32[]{:S(2)}) collective-permute-start(bf16[256,1024]{1,0:T(8,128)(2,1)S(1)} %bitcast.122), channel_id=1, source_target_pairs={{0,1},{1,0},{2,3},{3,2},{4,5},{5,4},{6,7},{7,6},{8,9},{9,8},{10,11... | collective-permute-start | bytes 1572872 | tf_op jit(solution)/shard_map/ppermute | solution.py:149
  153.1 1.1 collective-permute-done
  155.4 0.7 reshape.246
  (116 shorter events, 6.7 us)
Async XLA Ops:
  6.5 30.6 %copy-start = (bf16[1,2048,2]{1,2,0:T(2,128)(2,1)S(1)}, bf16[1,2048,2]{1,2,0:T(2,128)(2,1)}, u32[]{:S(2)}) copy-start(bf16[1,2048,2]{1,2,0:T(2,128)(2,1)} %param.19) | copy-start | bytes 24580
  6.5 20.2 %copy-start.5 = (bf16[4,2048]{1,0:T(4,128)(2,1)S(1)}, bf16[4,2048]{1,0:T(4,128)(2,1)}, u32[]{:S(2)}) copy-start(bf16[4,2048]{1,0:T(4,128)(2,1)} %param.15) | copy-start | bytes 49156
  6.5 30.6 %copy-start.9 = (f32[1,2048]{1,0:T(1,128)S(1)}, f32[1,2048]{1,0:T(1,128)}, u32[]{:S(2)}) copy-start(f32[1,2048]{1,0:T(1,128)} %param.21) | copy-start | bytes 24580
  6.5 18.9 %copy-start.2 = (bf16[1,96,256]{2,1,0:T(8,128)(2,1)S(1)}, bf16[1,96,256]{2,1,0:T(8,128)(2,1)}, u32[]{:S(2)}) copy-start(bf16[1,96,256]{2,1,0:T(8,128)(2,1)} %param.27) | copy-start | bytes 147460
  6.5 18.9 %copy-start.3 = (bf16[1,256,96]{1,2,0:T(8,128)(2,1)S(1)}, bf16[1,256,96]{1,2,0:T(8,128)(2,1)}, u32[]{:S(2)}) copy-start(bf16[1,256,96]{1,2,0:T(8,128)(2,1)} %param.26) | copy-start | bytes 147460
  6.5 18.9 %copy-start.4 = (bf16[1,256,96]{1,2,0:T(8,128)(2,1)S(1)}, bf16[1,256,96]{1,2,0:T(8,128)(2,1)}, u32[]{:S(2)}) copy-start(bf16[1,256,96]{1,2,0:T(8,128)(2,1)} %param.25) | copy-start | bytes 147460
  6.6 19.6 %copy-start.12 = (s32[256]{0:T(256)S(1)}, s32[256]{0:T(256)}, u32[]{:S(2)}) copy-start(s32[256]{0:T(256)} %param.16) | copy-start | bytes 3076
  6.6 20.3 %copy-start.6 = (bf16[1,32,1,512]{3,1,2,0:T(8,128)(2,1)S(1)}, bf16[1,32,1,512]{3,1,2,0:T(8,128)(2,1)}, u32[]{:S(2)}) copy-start(bf16[1,32,1,512]{3,1,2,0:T(8,128)(2,1)} %param.18) | copy-start | bytes 98308
  9.5 53.2 %copy-start.10 = (f32[1,128]{1,0:T(1,128)S(1)}, f32[1,128]{1,0:T(1,128)}, u32[]{:S(2)}) copy-start(f32[1,128]{1,0:T(1,128)} %param.23) | copy-start | bytes 1540
  9.5 53.5 %copy-start.11 = (f32[1,128]{1,0:T(1,128)S(1)}, f32[1,128]{1,0:T(1,128)}, u32[]{:S(2)}) copy-start(f32[1,128]{1,0:T(1,128)} %param.22) | copy-start | bytes 1540
  9.5 53.8 %copy-start.13 = (bf16[1,2,1024,1,128]{4,2,3,1,0:T(8,128)(2,1)S(1)}, bf16[1,2,1024,1,128]{4,2,3,1,0:T(8,128)(2,1)}, u32[]{:S(2)}) copy-start(bf16[1,2,1024,1,128]{4,2,3,1,0:T(8,128)(2,1)} %param.17) | copy-start | bytes 1572868
  9.5 29.6 %all-to-all-start = ((bf16[16,72,128]{2,1,0:T(8,128)(2,1)}), bf16[16,72,128]{2,1,0:T(8,128)(2,1)S(1)}, u32[]{:S(2)}, u32[]{:S(2)}) async-start(bf16[16,72,128]{2,1,0:T(8,128)(2,1)} %pad_maximum_fusion), calls=%async_computation | async-start | bytes 589824 | tf_op jit(solution)/shard_map/all_to_all | solution.py:27
  25.4 68.1 %all-gather.5.cloned.1.call-start = ((), (), s32[]{:S(2)}) async-start(), calls=%async_computation.8 | async-start | bytes 2506752 | tf_op jit(solution)/shard_map/all_gather | solution.py:61
  37.4 55.4 %copy-start.7 = (f32[1,2048]{1,0:T(1,128)S(1)}, f32[1,2048]{1,0:T(1,128)}, u32[]{:S(2)}) copy-start(f32[1,2048]{1,0:T(1,128)} %param.24) | copy-start | bytes 24580
  88.8 15.0 %all-to-all-start.4 = ((bf16[16,8,128]{2,1,0:T(8,128)(2,1)}), bf16[16,8,128]{2,1,0:T(8,128)(2,1)S(1)}, u32[]{:S(2)}, u32[]{:S(2)}) async-start(bf16[16,8,128]{2,1,0:T(8,128)(2,1)} %broadcast_in_dim.43), calls=%async_computation.4 | async-start | bytes 65536 | tf_op jit(solution)/shard_map/all_to_all | solution.py:27
  108.4 44.3 %copy-start.8 = (f32[2048]{0:T(1024)S(1)}, f32[2048]{0:T(1024)}, u32[]{:S(2)}) copy-start(f32[2048]{0:T(1024)} %param.28) | copy-start | bytes 24580
  108.5 44.3 %copy-start.1 = (bf16[2048,256]{1,0:T(8,128)(2,1)S(1)}, bf16[2048,256]{1,0:T(8,128)(2,1)}, u32[]{:S(2)}) copy-start(bf16[2048,256]{1,0:T(8,128)(2,1)} %param.29) | copy-start | bytes 3145732
  144.8 9.4 %collective-permute-start = (bf16[256,1024]{1,0:T(8,128)(2,1)S(1)}, bf16[256,1024]{1,0:T(8,128)(2,1)S(1)}, u32[]{:S(2)}, u32[]{:S(2)}) collective-permute-start(bf16[256,1024]{1,0:T(8,128)(2,1)S(1)} %bitcast.122), channel_id=1, source_target_pairs={{0,1},{1,0},{2,3},{3,2},{4,5},{5,4},{6,7},{7,6},{8,9},{9,8},{10,11... | collective-permute-start | bytes 1572872 | tf_op jit(solution)/shard_map/ppermute | solution.py:149
Sparse Core Ops, SparseCore 0:
  29.2 61.6 all-gather.4

commit v11 on v10

--- a/solution.py
+++ b/solution.py
@@ -141,8 +141,8 @@
     both = (both[:, :-head_dim] * scale).reshape(Z, Y, 2 * units)
     hidden = (jax.nn.silu(both[..., :units]) * both[..., units:]).astype(BF16)
     part = jnp.einsum("byf,yxfk->bxk", hidden, down, preferred_element_type=F32).astype(BF16)
-    part = jnp.sum(spread(part.reshape(Z, 8, head_dim), "zh", ZH).astype(F32), axis=0).astype(BF16)
-    lowered = jnp.sum(spread(part, "zl", ZL).astype(F32), axis=0)
+    part = jnp.sum(spread(part.reshape(Z, 8, head_dim), "zl", ZL).astype(F32), axis=0).astype(BF16)
+    lowered = jnp.sum(spread(part, "zh", ZH).astype(F32), axis=0)
     piece = (wide.reshape(Z, 8, head_dim) + lowered).astype(BF16).reshape(Z, part_width)
 
     near = spread(piece, ("y", "x"), Y * X).reshape(Y * X * Z, part_width)

time: 164 us -> 162 us (0.988)
  no operation moved by 1% of the time
where the time goes in v11:
time: 162 us
  blocking collectives  95.2 us (59%)
  starting transfers between devices  27.3 us (17%)
  between operations  13.9 us (9%)
  waiting for transfers between devices  10.4 us (6%)
  local copies, waits for them, and re-layouts  6.97 us (4%)
  other arithmetic  5.44 us (3%)
  matrix products  2.44 us (2%)
    all_to_all x6, blocking collectives, swap(): return lax.all_to_all(values, axes, split_axis=0, concat_axis=0, tiled=True)  82 us
    all_to_all x2, starting transfers between devices, swap(): return lax.all_to_all(values, axes, split_axis=0, concat_axis=0, tiled=True)  19.4 us
    all_gather x1, blocking collectives, local(): qkv_block = lax.all_gather(w_qkv[0, :, 0], 'y', axis=0, tiled=True)  10.4 us
    all_to_all x2, waiting for transfers between devices, swap(): return lax.all_to_all(values, axes, split_axis=0, concat_axis=0, tiled=True)  9.26 us
    ppermute x1, starting transfers between devices, local(): far = lax.ppermute(near, 'c', [(0, 1), (1, 0)])  7.85 us
  transfers between devices with their start and end apart: 4, of which 3 were waited for; matrix products, arithmetic and copies ran while one was open for 5% of the time, Pallas kernels for 0%

profile of v11, /device:TPU:1, one launch (start us, length us, event | category | flops | bytes accessed | tf_op | source)
XLA Modules:
  0.0 161.6 jit_solution(16570574454729380939)
XLA Ops:
  6.6 0.8 fusion.47
  7.4 0.8 fusion.26
  8.6 0.8 pad_maximum_fusion
  9.5 15.9 %all-to-all-start = ((bf16[16,72,128]{2,1,0:T(8,128)(2,1)}), bf16[16,72,128]{2,1,0:T(8,128)(2,1)S(1)}, u32[]{:S(2)}, u32[]{:S(2)}) async-start(bf16[16,72,128]{2,1,0:T(8,128)(2,1)} %pad_maximum_fusion), calls=%async_computation | async-start | bytes 589824 | tf_op jit(solution)/shard_map/all_to_all | solution.py:27
  25.4 0.7 pad_maximum_fusion.1
  26.8 10.4 %all-gather = bf16[1,128,1,512]{3,1,2,0:T(8,128)(2,1)S(1)} all-gather(bf16[1,32,1,512]{3,1,2,0:T(8,128)(2,1)S(1)} %copy-done.6), channel_id=2, replica_groups=mesh['y'=4,'zh'=4,'zl'=4,'x'=4,'c'=2] {'y'}, dimensions={1}, use_global_device_ids=true | all-gather | bytes 163840 | tf_op jit(solution)/shard_map/all_gather | solution.py:62
  37.4 1.7 %all-to-all-done = bf16[16,72,128]{2,1,0:T(8,128)(2,1)S(1)} async-done(((bf16[16,72,128]{2,1,0:T(8,128)(2,1)}), bf16[16,72,128]{2,1,0:T(8,128)(2,1)S(1)}, u32[]{:S(2)}, u32[]{:S(2)}) %all-to-all-start) | async-done | bytes 294944 | tf_op jit(solution)/shard_map/all_to_all | solution.py:27
  39.4 23.1 %all_to_all.40 = bf16[16,4,512]{2,1,0:T(4,128)(2,1)S(1)} all-to-all(bf16[16,4,512]{2,1,0:T(4,128)(2,1)S(1)} %reshape.228), channel_id=1, replica_groups=mesh['y'=4,'zh'=4,'zl'=4,'x'=4,'c'=2] {'zh','zl'}, dimensions={0} | all-to-all | bytes 131072 | tf_op jit(solution)/shard_map/all_to_all | solution.py:27
  63.8 8.2 %all_to_all.41 = bf16[4,8,128]{2,1,0:T(8,128)(2,1)S(1)} all-to-all(bf16[4,8,128]{2,1,0:T(8,128)(2,1)S(1)} %broadcast_in_dim.42), channel_id=1, replica_groups=mesh['y'=4,'zh'=4,'zl'=4,'x'=4,'c'=2] {'y'}, dimensions={0} | all-to-all | bytes 16384 | tf_op jit(solution)/shard_map/all_to_all | solution.py:27
  72.2 15.9 %all_to_all.42 = f32[32,2,128]{2,1,0:T(2,128)S(1)} all-to-all(f32[32,2,128]{2,1,0:T(2,128)S(1)} %reshape.233), channel_id=1, replica_groups=mesh['y'=4,'zh'=4,'zl'=4,'x'=4,'c'=2] {'y','x','c'}, dimensions={0} | all-to-all | bytes 65536 | tf_op jit(solution)/shard_map/all_to_all | solution.py:27
  88.2 0.6 broadcast_in_dim.43
  88.8 3.5 %all-to-all-start.4 = ((bf16[16,8,128]{2,1,0:T(8,128)(2,1)}), bf16[16,8,128]{2,1,0:T(8,128)(2,1)S(1)}, u32[]{:S(2)}, u32[]{:S(2)}) async-start(bf16[16,8,128]{2,1,0:T(8,128)(2,1)} %broadcast_in_dim.43), calls=%async_computation.4 | async-start | bytes 65536 | tf_op jit(solution)/shard_map/all_to_all | solution.py:27
  92.3 0.5 broadcast.164
  92.8 0.6 reduce.12
  93.5 1.5 slice_bitcast_fusion
  95.0 1.2 slice.85
  96.3 7.5 %all-to-all-done.4 = bf16[16,8,128]{2,1,0:T(8,128)(2,1)S(1)} async-done(((bf16[16,8,128]{2,1,0:T(8,128)(2,1)}), bf16[16,8,128]{2,1,0:T(8,128)(2,1)S(1)}, u32[]{:S(2)}, u32[]{:S(2)}) %all-to-all-start.4) | async-done | bytes 32800 | tf_op jit(solution)/shard_map/all_to_all | solution.py:27
  104.8 2.9 %all-gather.2 = f32[32,896]{1,0:T(8,128)S(1)} all-gather(f32[16,896]{1,0:T(8,128)S(1)} %pad_maximum_fusion.2), channel_id=4, replica_groups=mesh['y'=4,'zh'=4,'zl'=4,'x'=4,'c'=2] {'c'}, dimensions={0}, use_global_device_ids=true | all-gather | bytes 172032 | tf_op jit(solution)/shard_map/all_gather | solution.py:139
  108.5 7.4 %all_to_all.43 = bf16[4,16,8,128]{3,2,1,0:T(8,128)(2,1)S(1)} all-to-all(bf16[4,16,8,128]{3,2,1,0:T(8,128)(2,1)S(1)} %broadcast_in_dim.46), channel_id=1, replica_groups=mesh['y'=4,'zh'=4,'zl'=4,'x'=4,'c'=2] {'zl'}, dimensions={0} | all-to-all | bytes 262144 | tf_op jit(solution)/shard_map/all_to_all | solution.py:27
  116.0 15.6 %all_to_all.44 = bf16[4,16,8,128]{3,2,1,0:T(8,128)(2,1)S(1)} all-to-all(bf16[4,16,8,128]{3,2,1,0:T(8,128)(2,1)S(1)} %broadcast_in_dim.47), channel_id=1, replica_groups=mesh['y'=4,'zh'=4,'zl'=4,'x'=4,'c'=2] {'zh'}, dimensions={0} | all-to-all | bytes 262144 | tf_op jit(solution)/shard_map/all_to_all | solution.py:27
  131.7 11.8 %all_to_all.45 = bf16[16,16,1024]{2,1,0:T(8,128)(2,1)S(1)} all-to-all(bf16[16,16,1024]{2,1,0:T(8,128)(2,1)S(1)} %broadcast_in_dim.49), channel_id=1, replica_groups=mesh['y'=4,'zh'=4,'zl'=4,'x'=4,'c'=2] {'y','x'}, dimensions={0} | all-to-all | bytes 1048576 | tf_op jit(solution)/shard_map/all_to_all | solution.py:27
  143.5 7.9 %collective-permute-start = (bf16[256,1024]{1,0:T(8,128)(2,1)S(1)}, bf16[256,1024]{1,0:T(8,128)(2,1)S(1)}, u32[]{:S(2)}, u32[]{:S(2)}) collective-permute-start(bf16[256,1024]{1,0:T(8,128)(2,1)S(1)} %bitcast.122), channel_id=1, source_target_pairs={{0,1},{1,0},{2,3},{3,2},{4,5},{5,4},{6,7},{7,6},{8,9},{9,8},{10,11... | collective-permute-start | bytes 1572872 | tf_op jit(solution)/shard_map/ppermute | solution.py:149
  151.7 1.1 collective-permute-done
  154.1 0.7 reshape.246
  (116 shorter events, 6.7 us)
Async XLA Ops:
  6.5 30.6 %copy-start = (bf16[1,2048,2]{1,2,0:T(2,128)(2,1)S(1)}, bf16[1,2048,2]{1,2,0:T(2,128)(2,1)}, u32[]{:S(2)}) copy-start(bf16[1,2048,2]{1,2,0:T(2,128)(2,1)} %param.19) | copy-start | bytes 24580
  6.5 20.2 %copy-start.5 = (bf16[4,2048]{1,0:T(4,128)(2,1)S(1)}, bf16[4,2048]{1,0:T(4,128)(2,1)}, u32[]{:S(2)}) copy-start(bf16[4,2048]{1,0:T(4,128)(2,1)} %param.15) | copy-start | bytes 49156
  6.5 30.6 %copy-start.9 = (f32[1,2048]{1,0:T(1,128)S(1)}, f32[1,2048]{1,0:T(1,128)}, u32[]{:S(2)}) copy-start(f32[1,2048]{1,0:T(1,128)} %param.21) | copy-start | bytes 24580
  6.5 18.9 %copy-start.2 = (bf16[1,96,256]{2,1,0:T(8,128)(2,1)S(1)}, bf16[1,96,256]{2,1,0:T(8,128)(2,1)}, u32[]{:S(2)}) copy-start(bf16[1,96,256]{2,1,0:T(8,128)(2,1)} %param.27) | copy-start | bytes 147460
  6.5 18.9 %copy-start.3 = (bf16[1,256,96]{1,2,0:T(8,128)(2,1)S(1)}, bf16[1,256,96]{1,2,0:T(8,128)(2,1)}, u32[]{:S(2)}) copy-start(bf16[1,256,96]{1,2,0:T(8,128)(2,1)} %param.26) | copy-start | bytes 147460
  6.5 18.9 %copy-start.4 = (bf16[1,256,96]{1,2,0:T(8,128)(2,1)S(1)}, bf16[1,256,96]{1,2,0:T(8,128)(2,1)}, u32[]{:S(2)}) copy-start(bf16[1,256,96]{1,2,0:T(8,128)(2,1)} %param.25) | copy-start | bytes 147460
  6.6 19.6 %copy-start.12 = (s32[256]{0:T(256)S(1)}, s32[256]{0:T(256)}, u32[]{:S(2)}) copy-start(s32[256]{0:T(256)} %param.16) | copy-start | bytes 3076
  6.6 20.3 %copy-start.6 = (bf16[1,32,1,512]{3,1,2,0:T(8,128)(2,1)S(1)}, bf16[1,32,1,512]{3,1,2,0:T(8,128)(2,1)}, u32[]{:S(2)}) copy-start(bf16[1,32,1,512]{3,1,2,0:T(8,128)(2,1)} %param.18) | copy-start | bytes 98308
  9.5 53.2 %copy-start.10 = (f32[1,128]{1,0:T(1,128)S(1)}, f32[1,128]{1,0:T(1,128)}, u32[]{:S(2)}) copy-start(f32[1,128]{1,0:T(1,128)} %param.23) | copy-start | bytes 1540
  9.5 53.5 %copy-start.11 = (f32[1,128]{1,0:T(1,128)S(1)}, f32[1,128]{1,0:T(1,128)}, u32[]{:S(2)}) copy-start(f32[1,128]{1,0:T(1,128)} %param.22) | copy-start | bytes 1540
  9.5 53.8 %copy-start.13 = (bf16[1,2,1024,1,128]{4,2,3,1,0:T(8,128)(2,1)S(1)}, bf16[1,2,1024,1,128]{4,2,3,1,0:T(8,128)(2,1)}, u32[]{:S(2)}) copy-start(bf16[1,2,1024,1,128]{4,2,3,1,0:T(8,128)(2,1)} %param.17) | copy-start | bytes 1572868
  9.5 29.6 %all-to-all-start = ((bf16[16,72,128]{2,1,0:T(8,128)(2,1)}), bf16[16,72,128]{2,1,0:T(8,128)(2,1)S(1)}, u32[]{:S(2)}, u32[]{:S(2)}) async-start(bf16[16,72,128]{2,1,0:T(8,128)(2,1)} %pad_maximum_fusion), calls=%async_computation | async-start | bytes 589824 | tf_op jit(solution)/shard_map/all_to_all | solution.py:27
  25.4 68.1 %all-gather.5.cloned.1.call-start = ((), (), s32[]{:S(2)}) async-start(), calls=%async_computation.8 | async-start | bytes 2506752 | tf_op jit(solution)/shard_map/all_gather | solution.py:61
  37.4 55.4 %copy-start.7 = (f32[1,2048]{1,0:T(1,128)S(1)}, f32[1,2048]{1,0:T(1,128)}, u32[]{:S(2)}) copy-start(f32[1,2048]{1,0:T(1,128)} %param.24) | copy-start | bytes 24580
  88.8 15.0 %all-to-all-start.4 = ((bf16[16,8,128]{2,1,0:T(8,128)(2,1)}), bf16[16,8,128]{2,1,0:T(8,128)(2,1)S(1)}, u32[]{:S(2)}, u32[]{:S(2)}) async-start(bf16[16,8,128]{2,1,0:T(8,128)(2,1)} %broadcast_in_dim.43), calls=%async_computation.4 | async-start | bytes 65536 | tf_op jit(solution)/shard_map/all_to_all | solution.py:27
  108.4 42.9 %copy-start.8 = (f32[2048]{0:T(1024)S(1)}, f32[2048]{0:T(1024)}, u32[]{:S(2)}) copy-start(f32[2048]{0:T(1024)} %param.28) | copy-start | bytes 24580
  108.5 42.9 %copy-start.1 = (bf16[2048,256]{1,0:T(8,128)(2,1)S(1)}, bf16[2048,256]{1,0:T(8,128)(2,1)}, u32[]{:S(2)}) copy-start(bf16[2048,256]{1,0:T(8,128)(2,1)} %param.29) | copy-start | bytes 3145732
  143.5 9.4 %collective-permute-start = (bf16[256,1024]{1,0:T(8,128)(2,1)S(1)}, bf16[256,1024]{1,0:T(8,128)(2,1)S(1)}, u32[]{:S(2)}, u32[]{:S(2)}) collective-permute-start(bf16[256,1024]{1,0:T(8,128)(2,1)S(1)} %bitcast.122), channel_id=1, source_target_pairs={{0,1},{1,0},{2,3},{3,2},{4,5},{5,4},{6,7},{7,6},{8,9},{9,8},{10,11... | collective-permute-start | bytes 1572872 | tf_op jit(solution)/shard_map/ppermute | solution.py:149
Sparse Core Ops, SparseCore 0:
  29.2 61.6 all-gather.4

commit v12 on v11

--- a/solution.py
+++ b/solution.py
@@ -58,7 +58,6 @@
     ix, ic = lax.axis_index("x"), lax.axis_index("c")
 
     ffn = jnp.concatenate([w_gate[0].T, w_up[0].T, w_down[0]], axis=0)
-    ffn = lax.all_gather(ffn, ("y", "x"), axis=0).reshape(Y, X, -1, seg)
     qkv_block = lax.all_gather(w_qkv[0, :, 0], "y", axis=0, tiled=True)
 
     positions = lax.dynamic_slice_in_dim(lengths, req * rows, rows)
@@ -92,14 +91,15 @@
     halves = [jnp.broadcast_to(block[None, :, q * head_dim : (q + 1) * head_dim], (Z, block.shape[0], head_dim)) for q in (0, 1)]
     sent = jnp.concatenate([sent, jnp.zeros((Z, 8 - rows, head_dim), BF16)] + halves, axis=1)
     arrived = swap(sent, DEPTH)
-    arrived, qkv_block, in_scale, head_gate, cosine, sine, residual, inside = lax.optimization_barrier(
-        (arrived, qkv_block, in_scale, head_gate, cosine, sine, residual, inside)
+    arrived, qkv_block, in_scale, head_gate, cosine, sine, residual, inside, ffn = lax.optimization_barrier(
+        (arrived, qkv_block, in_scale, head_gate, cosine, sine, residual, inside, ffn)
     )
+    ffn = lax.all_gather(ffn, "x", axis=0)
     batch = arrived[:, :rows].reshape(Z * rows, Y * depth)
     out_block = arrived[:, 8:].reshape(Z, 2, -1, head_dim).transpose(1, 0, 2, 3).reshape(2, -1, head_dim)
     part = jnp.dot(batch, qkv_block, preferred_element_type=F32).astype(BF16)
     part, out_block = lax.optimization_barrier((part.reshape(Z, rows, columns), out_block))
-    part = swap(part, DEPTH)
+    part, ffn = lax.optimization_barrier((swap(part, DEPTH), ffn))
     qkv = jnp.sum(part.astype(F32), axis=0) * in_scale
 
     query = qkv[:, : 2 * head_dim].reshape(rows, 2, head_dim)
@@ -119,28 +119,31 @@
     attended = summed / total[..., None]
     mixed = (attended * head_gate[..., None]).astype(BF16)
 
-    everyone = spread(mixed.transpose(1, 0, 2).reshape(2 * rows, head_dim), "y", Y).reshape(Y, 2, rows, head_dim)
+    sent = jnp.broadcast_to(mixed.transpose(1, 0, 2).reshape(1, 2 * rows, head_dim), (Y, 2 * rows, head_dim))
+    residual = residual.reshape(Y, 2, head_dim)
+    arrived = swap(jnp.concatenate([sent, residual, jnp.zeros((Y, 6, head_dim), BF16)], axis=1), "y")
+    everyone = arrived[:, : 2 * rows].reshape(Y, 2, rows, head_dim)
+    residual = arrived[:, 2 * rows : 2 * rows + 2].reshape(8, head_dim)
     part = jnp.einsum("yqrd,qnd->yrn", everyone, out_block, preferred_element_type=F32)
-    part = swap(part.reshape(Y * rows * C, 2, head_dim), ("y", "x", "c"))
-    projected = jnp.sum(part.reshape(Y, X * C, 2, head_dim), axis=1).reshape(8, head_dim)
+    part = part.reshape(Y, rows, C, seg).transpose(1, 2, 0, 3).reshape(rows * C, 8, head_dim)
+    projected = jnp.sum(swap(part, ("x", "c")), axis=0)
     stream = (residual.astype(F32) + projected).astype(BF16)
 
-    stream, post_gain = lax.optimization_barrier((stream, post_gain))
     post_half = own_core(post_gain.reshape(X, C, seg), 1).reshape(X, seg)
-    gate_up = ffn[:, :, : 2 * units].transpose(1, 0, 2, 3)
-    down = ffn[:, :, 2 * units :]
-    batch, gate_up, down, post_half = lax.optimization_barrier((spread(stream, DEPTH, Z), gate_up, down, post_half))
-    batch = batch.reshape(Z, X, seg)
+    batch = spread(stream, ("y",) + DEPTH, Y * Z).reshape(Y, Z, Y, seg)
+    batch = batch.transpose(2, 1, 0, 3).reshape(Y * Z, X, seg)
     wide = batch.astype(F32)
-    squares = jnp.sum(wide * wide, axis=(1, 2)).reshape(Z, 1)
-    batch = (wide * post_half).astype(BF16)
-    part = jnp.einsum("bxk,xyfk->byf", batch, gate_up, preferred_element_type=F32)
-    part = jnp.concatenate([part.reshape(Z, -1), jnp.broadcast_to(squares, (Z, head_dim))], axis=1)
+    squares = jnp.sum(wide * wide, axis=(1, 2)).reshape(Y * Z, 1)
+    gained = (wide * post_half).astype(BF16)
+    part = jnp.einsum("bxk,xfk->bf", gained, ffn[:, : 2 * units], preferred_element_type=F32)
+    part = jnp.concatenate([part, jnp.broadcast_to(squares, (Y * Z, 64))], axis=1)
     both = jnp.sum(lax.all_gather(part, "c", axis=0), axis=0)
     scale = lax.rsqrt(both[:, -1:] / width + EPSILON)
-    both = (both[:, :-head_dim] * scale).reshape(Z, Y, 2 * units)
-    hidden = (jax.nn.silu(both[..., :units]) * both[..., units:]).astype(BF16)
-    part = jnp.einsum("byf,yxfk->bxk", hidden, down, preferred_element_type=F32).astype(BF16)
+    both = both[:, : 2 * units] * scale
+    hidden = (jax.nn.silu(both[:, :units]) * both[:, units:]).astype(BF16)
+    part = jnp.einsum("bf,xfk->bxk", hidden, ffn[:, 2 * units :], preferred_element_type=F32).astype(BF16)
+    part = jnp.sum(swap(part.reshape(Y, Z, 8, head_dim), "y").astype(F32), axis=0).astype(BF16)
+    wide = lax.dynamic_slice_in_dim(batch.reshape(Y, Z, X * seg), lax.axis_index("y"), 1, 0).astype(F32)
     part = jnp.sum(spread(part.reshape(Z, 8, head_dim), "zl", ZL).astype(F32), axis=0).astype(BF16)
     lowered = jnp.sum(spread(part, "zh", ZH).astype(F32), axis=0)
     piece = (wide.reshape(Z, 8, head_dim) + lowered).astype(BF16).reshape(Z, part_width)

time: 162 us -> 172 us (1.062)
  starting transfers between devices: 27.3 us -> 61.3 us
  blocking collectives: 95.2 us -> 61.8 us
  waiting for transfers between devices: 10.4 us -> 32.3 us
  between operations: 13.9 us -> 0.49 us
    all_to_all x6 -> x4, blocking collectives: 82 us -> 35.3 us  [swap(): return lax.all_to_all(values, axes, split_axis=0, concat_axis=0, tiled=True)]
    all_to_all x2 -> x5, starting transfers between devices: 19.4 us -> 53.6 us  [swap(): return lax.all_to_all(values, axes, split_axis=0, concat_axis=0, tiled=True)]
    all_to_all x2 -> x5, waiting for transfers between devices: 9.26 us -> 31.2 us  [swap(): return lax.all_to_all(values, axes, split_axis=0, concat_axis=0, tiled=True)]
    all_gather x0 -> x1, blocking collectives: none -> 11.2 us  [local(): ffn = lax.all_gather(ffn, 'x', axis=0)]
    unnamed x30, local copies, waits for them, and re-layouts: 0.07 us -> 2.61 us
    all_gather x1, blocking collectives: 2.92 us -> 4.88 us  [local(): both = jnp.sum(lax.all_gather(part, 'c', axis=0), axis=0)]
  transfers between devices with their start and end apart: 4 -> 6, of which waited for: 3 -> 6; matrix products, arithmetic and copies ran while one was open for 5% -> 2% of each run, Pallas kernels for 0% -> 0%
where the time goes in v12:
time: 172 us; the launch traced here: 171 us
  blocking collectives  61.8 us (36%)
  starting transfers between devices  61.3 us (36%)
  waiting for transfers between devices  32.3 us (19%)
  local copies, waits for them, and re-layouts  8.55 us (5%)
  other arithmetic  4.31 us (3%)
  matrix products  2.16 us (1%)
    all_to_all x5, starting transfers between devices, swap(): return lax.all_to_all(values, axes, split_axis=0, concat_axis=0, tiled=True)  53.6 us
    all_to_all x4, blocking collectives, swap(): return lax.all_to_all(values, axes, split_axis=0, concat_axis=0, tiled=True)  35.3 us
    all_to_all x5, waiting for transfers between devices, swap(): return lax.all_to_all(values, axes, split_axis=0, concat_axis=0, tiled=True)  31.2 us
    all_gather x1, blocking collectives, local(): ffn = lax.all_gather(ffn, 'x', axis=0)  11.2 us
    all_gather x1, blocking collectives, local(): qkv_block = lax.all_gather(w_qkv[0, :, 0], 'y', axis=0, tiled=True)  10.5 us
    ppermute x1, starting transfers between devices, local(): far = lax.ppermute(near, 'c', [(0, 1), (1, 0)])  7.77 us
    all_gather x1, blocking collectives, local(): both = jnp.sum(lax.all_gather(part, 'c', axis=0), axis=0)  4.88 us
  transfers between devices with their start and end apart: 6, of which 6 were waited for; matrix products, arithmetic and copies ran while one was open for 2% of the time, Pallas kernels for 0%

profile of v12, /device:TPU:1, one launch (start us, length us, event | category | flops | bytes accessed | tf_op | source)
XLA Modules:
  0.0 171.0 jit_solution(2780514890831868637)
XLA Ops:
  0.0 0.8 fusion.50
  1.3 0.8 pad_maximum_fusion
  2.1 15.7 %all-to-all-start = ((bf16[16,72,128]{2,1,0:T(8,128)(2,1)}), bf16[16,72,128]{2,1,0:T(8,128)(2,1)S(1)}, u32[]{:S(2)}, u32[]{:S(2)}) async-start(bf16[16,72,128]{2,1,0:T(8,128)(2,1)} %pad_maximum_fusion), calls=%async_computation | async-start | bytes 589824 | tf_op jit(solution)/shard_map/all_to_all | solution.py:27
  19.0 10.5 %all-gather = bf16[1,128,1,512]{3,1,2,0:T(8,128)(2,1)S(1)} all-gather(bf16[1,32,1,512]{3,1,2,0:T(8,128)(2,1)S(1)} %copy-done.6), channel_id=2, replica_groups=mesh['y'=4,'zh'=4,'zl'=4,'x'=4,'c'=2] {'y'}, dimensions={1}, use_global_device_ids=true | all-gather | bytes 163840 | tf_op jit(solution)/shard_map/all_gather | solution.py:61
  30.0 1.7 all-to-all-done
  32.5 11.8 %all-to-all-start.1 = ((bf16[16,4,512]{2,1,0:T(4,128)(2,1)}), bf16[16,4,512]{2,1,0:T(4,128)(2,1)S(1)}, u32[]{:S(2)}, u32[]{:S(2)}) async-start(bf16[16,4,512]{2,1,0:T(4,128)(2,1)} %reshape.236), calls=%async_computation.1 | async-start | bytes 131072 | tf_op jit(solution)/shard_map/all_to_all | solution.py:27
  44.4 11.2 %all-gather.1 = bf16[1152,256]{1,0:T(8,128)(2,1)S(1)} all-gather(bf16[288,256]{1,0:T(8,128)(2,1)S(1)} %pad_maximum_fusion.1), channel_id=3, replica_groups=mesh['y'=4,'zh'=4,'zl'=4,'x'=4,'c'=2] {'x'}, dimensions={0}, use_global_device_ids=true | all-gather | bytes 737280 | tf_op jit(solution)/shard_map/all_gather | solution.py:97
  58.7 8.5 %all_to_all.45 = bf16[4,16,128]{2,1,0:T(8,128)(2,1)S(1)} all-to-all(bf16[4,16,128]{2,1,0:T(8,128)(2,1)S(1)} %maximum_maximum_fusion), channel_id=1, replica_groups=mesh['y'=4,'zh'=4,'zl'=4,'x'=4,'c'=2] {'y'}, dimensions={0} | all-to-all | bytes 32768 | tf_op jit(solution)/shard_map/all_to_all | solution.py:27
  68.0 8.4 %all-to-all-start.3 = ((f32[8,8,128]{2,1,0:T(8,128)}), f32[8,8,128]{2,1,0:T(8,128)S(1)}, u32[]{:S(2)}, u32[]{:S(2)}) async-start(f32[8,8,128]{2,1,0:T(8,128)} %reshape.242), calls=%async_computation.3 | async-start | bytes 65536 | tf_op jit(solution)/shard_map/all_to_all | solution.py:27
  76.5 4.7 %all-to-all-done.3 = f32[8,8,128]{2,1,0:T(8,128)S(1)} async-done(((f32[8,8,128]{2,1,0:T(8,128)}), f32[8,8,128]{2,1,0:T(8,128)S(1)}, u32[]{:S(2)}, u32[]{:S(2)}) %all-to-all-start.3) | async-done | bytes 32800 | tf_op jit(solution)/shard_map/all_to_all | solution.py:27
  81.2 0.7 broadcast_in_dim.46
  81.9 13.3 %all-to-all-start.4 = ((bf16[64,8,128]{2,1,0:T(8,128)(2,1)}), bf16[64,8,128]{2,1,0:T(8,128)(2,1)S(1)}, u32[]{:S(2)}, u32[]{:S(2)}) async-start(bf16[64,8,128]{2,1,0:T(8,128)(2,1)} %broadcast_in_dim.46), calls=%async_computation.4 | async-start | bytes 262144 | tf_op jit(solution)/shard_map/all_to_all | solution.py:27
  95.8 0.7 reduce.13
  96.5 12.6 %all-to-all-done.4 = bf16[64,8,128]{2,1,0:T(8,128)(2,1)S(1)} async-done(((bf16[64,8,128]{2,1,0:T(8,128)(2,1)}), bf16[64,8,128]{2,1,0:T(8,128)(2,1)S(1)}, u32[]{:S(2)}, u32[]{:S(2)}) %all-to-all-start.4) | async-done | bytes 131104 | tf_op jit(solution)/shard_map/all_to_all | solution.py:27
  110.1 4.9 %all-gather.2 = f32[128,256]{1,0:T(8,128)S(1)} all-gather(f32[64,256]{1,0:T(8,128)S(1)} %pad_maximum_fusion.2), channel_id=4, replica_groups=mesh['y'=4,'zh'=4,'zl'=4,'x'=4,'c'=2] {'c'}, dimensions={0}, use_global_device_ids=true | all-gather | bytes 196608 | tf_op jit(solution)/shard_map/all_gather | solution.py:140
  115.6 7.9 %all_to_all.46 = bf16[4,16,8,128]{3,2,1,0:T(8,128)(2,1)S(1)} all-to-all(bf16[4,16,8,128]{3,2,1,0:T(8,128)(2,1)S(1)} %reshape.245), channel_id=1, replica_groups=mesh['y'=4,'zh'=4,'zl'=4,'x'=4,'c'=2] {'y'}, dimensions={0} | all-to-all | bytes 262144 | tf_op jit(solution)/shard_map/all_to_all | solution.py:27
  123.6 7.2 %all_to_all.47 = bf16[4,16,8,128]{3,2,1,0:T(8,128)(2,1)S(1)} all-to-all(bf16[4,16,8,128]{3,2,1,0:T(8,128)(2,1)S(1)} %broadcast_in_dim.49), channel_id=1, replica_groups=mesh['y'=4,'zh'=4,'zl'=4,'x'=4,'c'=2] {'zl'}, dimensions={0} | all-to-all | bytes 262144 | tf_op jit(solution)/shard_map/all_to_all | solution.py:27
  130.8 0.7 broadcast_in_dim.50
  131.5 4.3 %all-to-all-start.7 = ((bf16[4,16,8,128]{3,2,1,0:T(8,128)(2,1)}), bf16[4,16,8,128]{3,2,1,0:T(8,128)(2,1)S(1)}, u32[]{:S(2)}, u32[]{:S(2)}) async-start(bf16[4,16,8,128]{3,2,1,0:T(8,128)(2,1)} %broadcast_in_dim.50), calls=%async_computation.7 | async-start | bytes 262144 | tf_op jit(solution)/shard_map/all_to_all | solution.py:27
  136.0 11.9 %all-to-all-done.7 = bf16[4,16,8,128]{3,2,1,0:T(8,128)(2,1)S(1)} async-done(((bf16[4,16,8,128]{3,2,1,0:T(8,128)(2,1)}), bf16[4,16,8,128]{3,2,1,0:T(8,128)(2,1)S(1)}, u32[]{:S(2)}, u32[]{:S(2)}) %all-to-all-start.7) | async-done | bytes 131104 | tf_op jit(solution)/shard_map/all_to_all | solution.py:27
  148.1 11.7 %all_to_all.48 = bf16[16,16,1024]{2,1,0:T(8,128)(2,1)S(1)} all-to-all(bf16[16,16,1024]{2,1,0:T(8,128)(2,1)S(1)} %broadcast_in_dim.52), channel_id=1, replica_groups=mesh['y'=4,'zh'=4,'zl'=4,'x'=4,'c'=2] {'y','x'}, dimensions={0} | all-to-all | bytes 1048576 | tf_op jit(solution)/shard_map/all_to_all | solution.py:27
  159.7 7.8 %collective-permute-start = (bf16[256,1024]{1,0:T(8,128)(2,1)S(1)}, bf16[256,1024]{1,0:T(8,128)(2,1)S(1)}, u32[]{:S(2)}, u32[]{:S(2)}) collective-permute-start(bf16[256,1024]{1,0:T(8,128)(2,1)S(1)} %bitcast.124), channel_id=1, source_target_pairs={{0,1},{1,0},{2,3},{3,2},{4,5},{5,4},{6,7},{7,6},{8,9},{9,8},{10,11... | collective-permute-start | bytes 1572872 | tf_op jit(solution)/shard_map/ppermute | solution.py:152
  167.9 1.1 collective-permute-done
  170.3 0.7 reshape.252
  (125 shorter events, 10.9 us)
Async XLA Ops:
  0.0 29.8 %copy-start = (bf16[1,2048,2]{1,2,0:T(2,128)(2,1)S(1)}, bf16[1,2048,2]{1,2,0:T(2,128)(2,1)}, u32[]{:S(2)}) copy-start(bf16[1,2048,2]{1,2,0:T(2,128)(2,1)} %param.19) | copy-start | bytes 24580
  0.0 0.8 copy-start.5
  0.0 0.8 copy-start.9
  2.1 29.5 %all-to-all-start = ((bf16[16,72,128]{2,1,0:T(8,128)(2,1)}), bf16[16,72,128]{2,1,0:T(8,128)(2,1)S(1)}, u32[]{:S(2)}, u32[]{:S(2)}) async-start(bf16[16,72,128]{2,1,0:T(8,128)(2,1)} %pad_maximum_fusion), calls=%async_computation | async-start | bytes 589824 | tf_op jit(solution)/shard_map/all_to_all | solution.py:27
  17.9 0.7 copy-start.12
  17.9 1.0 copy-start.6
  19.0 10.5 %copy-start.2 = (bf16[1,96,256]{2,1,0:T(8,128)(2,1)S(1)}, bf16[1,96,256]{2,1,0:T(8,128)(2,1)}, u32[]{:S(2)}) copy-start(bf16[1,96,256]{2,1,0:T(8,128)(2,1)} %param.27) | copy-start | bytes 147460
  19.0 10.5 %copy-start.3 = (bf16[1,256,96]{1,2,0:T(8,128)(2,1)S(1)}, bf16[1,256,96]{1,2,0:T(8,128)(2,1)}, u32[]{:S(2)}) copy-start(bf16[1,256,96]{1,2,0:T(8,128)(2,1)} %param.26) | copy-start | bytes 147460
  19.0 10.5 %copy-start.4 = (bf16[1,256,96]{1,2,0:T(8,128)(2,1)S(1)}, bf16[1,256,96]{1,2,0:T(8,128)(2,1)}, u32[]{:S(2)}) copy-start(bf16[1,256,96]{1,2,0:T(8,128)(2,1)} %param.25) | copy-start | bytes 147460
  32.5 25.6 %copy-start.13 = (bf16[1,2,1024,1,128]{4,2,3,1,0:T(8,128)(2,1)S(1)}, bf16[1,2,1024,1,128]{4,2,3,1,0:T(8,128)(2,1)}, u32[]{:S(2)}) copy-start(bf16[1,2,1024,1,128]{4,2,3,1,0:T(8,128)(2,1)} %param.17) | copy-start | bytes 1572868
  32.5 23.4 %all-to-all-start.1 = ((bf16[16,4,512]{2,1,0:T(4,128)(2,1)}), bf16[16,4,512]{2,1,0:T(4,128)(2,1)S(1)}, u32[]{:S(2)}, u32[]{:S(2)}) async-start(bf16[16,4,512]{2,1,0:T(4,128)(2,1)} %reshape.236), calls=%async_computation.1 | async-start | bytes 131072 | tf_op jit(solution)/shard_map/all_to_all | solution.py:27
  56.3 0.7 copy-start.10
  57.0 0.7 copy-start.11
  68.0 13.2 %all-to-all-start.3 = ((f32[8,8,128]{2,1,0:T(8,128)}), f32[8,8,128]{2,1,0:T(8,128)S(1)}, u32[]{:S(2)}, u32[]{:S(2)}) async-start(f32[8,8,128]{2,1,0:T(8,128)} %reshape.242), calls=%async_computation.3 | async-start | bytes 65536 | tf_op jit(solution)/shard_map/all_to_all | solution.py:27
  81.9 13.9 %copy-start.7 = (f32[1,2048]{1,0:T(1,128)S(1)}, f32[1,2048]{1,0:T(1,128)}, u32[]{:S(2)}) copy-start(f32[1,2048]{1,0:T(1,128)} %param.24) | copy-start | bytes 24580
  81.9 27.3 %all-to-all-start.4 = ((bf16[64,8,128]{2,1,0:T(8,128)(2,1)}), bf16[64,8,128]{2,1,0:T(8,128)(2,1)S(1)}, u32[]{:S(2)}, u32[]{:S(2)}) async-start(bf16[64,8,128]{2,1,0:T(8,128)(2,1)} %broadcast_in_dim.46), calls=%async_computation.4 | async-start | bytes 262144 | tf_op jit(solution)/shard_map/all_to_all | solution.py:27
  131.5 16.4 %all-to-all-start.7 = ((bf16[4,16,8,128]{3,2,1,0:T(8,128)(2,1)}), bf16[4,16,8,128]{3,2,1,0:T(8,128)(2,1)S(1)}, u32[]{:S(2)}, u32[]{:S(2)}) async-start(bf16[4,16,8,128]{3,2,1,0:T(8,128)(2,1)} %broadcast_in_dim.50), calls=%async_computation.7 | async-start | bytes 262144 | tf_op jit(solution)/shard_map/all_to_all | solution.py:27
  136.0 31.6 %copy-start.1 = (bf16[2048,256]{1,0:T(8,128)(2,1)S(1)}, bf16[2048,256]{1,0:T(8,128)(2,1)}, u32[]{:S(2)}) copy-start(bf16[2048,256]{1,0:T(8,128)(2,1)} %param.29) | copy-start | bytes 3145732
  148.1 19.4 %copy-start.8 = (f32[2048]{0:T(1024)S(1)}, f32[2048]{0:T(1024)}, u32[]{:S(2)}) copy-start(f32[2048]{0:T(1024)} %param.28) | copy-start | bytes 24580
  159.7 9.3 %collective-permute-start = (bf16[256,1024]{1,0:T(8,128)(2,1)S(1)}, bf16[256,1024]{1,0:T(8,128)(2,1)S(1)}, u32[]{:S(2)}, u32[]{:S(2)}) collective-permute-start(bf16[256,1024]{1,0:T(8,128)(2,1)S(1)} %bitcast.124), channel_id=1, source_target_pairs={{0,1},{1,0},{2,3},{3,2},{4,5},{5,4},{6,7},{7,6},{8,9},{9,8},{10,11... | collective-permute-start | bytes 1572872 | tf_op jit(solution)/shard_map/ppermute | solution.py:152

commit v13 on v11

--- a/solution.py
+++ b/solution.py
@@ -82,7 +82,8 @@
     def own_core(array, axis):
         return lax.dynamic_slice_in_dim(array, ic, 1, axis)
 
-    residual = own_core(own_row(tokens).reshape(Y, C, seg), 1).reshape(8, head_dim)
+    residual = own_core(own_row(tokens).reshape(Y, C, seg), 1).reshape(Y, 2, head_dim)
+    residual = jnp.concatenate([residual, jnp.zeros((Y, 6, head_dim), BF16)], axis=1)
     slot = jnp.arange(kv_cache.shape[2], dtype=jnp.int32)
     inside = (slot[None, :] >= starts[:, None]) & (slot[None, :] < limits[:, None])
 
@@ -119,18 +120,23 @@
     attended = summed / total[..., None]
     mixed = (attended * head_gate[..., None]).astype(BF16)
 
-    everyone = spread(mixed.transpose(1, 0, 2).reshape(2 * rows, head_dim), "y", Y).reshape(Y, 2, rows, head_dim)
+    sent = jnp.broadcast_to(mixed.transpose(1, 0, 2).reshape(1, 2 * rows, head_dim), (Y, 2 * rows, head_dim))
+    arrived = swap(jnp.concatenate([sent, residual], axis=1), "y")
+    everyone = arrived[:, : 2 * rows].reshape(Y, 2, rows, head_dim)
+    residual = arrived[:, 2 * rows : 2 * rows + 2].reshape(8, head_dim)
     part = jnp.einsum("yqrd,qnd->yrn", everyone, out_block, preferred_element_type=F32)
-    part = swap(part.reshape(Y * rows * C, 2, head_dim), ("y", "x", "c"))
-    projected = jnp.sum(part.reshape(Y, X * C, 2, head_dim), axis=1).reshape(8, head_dim)
+    part = part.reshape(Y, rows, C, seg).transpose(1, 2, 0, 3).reshape(rows * C, 8, head_dim)
+    part, residual = lax.optimization_barrier((part, residual))
+    projected = jnp.sum(swap(part, ("x", "c")), axis=0)
     stream = (residual.astype(F32) + projected).astype(BF16)
 
     stream, post_gain = lax.optimization_barrier((stream, post_gain))
     post_half = own_core(post_gain.reshape(X, C, seg), 1).reshape(X, seg)
     gate_up = ffn[:, :, : 2 * units].transpose(1, 0, 2, 3)
     down = ffn[:, :, 2 * units :]
-    batch, gate_up, down, post_half = lax.optimization_barrier((spread(stream, DEPTH, Z), gate_up, down, post_half))
-    batch = batch.reshape(Z, X, seg)
+    sent = jnp.broadcast_to(stream.reshape(Y, 1, 2, head_dim), (Y, Z, 2, head_dim)).reshape(Y * Z, 2, head_dim)
+    batch, gate_up, down, post_half = lax.optimization_barrier((swap(sent, ("y",) + DEPTH), gate_up, down, post_half))
+    batch = batch.reshape(Y, Z, seg).transpose(1, 0, 2)
     wide = batch.astype(F32)
     squares = jnp.sum(wide * wide, axis=(1, 2)).reshape(Z, 1)
     batch = (wide * post_half).astype(BF16)
@@ -141,9 +147,10 @@
     both = (both[:, :-head_dim] * scale).reshape(Z, Y, 2 * units)
     hidden = (jax.nn.silu(both[..., :units]) * both[..., units:]).astype(BF16)
     part = jnp.einsum("byf,yxfk->bxk", hidden, down, preferred_element_type=F32).astype(BF16)
+    part, wide = lax.optimization_barrier((part, wide.reshape(Z, 8, head_dim)))
     part = jnp.sum(spread(part.reshape(Z, 8, head_dim), "zl", ZL).astype(F32), axis=0).astype(BF16)
     lowered = jnp.sum(spread(part, "zh", ZH).astype(F32), axis=0)
-    piece = (wide.reshape(Z, 8, head_dim) + lowered).astype(BF16).reshape(Z, part_width)
+    piece = (wide + lowered).astype(BF16).reshape(Z, part_width)
 
     near = spread(piece, ("y", "x"), Y * X).reshape(Y * X * Z, part_width)
     far = lax.ppermute(near, "c", [(0, 1), (1, 0)])

time: 162 us -> 162 us (level)
  waiting for transfers between devices: 10.4 us -> 12.2 us
    all_to_all x6, blocking collectives: 82 us -> 79.9 us  [swap(): return lax.all_to_all(values, axes, split_axis=0, concat_axis=0, tiled=True)]
    all_to_all x2, waiting for transfers between devices: 9.26 us -> 11 us  [swap(): return lax.all_to_all(values, axes, split_axis=0, concat_axis=0, tiled=True)]
where the time goes in v13:
time: 162 us
  blocking collectives  93.7 us (58%)
  starting transfers between devices  27 us (17%)
  between operations  13.9 us (9%)
  waiting for transfers between devices  12.2 us (8%)
  local copies, waits for them, and re-layouts  7.09 us (4%)
  other arithmetic  5.36 us (3%)
  matrix products  2.43 us (2%)
    all_to_all x6, blocking collectives, swap(): return lax.all_to_all(values, axes, split_axis=0, concat_axis=0, tiled=True)  79.9 us
    all_to_all x2, starting transfers between devices, swap(): return lax.all_to_all(values, axes, split_axis=0, concat_axis=0, tiled=True)  20.5 us
    all_to_all x2, waiting for transfers between devices, swap(): return lax.all_to_all(values, axes, split_axis=0, concat_axis=0, tiled=True)  11 us
    all_gather x1, blocking collectives, local(): qkv_block = lax.all_gather(w_qkv[0, :, 0], 'y', axis=0, tiled=True)  10.4 us
    ppermute x1, starting transfers between devices, local(): far = lax.ppermute(near, 'c', [(0, 1), (1, 0)])  6.5 us
    all_gather x1, blocking collectives, local(): both = jnp.sum(lax.all_gather(part, 'c', axis=0), axis=0)  3.4 us
  transfers between devices with their start and end apart: 4, of which 3 were waited for; matrix products, arithmetic and copies ran while one was open for 5% of the time, Pallas kernels for 0%

profile of v13, /device:TPU:1, one launch (start us, length us, event | category | flops | bytes accessed | tf_op | source)
XLA Modules:
  0.0 161.6 jit_solution(3162125941610880308)
XLA Ops:
  6.6 0.8 fusion.51
  7.4 0.8 fusion.27
  8.6 0.8 pad_maximum_fusion
  9.5 15.9 %all-to-all-start = ((bf16[16,72,128]{2,1,0:T(8,128)(2,1)}), bf16[16,72,128]{2,1,0:T(8,128)(2,1)S(1)}, u32[]{:S(2)}, u32[]{:S(2)}) async-start(bf16[16,72,128]{2,1,0:T(8,128)(2,1)} %pad_maximum_fusion), calls=%async_computation | async-start | bytes 589824 | tf_op jit(solution)/shard_map/all_to_all | solution.py:27
  25.4 0.7 pad_maximum_fusion.1
  26.8 10.4 %all-gather = bf16[1,128,1,512]{3,1,2,0:T(8,128)(2,1)S(1)} all-gather(bf16[1,32,1,512]{3,1,2,0:T(8,128)(2,1)S(1)} %copy-done.6), channel_id=2, replica_groups=mesh['y'=4,'zh'=4,'zl'=4,'x'=4,'c'=2] {'y'}, dimensions={1}, use_global_device_ids=true | all-gather | bytes 163840 | tf_op jit(solution)/shard_map/all_gather | solution.py:62
  37.4 1.7 %all-to-all-done = bf16[16,72,128]{2,1,0:T(8,128)(2,1)S(1)} async-done(((bf16[16,72,128]{2,1,0:T(8,128)(2,1)}), bf16[16,72,128]{2,1,0:T(8,128)(2,1)S(1)}, u32[]{:S(2)}, u32[]{:S(2)}) %all-to-all-start) | async-done | bytes 294944 | tf_op jit(solution)/shard_map/all_to_all | solution.py:27
  39.4 23.1 %all_to_all.40 = bf16[16,4,512]{2,1,0:T(4,128)(2,1)S(1)} all-to-all(bf16[16,4,512]{2,1,0:T(4,128)(2,1)S(1)} %reshape.235), channel_id=1, replica_groups=mesh['y'=4,'zh'=4,'zl'=4,'x'=4,'c'=2] {'zh','zl'}, dimensions={0} | all-to-all | bytes 131072 | tf_op jit(solution)/shard_map/all_to_all | solution.py:27
  63.9 8.2 %all_to_all.41 = bf16[4,16,128]{2,1,0:T(8,128)(2,1)S(1)} all-to-all(bf16[4,16,128]{2,1,0:T(8,128)(2,1)S(1)} %copy.92), channel_id=1, replica_groups=mesh['y'=4,'zh'=4,'zl'=4,'x'=4,'c'=2] {'y'}, dimensions={0} | all-to-all | bytes 32768 | tf_op jit(solution)/shard_map/all_to_all | solution.py:27
  72.3 12.6 %all_to_all.42 = f32[8,8,128]{2,1,0:T(8,128)S(1)} all-to-all(f32[8,8,128]{2,1,0:T(8,128)S(1)} %reshape.240), channel_id=1, replica_groups=mesh['y'=4,'zh'=4,'zl'=4,'x'=4,'c'=2] {'x','c'}, dimensions={0} | all-to-all | bytes 65536 | tf_op jit(solution)/shard_map/all_to_all | solution.py:27
  84.9 0.6 broadcast_in_dim.46
  85.6 4.6 %all-to-all-start.4 = ((bf16[64,2,128]{2,1,0:T(2,128)(2,1)}), bf16[64,2,128]{2,1,0:T(2,128)(2,1)S(1)}, u32[]{:S(2)}, u32[]{:S(2)}) async-start(bf16[64,2,128]{2,1,0:T(2,128)(2,1)} %bitcast.39), calls=%async_computation.4 | async-start | bytes 65536 | tf_op jit(solution)/shard_map/all_to_all | solution.py:27
  90.7 0.6 reduce.9
  91.4 1.5 slice_bitcast_fusion
  92.9 1.2 slice.95
  94.1 9.3 %all-to-all-done.4 = bf16[64,2,128]{2,1,0:T(2,128)(2,1)S(1)} async-done(((bf16[64,2,128]{2,1,0:T(2,128)(2,1)}), bf16[64,2,128]{2,1,0:T(2,128)(2,1)S(1)}, u32[]{:S(2)}, u32[]{:S(2)}) %all-to-all-start.4) | async-done | bytes 32800 | tf_op jit(solution)/shard_map/all_to_all | solution.py:27
  103.5 0.5 convolution_bitcast_fusion
  104.3 3.4 %all-gather.2 = f32[32,896]{1,0:T(8,128)S(1)} all-gather(f32[16,896]{1,0:T(8,128)S(1)} %pad_maximum_fusion.2), channel_id=4, replica_groups=mesh['y'=4,'zh'=4,'zl'=4,'x'=4,'c'=2] {'c'}, dimensions={0}, use_global_device_ids=true | all-gather | bytes 172032 | tf_op jit(solution)/shard_map/all_gather | solution.py:145
  108.6 7.4 %all_to_all.43 = bf16[4,16,8,128]{3,2,1,0:T(8,128)(2,1)S(1)} all-to-all(bf16[4,16,8,128]{3,2,1,0:T(8,128)(2,1)S(1)} %broadcast_in_dim.49), channel_id=1, replica_groups=mesh['y'=4,'zh'=4,'zl'=4,'x'=4,'c'=2] {'zl'}, dimensions={0} | all-to-all | bytes 262144 | tf_op jit(solution)/shard_map/all_to_all | solution.py:27
  116.1 15.3 %all_to_all.44 = bf16[4,16,8,128]{3,2,1,0:T(8,128)(2,1)S(1)} all-to-all(bf16[4,16,8,128]{3,2,1,0:T(8,128)(2,1)S(1)} %broadcast_in_dim.50), channel_id=1, replica_groups=mesh['y'=4,'zh'=4,'zl'=4,'x'=4,'c'=2] {'zh'}, dimensions={0} | all-to-all | bytes 262144 | tf_op jit(solution)/shard_map/all_to_all | solution.py:27
  131.5 13.3 %all_to_all.45 = bf16[16,16,1024]{2,1,0:T(8,128)(2,1)S(1)} all-to-all(bf16[16,16,1024]{2,1,0:T(8,128)(2,1)S(1)} %broadcast_in_dim.52), channel_id=1, replica_groups=mesh['y'=4,'zh'=4,'zl'=4,'x'=4,'c'=2] {'y','x'}, dimensions={0} | all-to-all | bytes 1048576 | tf_op jit(solution)/shard_map/all_to_all | solution.py:27
  144.8 6.5 %collective-permute-start = (bf16[256,1024]{1,0:T(8,128)(2,1)S(1)}, bf16[256,1024]{1,0:T(8,128)(2,1)S(1)}, u32[]{:S(2)}, u32[]{:S(2)}) collective-permute-start(bf16[256,1024]{1,0:T(8,128)(2,1)S(1)} %bitcast.140), channel_id=1, source_target_pairs={{0,1},{1,0},{2,3},{3,2},{4,5},{5,4},{6,7},{7,6},{8,9},{9,8},{10,11... | collective-permute-start | bytes 1572872 | tf_op jit(solution)/shard_map/ppermute | solution.py:156
  151.8 1.1 collective-permute-done
  154.1 0.7 reshape.255
  (124 shorter events, 6.7 us)
Async XLA Ops:
  6.5 30.6 %copy-start = (bf16[1,2048,2]{1,2,0:T(2,128)(2,1)S(1)}, bf16[1,2048,2]{1,2,0:T(2,128)(2,1)}, u32[]{:S(2)}) copy-start(bf16[1,2048,2]{1,2,0:T(2,128)(2,1)} %param.19) | copy-start | bytes 24580
  6.5 19.9 %copy-start.5 = (bf16[4,2048]{1,0:T(4,128)(2,1)S(1)}, bf16[4,2048]{1,0:T(4,128)(2,1)}, u32[]{:S(2)}) copy-start(bf16[4,2048]{1,0:T(4,128)(2,1)} %param.15) | copy-start | bytes 49156
  6.5 30.6 %copy-start.9 = (f32[1,2048]{1,0:T(1,128)S(1)}, f32[1,2048]{1,0:T(1,128)}, u32[]{:S(2)}) copy-start(f32[1,2048]{1,0:T(1,128)} %param.21) | copy-start | bytes 24580
  6.5 18.9 %copy-start.2 = (bf16[1,96,256]{2,1,0:T(8,128)(2,1)S(1)}, bf16[1,96,256]{2,1,0:T(8,128)(2,1)}, u32[]{:S(2)}) copy-start(bf16[1,96,256]{2,1,0:T(8,128)(2,1)} %param.27) | copy-start | bytes 147460
  6.5 18.9 %copy-start.3 = (bf16[1,256,96]{1,2,0:T(8,128)(2,1)S(1)}, bf16[1,256,96]{1,2,0:T(8,128)(2,1)}, u32[]{:S(2)}) copy-start(bf16[1,256,96]{1,2,0:T(8,128)(2,1)} %param.26) | copy-start | bytes 147460
  6.5 18.9 %copy-start.4 = (bf16[1,256,96]{1,2,0:T(8,128)(2,1)S(1)}, bf16[1,256,96]{1,2,0:T(8,128)(2,1)}, u32[]{:S(2)}) copy-start(bf16[1,256,96]{1,2,0:T(8,128)(2,1)} %param.25) | copy-start | bytes 147460
  6.6 19.6 %copy-start.12 = (s32[256]{0:T(256)S(1)}, s32[256]{0:T(256)}, u32[]{:S(2)}) copy-start(s32[256]{0:T(256)} %param.16) | copy-start | bytes 3076
  6.6 20.2 %copy-start.6 = (bf16[1,32,1,512]{3,1,2,0:T(8,128)(2,1)S(1)}, bf16[1,32,1,512]{3,1,2,0:T(8,128)(2,1)}, u32[]{:S(2)}) copy-start(bf16[1,32,1,512]{3,1,2,0:T(8,128)(2,1)} %param.18) | copy-start | bytes 98308
  9.5 53.2 %copy-start.10 = (f32[1,128]{1,0:T(1,128)S(1)}, f32[1,128]{1,0:T(1,128)}, u32[]{:S(2)}) copy-start(f32[1,128]{1,0:T(1,128)} %param.23) | copy-start | bytes 1540
  9.5 53.5 %copy-start.11 = (f32[1,128]{1,0:T(1,128)S(1)}, f32[1,128]{1,0:T(1,128)}, u32[]{:S(2)}) copy-start(f32[1,128]{1,0:T(1,128)} %param.22) | copy-start | bytes 1540
  9.5 53.9 %copy-start.13 = (bf16[1,2,1024,1,128]{4,2,3,1,0:T(8,128)(2,1)S(1)}, bf16[1,2,1024,1,128]{4,2,3,1,0:T(8,128)(2,1)}, u32[]{:S(2)}) copy-start(bf16[1,2,1024,1,128]{4,2,3,1,0:T(8,128)(2,1)} %param.17) | copy-start | bytes 1572868
  9.5 29.6 %all-to-all-start = ((bf16[16,72,128]{2,1,0:T(8,128)(2,1)}), bf16[16,72,128]{2,1,0:T(8,128)(2,1)S(1)}, u32[]{:S(2)}, u32[]{:S(2)}) async-start(bf16[16,72,128]{2,1,0:T(8,128)(2,1)} %pad_maximum_fusion), calls=%async_computation | async-start | bytes 589824 | tf_op jit(solution)/shard_map/all_to_all | solution.py:27
  25.4 66.0 %all-gather.5.cloned.1.call-start = ((), (), s32[]{:S(2)}) async-start(), calls=%async_computation.8 | async-start | bytes 2506752 | tf_op jit(solution)/shard_map/all_gather | solution.py:61
  39.1 51.6 %copy-start.7 = (f32[1,2048]{1,0:T(1,128)S(1)}, f32[1,2048]{1,0:T(1,128)}, u32[]{:S(2)}) copy-start(f32[1,2048]{1,0:T(1,128)} %param.24) | copy-start | bytes 24580
  85.6 17.8 %all-to-all-start.4 = ((bf16[64,2,128]{2,1,0:T(2,128)(2,1)}), bf16[64,2,128]{2,1,0:T(2,128)(2,1)S(1)}, u32[]{:S(2)}, u32[]{:S(2)}) async-start(bf16[64,2,128]{2,1,0:T(2,128)(2,1)} %bitcast.39), calls=%async_computation.4 | async-start | bytes 65536 | tf_op jit(solution)/shard_map/all_to_all | solution.py:27
  108.5 42.8 %copy-start.8 = (f32[2048]{0:T(1024)S(1)}, f32[2048]{0:T(1024)}, u32[]{:S(2)}) copy-start(f32[2048]{0:T(1024)} %param.28) | copy-start | bytes 24580
  108.6 42.8 %copy-start.1 = (bf16[2048,256]{1,0:T(8,128)(2,1)S(1)}, bf16[2048,256]{1,0:T(8,128)(2,1)}, u32[]{:S(2)}) copy-start(bf16[2048,256]{1,0:T(8,128)(2,1)} %param.29) | copy-start | bytes 3145732
  144.8 8.0 %collective-permute-start = (bf16[256,1024]{1,0:T(8,128)(2,1)S(1)}, bf16[256,1024]{1,0:T(8,128)(2,1)S(1)}, u32[]{:S(2)}, u32[]{:S(2)}) collective-permute-start(bf16[256,1024]{1,0:T(8,128)(2,1)S(1)} %bitcast.140), channel_id=1, source_target_pairs={{0,1},{1,0},{2,3},{3,2},{4,5},{5,4},{6,7},{7,6},{8,9},{9,8},{10,11... | collective-permute-start | bytes 1572872 | tf_op jit(solution)/shard_map/ppermute | solution.py:156
Sparse Core Ops, SparseCore 0:
  29.2 61.7 all-gather.4
